TPU v7x, 128 devices: a whole 4x4x4 slice. The times are simulated.
128 devices in a mesh: req: 16 (over x, y), exp: 8 (over z, core).
Axes of the slice: x: 4, y: 4, z: 4, core: 2. Of those that a mesh axis runs over, the one named last changes fastest.
Arguments:
- tokens: bfloat16 [16384, 2048], P(('req', 'exp')), may hold values from -6 to 6
- attn_gain: float32 [2048], replicated, may hold values from 0.1 to 1.9
- w_query: bfloat16 [2048, 2048], P(None, 'exp'), may hold values from -0.25 to 0.25
- w_key: bfloat16 [2048, 2048], P(None, 'exp'), may hold values from -0.125 to 0.125
- w_value: bfloat16 [2048, 2048], P(None, 'exp'), may hold values from -0.125 to 0.125
- w_out: bfloat16 [2048, 2048], P('exp'), may hold values from -0.375 to 0.375
- prefix_cache: bfloat16 [8, 1024, 2, 2048], P(None, 'req', None, 'exp'), may hold values from -205 to 205
- group_of: int32 [16], replicated, may hold values from 0 to 7
- lengths: int32 [16], replicated, may hold values from 1 to 1024, 10240 in all
- moe_gain: float32 [2048], replicated, may hold values from 0.1 to 1.9
- w_gate: bfloat16 [128, 2048, 512], P(('req', 'exp')), may hold values from -0.125 to 0.125
- w_up: bfloat16 [128, 2048, 512], P(('req', 'exp')), may hold values from -0.125 to 0.125
- w_down: bfloat16 [128, 512, 2048], P(('req', 'exp')), may hold values from -0.25 to 0.25
- routes: int32 [16384, 8], P(('req', 'exp')), may hold values from 0 to 63, all different within a row; in each aligned block of 128 rows (0 to 127, 128 to 255, ...) at most 18 rows name the same one
- route_weights: float32 [16384, 8], P(('req', 'exp')), may hold values from 0.1 to 0.4
Outputs:
- layer_out: bfloat16 [16384, 2048], P(('req', 'exp'))
Inputs may be any that keep to these rules, and one draw needn't show every extreme that they name: `routes`: in the rows of one device no expert is named more than 18 times.
All inputs are finite; a program needn't handle non-finite values.
Results may differ from a plain program's by a relative error of at most 0.017.
Values may be sent and summed in bfloat16 or wider, within the bound.
No kernel may reach another device: no remote copies, remote signals or barrier semaphores. Data moves between devices by JAX's collectives and lax.ppermute only.
A program may use at most 192 MiB of HBM per device.

v0:
```python
import functools
import math

import jax
import jax.numpy as jnp
from jax import lax
from jax.experimental import pallas as pl
from jax.experimental.pallas import tpu as pltpu
from jax.sharding import Mesh
from jax.sharding import PartitionSpec as P


HD = 128
PREFIX = 1024
BF = jnp.bfloat16
F32 = jnp.float32
SUB = 8


def vmem():
    return pl.BlockSpec(memory_space=pltpu.VMEM)


def limit(mib):
    return pltpu.CompilerParams(vmem_limit_bytes=mib << 20)


def call(kernel, out_shape, n_in, mib=16, **kw):
    outs = jax.tree.map(lambda _: vmem(), out_shape)
    return pl.pallas_call(
        kernel, out_shape=out_shape, in_specs=[vmem()] * n_in, out_specs=outs,
        compiler_params=limit(mib), **kw
    )


def shape(dims, dtype):
    return jax.ShapeDtypeStruct(dims, dtype)


def dot(a, b):
    return jnp.dot(a, b, preferred_element_type=F32)


def rms(wide, gain):
    return wide * lax.rsqrt(jnp.mean(wide * wide, axis=-1, keepdims=True) + 1e-05) * gain


def norm_kernel(x_ref, g_ref, o_ref, first_ref, last_ref):
    normed = rms(x_ref[...].astype(F32), g_ref[...]).astype(BF)
    o_ref[...] = normed
    half = first_ref.shape[0]
    first_ref[...] = normed[:half]
    last_ref[...] = normed[half:]


def slots_of(index):
    block = index // SUB
    return block // 2, (block % 2) * (SUB + 1) + index % SUB


def route_kernel(r_ref, rt_ref, w_ref, dt_ref, wm_ref, wx_ref):
    rows, top = r_ref.shape
    blocks = wx_ref.shape[1]
    experts = blocks // 2
    wide = blocks * SUB
    iota = lambda dims, axis: lax.broadcasted_iota(jnp.int32, dims, axis)
    one = lambda hit: jnp.where(hit, 1.0, 0.0)
    row_i = iota((rows, rows), 0)
    col_i = iota((rows, rows), 1)
    e_t = iota((experts, rows), 0)
    named_t = jnp.zeros((experts, rows), F32)
    for k in range(top):
        named_t += one(rt_ref[k : k + 1, :] == e_t)
    rank_t = dot(named_t.astype(BF), one(row_i < col_i).astype(BF))
    rank_t = jnp.where(named_t > 0.5, rank_t, -1.0).astype(BF)
    expert, _ = slots_of(iota((wide, experts), 0))
    spread = one(expert == iota((wide, experts), 1)).astype(BF)
    _, slot = slots_of(iota((wide, rows), 0))
    dt_ref[:wide, :] = one(dot(spread, rank_t) == slot.astype(F32)).astype(BF)
    block = iota((blocks, experts), 0)
    spread = one(block // 2 == iota((blocks, experts), 1)).astype(BF)
    slot = (iota((blocks, rows), 0) % 2) * (SUB + 1) + SUB
    dt_ref[wide:, :] = one(dot(spread, rank_t) == slot.astype(F32)).astype(BF)
    e_n = iota((rows, experts), 1)
    named = jnp.zeros((rows, experts), F32)
    weight = jnp.zeros((rows, experts), F32)
    for k in range(top):
        hit = r_ref[:, k : k + 1] == e_n
        named += one(hit)
        weight += jnp.where(hit, w_ref[:, k : k + 1], 0.0)
    rank = dot(one(col_i < row_i).astype(BF), named.astype(BF))
    rank = jnp.where(named > 0.5, rank, -1.0).astype(BF)
    high = weight.astype(BF)
    low = (weight - high.astype(F32)).astype(BF)
    expert, _ = slots_of(iota((experts, wide), 1))
    spread = one(expert == iota((experts, wide), 0)).astype(BF)
    _, slot = slots_of(iota((rows, wide), 1))
    hit = dot(rank, spread) == slot.astype(F32)
    wm_ref[:rows, :] = jnp.where(hit, dot(high, spread), 0.0).astype(BF)
    wm_ref[rows:, :] = jnp.where(hit, dot(low, spread), 0.0).astype(BF)
    block = iota((experts, blocks), 1)
    spread = one(block // 2 == iota((experts, blocks), 0)).astype(BF)
    slot = (iota((rows, blocks), 1) % 2) * (SUB + 1) + SUB
    hit = dot(rank, spread) == slot.astype(F32)
    wx_ref[:rows, :] = jnp.where(hit, dot(high, spread), 0.0).astype(BF)
    wx_ref[rows:, :] = jnp.where(hit, dot(low, spread), 0.0).astype(BF)


def prefix_kernel(group_ref, x_ref, o_ref):
    rows, width = x_ref.shape[2:]
    for r in range(o_ref.shape[0] // rows):
        for j in range(2):
            o_ref[r * rows : (r + 1) * rows, j * width : (j + 1) * width] = x_ref[group_ref[r], j]


def qkv_kernel(count, *refs):
    pieces = refs[:count]
    wq, wk, wv = refs[count : count + 2], refs[count + 2 : count + 4], refs[count + 4 : count + 6]
    cos_ref, sin_ref, q_ref, k_ref, v_ref, x_ref = refs[count + 6 :]
    at = 0
    for piece in pieces:
        x_ref[at : at + piece.shape[0], :] = piece[...]
        at += piece.shape[0]
    local = wq[0].shape[1]
    for side in range(2):
        for w_ref, o_ref in ((wk[side], k_ref), (wq[side], q_ref)):
            rows = o_ref.shape[0]
            mixed = dot(x_ref[:rows, :], w_ref[...])
            for h in range(local // HD):
                v = mixed[:, h * HD : (h + 1) * HD]
                turned = v * cos_ref[:rows, :] + pltpu.roll(v, HD // 2, 1) * sin_ref[:rows, :]
                col = side * local + h * HD
                o_ref[:, col : col + HD] = turned.astype(BF)
        v_ref[:, side * local : (side + 1) * local] = dot(x_ref[...], wv[side][...]).astype(BF)


def attend(scale, q_ref, keys, values, pre_refs, bias_ref, o_ref):
    local = pre_refs[0].shape[1] // 2
    nt = (((1,), (1,)), ((), ()))
    for h in range(q_ref.shape[1] // HD):
        side, col = divmod(h * HD, local)
        pre_ref = pre_refs[side]
        cols = slice(h * HD, (h + 1) * HD)
        q = q_ref[:, cols]
        scores = [
            lax.dot_general(q, pre_ref[:, col : col + HD], nt, preferred_element_type=F32)
        ]
        at = 0
        for k_ref in keys:
            n = k_ref.shape[0]
            s = lax.dot_general(q, k_ref[:, cols], nt, preferred_element_type=F32)
            scores.append(s + bias_ref[:, at : at + n])
            at += n
        top = jnp.max(scores[0], axis=-1, keepdims=True)
        for s in scores[1:]:
            top = jnp.maximum(top, jnp.max(s, axis=-1, keepdims=True))
        raised = [jnp.exp2((s - top) * scale) for s in scores]
        total = sum(jnp.sum(e, axis=-1, keepdims=True) for e in raised)
        out = dot(raised[0].astype(BF), pre_ref[:, local + col : local + col + HD])
        for e, v_ref in zip(raised[1:], values):
            out += dot(e.astype(BF), v_ref[:, cols])
        o_ref[:, cols] = (out / total).astype(BF)


def project(a_ref, wa_ref, wb_ref):
    local = wa_ref.shape[0]
    return dot(a_ref[:, :local], wa_ref[...]) + dot(a_ref[:, local:], wb_ref[...])


def attn_far_kernel(scale, q, k0, k1, k2, v0, v1, v2, pa, pb, bias, wa, wb, o1, o2, tmp):
    attend(scale, q, (k0, k1, k2), (v0, v1, v2), (pa, pb), bias, tmp)
    total = project(tmp, wa, wb).astype(BF)
    rows = o1.shape[0]
    o1[...] = total[:rows]
    o2[...] = total[rows:]


def attn_near_kernel(scale, q, k0, k1, k2, v0, v1, v2, pa, pb, bias, o):
    attend(scale, q, (k0, k1, k2), (v0, v1, v2), (pa, pb), bias, o)


def attn_own_kernel(scale, q, k0, k1, k2, v0, v1, v2, pa, pb, bias, wa, wb, o, tmp):
    attend(scale, q, (k0, k1, k2), (v0, v1, v2), (pa, pb), bias, tmp)
    o[...] = project(tmp, wa, wb)


def proj_near_kernel(a_ref, wa, wb, got1, got2, low_ref, high_ref):
    total = project(a_ref, wa, wb)
    rows = low_ref.shape[0]
    half = rows // 2
    low_ref[:half, :] = total[:half].astype(BF)
    low_ref[half:, :] = (total[half:rows] + got2[...].astype(F32)).astype(BF)
    high_ref[:half, :] = (total[rows : rows + half] + got1[...].astype(F32)).astype(BF)
    high_ref[half:, :] = total[rows + half :].astype(BF)


def dispatch_kernel(t_ref, own_ref, b1_ref, b2_ref, g_ref, d_ref, h_ref, o_ref, normed, extra):
    b = pl.program_id(0)
    part = o_ref.shape[1]
    wide = o_ref.shape[0]
    blocks = wide // SUB

    @pl.when(b == 0)
    def _():
        attn_out = own_ref[...] + b1_ref[...].astype(F32) + b2_ref[...].astype(F32)
        hidden = (t_ref[...].astype(F32) + attn_out).astype(BF)
        h_ref[...] = hidden
        rows = rms(hidden.astype(F32), g_ref[...]).astype(BF)
        for i in range(SUB):
            normed[i] = rows[:, i * part : (i + 1) * part]

    @pl.when(b < SUB)
    def _():
        x = normed[b]
        o_ref[...] = dot(d_ref[:wide, :], x).astype(BF)
        more = dot(d_ref[wide:, :], x)
        for i in range(part // 128):
            extra[i, pl.ds(b, blocks, stride=SUB), :] = more[:, i * 128 : (i + 1) * 128]

    @pl.when(b == SUB)
    def _():
        for i in range(part // 128):
            o_ref[:, i * 128 : (i + 1) * 128] = extra[i].astype(BF)


def dispatch(tokens, own, b1, b2, gain, table):
    rows, width = tokens.shape
    part = width // SUB
    blocks = table.shape[0] // (SUB + 1)
    wide = blocks * SUB
    whole = lambda a: pl.BlockSpec(a.shape, lambda b: (0, 0))
    args = (tokens, own, b1, b2, gain, table)
    return pl.pallas_call(
        dispatch_kernel,
        grid=(SUB + 1,),
        out_shape=(shape((rows, width), BF), shape((wide, width + part), BF)),
        in_specs=[whole(a) for a in args],
        out_specs=(whole(tokens), pl.BlockSpec((wide, part), lambda b: (0, b))),
        scratch_shapes=[
            pltpu.VMEM((SUB, rows, part), BF), pltpu.VMEM((part // 128, wide, 128), F32),
        ],
        compiler_params=limit(20),
        name="dispatch",
    )(*args)


def ffn_kernel(x_ref, *refs):
    sources, (o_ref, wg, wu, wd, rows_ref, extra, sem) = refs[:6], refs[6:]
    j = pl.program_id(0)
    width = rows_ref.shape[1]
    part = width // SUB
    wide = x_ref.shape[0]
    blocks = wide // SUB
    copies = [
        pltpu.make_async_copy(source, target.at[h], sem.at[h, i])
        for h in range(2)
        for i, (source, target) in enumerate(zip(sources[3 * h : 3 * h + 3], (wg, wu, wd)))
    ]

    @pl.when(j == 0)
    def _():
        for copy in copies:
            copy.start()

    rows_ref[:wide, :] = x_ref[:, :width]
    for i in range(part // 128):
        extra[i] = x_ref[:, width + i * 128 : width + (i + 1) * 128].astype(F32)
    for b in range(SUB):
        for i in range(part // 128):
            col = b * part + i * 128
            rows_ref[wide:, col : col + 128] = extra[i, pl.ds(b, blocks, stride=SUB), :].astype(BF)
    total = None
    for h in range(2):

        @pl.when(j == 0)
        def _():
            copies[3 * h].wait()
            copies[3 * h + 1].wait()

        gate = dot(rows_ref[...], wg[h])
        upper = dot(rows_ref[...], wu[h])
        act = (gate / (1.0 + jnp.exp(-gate)) * upper).astype(BF)

        @pl.when(j == 0)
        def _():
            copies[3 * h + 2].wait()

        out = dot(act, wd[h])
        total = out if total is None else total + out
    o_ref[:, :width] = total[:wide].astype(BF)
    for b in range(SUB):
        for i in range(part // 128):
            col = b * part + i * 128
            extra[i, pl.ds(b, blocks, stride=SUB), :] = total[wide:, col : col + 128]
    for i in range(part // 128):
        o_ref[:, width + i * 128 : width + (i + 1) * 128] = extra[i].astype(BF)


def ffn(x, w0, w1):
    wide, packed = x.shape
    width, hidden = w0[0].shape
    step = 256
    rows = step + step // SUB
    block = pl.BlockSpec((step, packed), lambda j: (j, 0))
    return pl.pallas_call(
        ffn_kernel,
        grid=(wide // step,),
        out_shape=shape((wide, packed), BF),
        in_specs=[block] + [pl.BlockSpec(memory_space=pltpu.HBM)] * 6,
        out_specs=block,
        scratch_shapes=[
            pltpu.VMEM((2, width, hidden), BF),
            pltpu.VMEM((2, width, hidden), BF),
            pltpu.VMEM((2, hidden, width), BF),
            pltpu.VMEM((rows, width), BF),
            pltpu.VMEM((width // SUB // 128, step, 128), F32),
            pltpu.SemaphoreType.DMA((2, 3)),
        ],
        compiler_params=limit(40),
        name="ffn",
    )(x, *w0, *w1)


def combine_kernel(live_ref, r_ref, x_ref, wm_ref, wx_ref, h_ref, o_ref, extra):
    b = pl.program_id(0)
    rows, part = o_ref.shape
    blocks = r_ref.shape[0] // SUB

    @pl.when(b == 0)
    def _():
        for i in range(part // 128):
            extra[i] = x_ref[:, i * 128 : (i + 1) * 128].astype(F32)

    more = jnp.concatenate(
        [extra[i, pl.ds(b, blocks, stride=SUB), :] for i in range(part // 128)], axis=1
    ).astype(BF)
    both = dot(wm_ref[...], r_ref[...]) + dot(wx_ref[...], more)
    out = h_ref[...].astype(F32) + both[:rows] + both[rows:]
    row = lax.broadcasted_iota(jnp.int32, out.shape, 0)
    o_ref[...] = jnp.where(row < live_ref[0], out, 0.0).astype(BF)


def combine(live, back, wm, wx, hidden):
    rows, width = hidden.shape
    part = width // SUB
    wide = back.shape[0]
    whole = lambda a: pl.BlockSpec(a.shape, lambda b: (0, 0))
    cols = lambda n: pl.BlockSpec((n, part), lambda b: (0, b))
    return pl.pallas_call(
        combine_kernel,
        grid=(SUB,),
        out_shape=shape((rows, width), BF),
        in_specs=[
            pl.BlockSpec(memory_space=pltpu.SMEM), cols(wide),
            pl.BlockSpec((wide, part), lambda b: (0, SUB)), whole(wm), whole(wx), cols(rows),
        ],
        out_specs=cols(rows),
        scratch_shapes=[pltpu.VMEM((part // 128, wide, 128), F32)],
        compiler_params=limit(20),
        name="combine",
    )(live, back, back, wm, wx, hidden)


def layer(
    tokens, attn_gain, w_query, w_key, w_value, w_out, prefix_cache, group_of, lengths,
    moe_gain, w_gate, w_up, w_down, routes, route_weights,
):
    rows, width = tokens.shape
    zs = lax.axis_size("z")
    reqs = lax.axis_size("x") * lax.axis_size("y")
    experts = reqs * zs
    z = lax.axis_index("z")
    core = lax.axis_index("c")
    req = lax.axis_index("x") * lax.axis_size("y") + lax.axis_index("y")
    local = w_query.shape[1]
    up = [(i, (i + 1) % zs) for i in range(zs)]
    down = [(i, (i - 1) % zs) for i in range(zs)]
    swap = lambda v: lax.ppermute(v, "c", [(0, 1), (1, 0)])
    to_up = lambda v: lax.ppermute(v, "z", up)
    to_down = lambda v: lax.ppermute(v, "z", down)
    half = rows // 2

    part = shape((half, width), BF)
    normed, first, last = call(norm_kernel, (shape((rows, width), BF), part, part), 2, name="norm")(
        tokens, attn_gain[None]
    )
    low0 = to_up(first)
    high1 = to_down(last)
    low1 = to_up(last)
    high0 = to_down(first)
    own_b = swap(normed)
    far0 = to_up(low0)
    far1 = to_down(high1)
    near_a = (low0, low1, high0, high1)
    near_b = tuple(swap(v) for v in near_a)

    out_b = swap(w_out)
    wq = (w_query, swap(w_query))
    wk = (w_key, swap(w_key))
    wv = (w_value, swap(w_value))

    spread = prefix_cache.shape[1]
    outgoing = pl.pallas_call(
        prefix_kernel,
        out_shape=shape((reqs * spread, 2 * local), BF),
        in_specs=[pl.BlockSpec(memory_space=pltpu.SMEM), vmem()],
        out_specs=vmem(),
        compiler_params=limit(16),
        name="prefix",
    )(group_of, jnp.transpose(prefix_cache, (0, 2, 1, 3)))
    pre_a = lax.all_to_all(outgoing, ("x", "y"), split_axis=0, concat_axis=0, tiled=True)
    pre_b = swap(pre_a)

    own_w = (w_gate[0], w_up[0], w_down[0])
    other_w = tuple(swap(w) for w in own_w)

    blocks = 2 * experts
    wide = blocks * SUB
    table, wm, wx = call(
        route_kernel,
        [
            shape((wide + blocks, rows), BF), shape((2 * rows, wide), BF),
            shape((2 * rows, blocks), BF),
        ],
        3,
        name="route",
    )(routes, routes.T, route_weights)

    mine, yours = core * rows, (1 - core) * rows
    z_low, z_high, z_far = (z + zs - 1) % zs, (z + 1) % zs, (z + 2) % zs
    starts = jnp.stack(
        [
            z * 2 * rows + mine, z * 2 * rows + yours,
            z_low * 2 * rows + mine, z_high * 2 * rows + mine,
            z_low * 2 * rows + yours, z_high * 2 * rows + yours,
            z_far * 2 * rows + mine, z_far * 2 * rows + yours,
        ]
    )
    place = (starts[:, None] + jnp.arange(rows, dtype=jnp.int32)).reshape(-1)
    spots = (PREFIX + place).astype(F32)
    freqs = 10000.0 ** (-(jnp.arange(HD // 2, dtype=F32) * 2.0) / HD)
    angles = spots[:, None] * freqs[None, :]
    cosine = jnp.cos(angles)
    sine = jnp.sin(angles)
    cosine = jnp.concatenate([cosine, cosine], axis=1)
    sine = jnp.concatenate([-sine, sine], axis=1)
    length = lengths[req]
    bias = jnp.where(place < length, 0.0, -1e30)[None, :]

    def projections(pieces, first, count, name):
        return call(
            lambda *refs: qkv_kernel(len(pieces), *refs),
            (
                shape((count // 2, 2 * local), BF),
                shape((count, 2 * local), BF),
                shape((count, 2 * local), BF),
            ),
            len(pieces) + 8,
            scratch_shapes=[pltpu.VMEM((count, width), BF)],
            name=name,
        )(*pieces, *wq, *wk, *wv, cosine[first : first + count], sine[first : first + count])

    q0, k0, v0 = projections((normed, own_b), 0, 2 * rows, "qkv_own")
    *near_b, k0 = lax.optimization_barrier((*near_b, k0))
    q1, k1, v1 = projections((*near_a, *near_b), 2 * rows, 4 * rows, "qkv_near")
    far0, far1, k1 = lax.optimization_barrier((far0, far1, k1))
    q2, k2, v2 = projections((far0, far1, swap(far0), swap(far1)), 6 * rows, 2 * rows, "qkv_far")
    cache = (k0, k1, k2, v0, v1, v2, pre_a, pre_b, bias)
    scale = math.log2(math.e) / math.sqrt(HD)
    tmp = [pltpu.VMEM((rows, 2 * local), BF)]

    far1, far2 = call(
        functools.partial(attn_far_kernel, scale),
        [shape((half, width), BF)] * 2,
        12,
        scratch_shapes=tmp,
        name="attn_far",
    )(q2, *cache, w_out, out_b)
    got1 = to_up(far1)
    got2 = to_down(far2)
    near = call(
        functools.partial(attn_near_kernel, scale), shape((2 * rows, 2 * local), BF), 10,
        name="attn_near",
    )(q1, *cache)
    to_low, to_high = call(
        proj_near_kernel, [shape((rows, width), BF)] * 2, 5, name="proj_near"
    )(near, w_out, out_b, got1, got2)
    to_low, to_high, q0 = lax.optimization_barrier((to_low, to_high, q0))
    b1 = to_up(to_high)
    b2 = to_down(to_low)
    own = call(
        functools.partial(attn_own_kernel, scale),
        shape((rows, width), F32),
        12,
        scratch_shapes=tmp,
        name="attn_own",
    )(q0, *cache, w_out, out_b)
    own, other_w = lax.optimization_barrier((own, other_w))

    hidden, send = dispatch(tokens, own, b1, b2, moe_gain[None], table)

    def exchange(v):
        return lax.all_to_all(
            v.reshape(experts, 2 * SUB, v.shape[1]), ("x", "y", "z"), 0, 0, tiled=True
        ).reshape(v.shape)

    back = exchange(ffn(exchange(send), own_w, other_w))
    live = jnp.clip(length - (z * 2 + core) * rows, 0, rows).astype(jnp.int32)[None]
    return combine(live, back, wm, wx, hidden)


def solution(mesh):
    side = math.isqrt(mesh.shape["req"])
    grid = Mesh(
        mesh.devices.reshape(side, side, mesh.shape["exp"] // 2, 2), ("x", "y", "z", "c")
    )
    req, exp = ("x", "y"), ("z", "c")
    every = req + exp
    return jax.shard_map(
        layer,
        mesh=grid,
        in_specs=(
            P(every, None), P(), P(None, exp), P(None, exp), P(None, exp), P(exp, None),
            P(None, req, None, exp), P(), P(), P(),
            P(every, None, None), P(every, None, None), P(every, None, None),
            P(every, None), P(every, None),
        ),
        out_specs=P(every, None),
        check_vma=False,
    )
```

profile of v0, /device:TPU:82, one launch (start us, length us, event | category | flops | bytes accessed | tf_op | source)
XLA Modules:
  0.0 273.4 jit_solution(11706101549866956881)
XLA Ops:
  3.5 1.9 collective-permute-start
  5.4 5.5 %collective-permute-done.2.refs_2_ = bf16[64,2048]{1,0:T(8,128)(2,1)S(1)} collective-permute-done((bf16[64,2048]{1,0:T(8,128)(2,1)S(1)}, bf16[64,2048]{1,0:T(8,128)(2,1)S(1)}, u32[]{:S(2)}, u32[]{:S(2)}) %collective-permute-start.2) | collective-permute-done | bytes 262176 | tf_op jit(solution)/shard_map/ppermute | solution.py:380
  12.2 2.3 collective-permute-start.1
  14.4 4.9 %collective-permute-done.3.refs_3_ = bf16[64,2048]{1,0:T(8,128)(2,1)S(1)} collective-permute-done((bf16[64,2048]{1,0:T(8,128)(2,1)}, bf16[64,2048]{1,0:T(8,128)(2,1)S(1)}, u32[]{:S(2)}, u32[]{:S(2)}) %collective-permute-start.3) | collective-permute-done | bytes 262176 | tf_op jit(solution)/shard_map/ppermute | solution.py:380
  20.1 1.1 copy.20
  23.5 7.3 %all-to-all-start = ((bf16[16,64,512]{2,1,0:T(8,128)(2,1)}), bf16[16,64,512]{2,1,0:T(8,128)(2,1)S(1)}, u32[]{:S(2)}, u32[]{:S(2)}) async-start(bf16[16,64,512]{2,1,0:T(8,128)(2,1)} %bitcast.33), calls=%async_computation | async-start | bytes 2097152 | tf_op jit(solution)/shard_map/all_to_all | solution.py:411
  31.1 1.4 collective-permute-done.6.refs_6_
  32.5 3.0 %collective-permute-start.12 = (bf16[64,2048]{1,0:T(8,128)(2,1)}, bf16[64,2048]{1,0:T(8,128)(2,1)S(1)}, u32[]{:S(2)}, u32[]{:S(2)}) collective-permute-start(bf16[64,2048]{1,0:T(8,128)(2,1)} %copy-done.33), channel_id=1, source_target_pairs={{0,2},{2,4},{4,6},{6,0},{1,3},{3,5},{5,7},{7,1},{8,10},{10,12},{12... | collective-permute-start | bytes 786440 | tf_op jit(solution)/shard_map/ppermute | solution.py:379
  36.2 1.9 fusion.2
  40.0 3.2 %qkv_own.1 = (bf16[128,512]{1,0:T(8,128)(2,1)S(1)}, bf16[256,512]{1,0:T(8,128)(2,1)S(1)}, bf16[256,512]{1,0:T(8,128)(2,1)S(1)}) custom-call(bf16[128,2048]{1,0:T(8,128)(2,1)} %get-tuple-element.43.refs_0_, bf16[128,2048]{1,0:T(8,128)(2,1)} %collective-permute-done.8.refs_1_, bf16[2048,256]{1,0:T(8,128)(2,1)S(1)} %copy-done.1, ...), custom_call_target="tpu_custom_call" | custom-call | tf_op jit(solution)/shard_map/qkv_own/pallas_call | solution.py:451
  44.6 1.2 copy-done.10
  45.8 4.4 %qkv_near.1 = (bf16[256,512]{1,0:T(8,128)(2,1)S(1)}, bf16[512,512]{1,0:T(8,128)(2,1)S(1)}, bf16[512,512]{1,0:T(8,128)(2,1)S(1)}) custom-call(bf16[64,2048]{1,0:T(8,128)(2,1)S(1)} %copy-done.34, bf16[64,2048]{1,0:T(8,128)(2,1)} %collective-permute-done.1.refs_1_, bf16[64,2048]{1,0:T(8,128)(2,1)S(1)} %copy-done.32, bf16[64,2048]{1,0:T(8,128)(2,1)S(1)} %copy-done.36, ...), custom_call_target="tpu_custom_call" | custom-call | tf_op jit(solution)/shard_map/qkv_near/pallas_call | solution.py:451
  57.3 1.2 copy-done.2
  58.6 1.2 copy-done.4
  59.8 1.2 copy-done.6
  61.0 1.2 copy-done.8
  62.2 1.2 copy-done.11
  66.3 3.1 %qkv_far.1 = (bf16[128,512]{1,0:T(8,128)(2,1)S(1)}, bf16[256,512]{1,0:T(8,128)(2,1)S(1)}, bf16[256,512]{1,0:T(8,128)(2,1)S(1)}) custom-call(bf16[64,2048]{1,0:T(8,128)(2,1)S(1)} %copy-done.40, bf16[64,2048]{1,0:T(8,128)(2,1)} %collective-permute-done.13.refs_1_, bf16[64,2048]{1,0:T(8,128)(2,1)S(1)} %copy-done.42, ...), custom_call_target="tpu_custom_call" | custom-call | tf_op jit(solution)/shard_map/qkv_far/pallas_call | solution.py:451
  69.4 4.0 %attn_far.1 = (bf16[64,2048]{1,0:T(8,128)(2,1)S(1)}, bf16[64,2048]{1,0:T(8,128)(2,1)S(1)}) custom-call(bf16[128,512]{1,0:T(8,128)(2,1)S(1)} %get-tuple-element.59.q, bf16[256,512]{1,0:T(8,128)(2,1)S(1)} %get-tuple-element.50.k0, bf16[512,512]{1,0:T(8,128)(2,1)S(1)} %copy-done.13, bf16[256,512]{1,0:T(8,128)(2,1)S(1)} %get-tuple-element.55.k2, ...), custom_call_target="tpu_custom_call" | custom-call | tf_op jit(solution)/shard_map/attn_far/pallas_call | solution.py:472
  73.4 1.7 collective-permute-start.18
  75.5 4.7 %attn_near.1.a_ref = bf16[256,512]{1,0:T(8,128)(2,1)S(1)} custom-call(bf16[256,512]{1,0:T(8,128)(2,1)S(1)} %copy-done.38, bf16[256,512]{1,0:T(8,128)(2,1)S(1)} %get-tuple-element.50.k0, bf16[512,512]{1,0:T(8,128)(2,1)S(1)} %copy-done.13, bf16[256,512]{1,0:T(8,128)(2,1)S(1)} %get-tuple-element.55.k2, bf16[256,512]{1,0:T(8,128)(2,1)S(1)} %copy-done.20, ...), custom_call_target="tpu_custom_call" | custom-call | tf_op jit(solution)/shard_map/attn_near/pallas_call | solution.py:481
  80.2 1.6 collective-permute-done.18.got1
  81.8 1.6 collective-permute-done.19.got2
  83.4 1.6 proj_near.1
  85.1 2.5 collective-permute-start.23
  95.9 3.9 %attn_own.1.own_ref = f32[128,2048]{1,0:T(8,128)S(1)} custom-call(bf16[128,512]{1,0:T(8,128)(2,1)S(1)} %copy-done.44, bf16[256,512]{1,0:T(8,128)(2,1)S(1)} %get-tuple-element.50.k0, bf16[512,512]{1,0:T(8,128)(2,1)S(1)} %copy-done.14, bf16[256,512]{1,0:T(8,128)(2,1)S(1)} %copy-done.23, bf16[256,512]{1,0:T(8,128)(2,1)S(1)} %copy-done.21, ...), custom_call_target="tpu_custom_call" | custom-call | tf_op jit(solution)/shard_map/attn_own/pallas_call | solution.py:491
  100.6 4.6 %dispatch.1 = (bf16[128,2048]{1,0:T(8,128)(2,1)S(1)}, bf16[1024,2304]{1,0:T(8,128)(2,1)S(1)}) custom-call(bf16[128,2048]{1,0:T(8,128)(2,1)S(1)} %copy-done.27, f32[128,2048]{1,0:T(8,128)S(1)} %attn_own.1.own_ref, bf16[128,2048]{1,0:T(8,128)(2,1)} %collective-permute-done.23.b1_ref, bf16[128,2048]{1,0:T(8,128)(2,1)} %collective-permute-done.24.b2_ref, ...), custom_call_target="tpu_custom_call" | custom-call | tf_op jit(solution)/shard_map/dispatch/pallas_call | solution.py:233
  105.3 62.2 %all_to_all.21 = bf16[64,16,2304]{2,1,0:T(8,128)(2,1)} all-to-all(bf16[64,16,2304]{2,1,0:T(8,128)(2,1)S(1)} %bitcast.32), channel_id=1, replica_groups=mesh['x'=4,'y'=4,'z'=4,'c'=2] {'x','y','z'}, dimensions={0} | all-to-all | bytes 9437184 | tf_op jit(solution)/shard_map/all_to_all | solution.py:503
  167.5 22.7 %ffn.1 = bf16[1024,2304]{1,0:T(8,128)(2,1)} custom-call(bf16[1024,2304]{1,0:T(8,128)(2,1)} %bitcast.42, bf16[2048,512]{1,0:T(8,128)(2,1)} %bitcast.16.refs_0_, bf16[2048,512]{1,0:T(8,128)(2,1)} %bitcast.17.refs_1_, bf16[512,2048]{1,0:T(8,128)(2,1)} %bitcast.18.refs_2_, bf16[2048,512]{1,0:T(8,128)(2,1)} %collective-permute-done.20.refs_3_, ...), custom_call_target="tpu_custom_call" | custom-call | tf_op jit(solution)/shard_map/ffn/pallas_call | solution.py:305
  190.3 12.0 %all-to-all-start.2 = ((bf16[64,16,2304]{2,1,0:T(8,128)(2,1)}), bf16[64,16,2304]{2,1,0:T(8,128)(2,1)}, u32[]{:S(2)}, u32[]{:S(2)}) async-start(bf16[64,16,2304]{2,1,0:T(8,128)(2,1)} %bitcast.41), calls=%async_computation.2 | async-start | bytes 9437184 | tf_op jit(solution)/shard_map/all_to_all | solution.py:503
  203.0 63.1 %all-to-all-done.2 = bf16[64,16,2304]{2,1,0:T(8,128)(2,1)} async-done(((bf16[64,16,2304]{2,1,0:T(8,128)(2,1)}), bf16[64,16,2304]{2,1,0:T(8,128)(2,1)}, u32[]{:S(2)}, u32[]{:S(2)}) %all-to-all-start.2) | async-done | bytes 4718624 | tf_op jit(solution)/shard_map/all_to_all | solution.py:503
  266.1 7.3 %combine.1 = bf16[128,2048]{1,0:T(8,128)(2,1)} custom-call(s32[1]{0:T(128)} %bitcast.1.live_ref, bf16[1024,2304]{1,0:T(8,128)(2,1)} %bitcast.24.r_ref.x_ref, bf16[1024,2304]{1,0:T(8,128)(2,1)} %bitcast.24.r_ref.x_ref, bf16[256,1024]{1,0:T(8,128)(2,1)S(1)} %copy-done.29, bf16[256,128]{1,0:T(8,128)(2,1)S(1)} %copy-done.46, ...), custom_call_target="tpu_custom_call" | custom-call | tf_op jit(solution)/shard_map/combine/pallas_call | solution.py:349
  (153 shorter events, 31.4 us)
Async XLA Ops:
  2.8 8.0 %collective-permute-start.2 = (bf16[64,2048]{1,0:T(8,128)(2,1)S(1)}, bf16[64,2048]{1,0:T(8,128)(2,1)S(1)}, u32[]{:S(2)}, u32[]{:S(2)}) collective-permute-start(bf16[64,2048]{1,0:T(8,128)(2,1)S(1)} %get-tuple-element.41), channel_id=1, source_target_pairs={{0,6},{2,0},{4,2},{6,4},{1,7},{3,1},{5,3},{7,5},{8,14},{10,8},{12,... | collective-permute-start | bytes 786440 | tf_op jit(solution)/shard_map/ppermute | solution.py:380
  2.9 32.5 %collective-permute-start.9 = (bf16[2048,256]{1,0:T(8,128)(2,1)}, bf16[2048,256]{1,0:T(8,128)(2,1)S(1)}, u32[]{:S(2)}, u32[]{:S(2)}) collective-permute-start(bf16[2048,256]{1,0:T(8,128)(2,1)} %refs_4_.3), channel_id=1, source_target_pairs={{0,1},{1,0},{2,3},{3,2},{4,5},{5,4},{6,7},{7,6},{8,9},{9,8},{10,11... | collective-permute-start | bytes 3145736 | tf_op jit(solution)/shard_map/ppermute | solution.py:378
  2.9 32.6 %collective-permute-start.10 = (bf16[2048,256]{1,0:T(8,128)(2,1)}, bf16[2048,256]{1,0:T(8,128)(2,1)S(1)}, u32[]{:S(2)}, u32[]{:S(2)}) collective-permute-start(bf16[2048,256]{1,0:T(8,128)(2,1)} %refs_6_.3), channel_id=1, source_target_pairs={{0,1},{1,0},{2,3},{3,2},{4,5},{5,4},{6,7},{7,6},{8,9},{9,8},{10,11... | collective-permute-start | bytes 3145736 | tf_op jit(solution)/shard_map/ppermute | solution.py:378
  3.5 32.6 %collective-permute-start.11 = (bf16[2048,256]{1,0:T(8,128)(2,1)}, bf16[2048,256]{1,0:T(8,128)(2,1)}, u32[]{:S(2)}, u32[]{:S(2)}) collective-permute-start(bf16[2048,256]{1,0:T(8,128)(2,1)} %refs_8_.3), channel_id=1, source_target_pairs={{0,1},{1,0},{2,3},{3,2},{4,5},{5,4},{6,7},{7,6},{8,9},{9,8},{10,11... | collective-permute-start | bytes 3145736 | tf_op jit(solution)/shard_map/ppermute | solution.py:378
  3.5 8.7 %collective-permute-start = (bf16[64,2048]{1,0:T(8,128)(2,1)S(1)}, bf16[64,2048]{1,0:T(8,128)(2,1)S(1)}, u32[]{:S(2)}, u32[]{:S(2)}) collective-permute-start(bf16[64,2048]{1,0:T(8,128)(2,1)S(1)} %get-tuple-element.41), channel_id=1, source_target_pairs={{0,2},{2,4},{4,6},{6,0},{1,3},{3,5},{5,7},{7,1},{8,10},{10,12},{12... | collective-permute-start | bytes 786440 | tf_op jit(solution)/shard_map/ppermute | solution.py:379
  10.9 19.9 %copy-start.31 = (bf16[64,2048]{1,0:T(8,128)(2,1)}, bf16[64,2048]{1,0:T(8,128)(2,1)S(1)}, u32[]{:S(2)}) copy-start(bf16[64,2048]{1,0:T(8,128)(2,1)S(1)} %collective-permute-done.2.refs_2_) | copy-start | bytes 786436
  10.9 8.5 %collective-permute-start.3 = (bf16[64,2048]{1,0:T(8,128)(2,1)}, bf16[64,2048]{1,0:T(8,128)(2,1)S(1)}, u32[]{:S(2)}, u32[]{:S(2)}) collective-permute-start(bf16[64,2048]{1,0:T(8,128)(2,1)} %get-tuple-element.42), channel_id=1, source_target_pairs={{0,6},{2,0},{4,2},{6,4},{1,7},{3,1},{5,3},{7,5},{8,14},{10,8},{12,... | collective-permute-start | bytes 786440 | tf_op jit(solution)/shard_map/ppermute | solution.py:380
  12.2 18.6 %collective-permute-start.1 = (bf16[64,2048]{1,0:T(8,128)(2,1)}, bf16[64,2048]{1,0:T(8,128)(2,1)}, u32[]{:S(2)}, u32[]{:S(2)}) collective-permute-start(bf16[64,2048]{1,0:T(8,128)(2,1)} %get-tuple-element.42), channel_id=1, source_target_pairs={{0,2},{2,4},{4,6},{6,0},{1,3},{3,5},{5,7},{7,1},{8,10},{10,12},{12... | collective-permute-start | bytes 786440 | tf_op jit(solution)/shard_map/ppermute | solution.py:379
  20.1 15.4 %collective-permute-start.8 = (bf16[128,2048]{1,0:T(8,128)(2,1)}, bf16[128,2048]{1,0:T(8,128)(2,1)}, u32[]{:S(2)}, u32[]{:S(2)}) collective-permute-start(bf16[128,2048]{1,0:T(8,128)(2,1)} %get-tuple-element.43.refs_0_), channel_id=1, source_target_pairs={{0,1},{1,0},{2,3},{3,2},{4,5},{5,4},{6,7},{7,6},{8,9},{9,8},{10,11... | collective-permute-start | bytes 1572872 | tf_op jit(solution)/shard_map/ppermute | solution.py:378
  23.5 32.0 %all-to-all-start = ((bf16[16,64,512]{2,1,0:T(8,128)(2,1)}), bf16[16,64,512]{2,1,0:T(8,128)(2,1)S(1)}, u32[]{:S(2)}, u32[]{:S(2)}) async-start(bf16[16,64,512]{2,1,0:T(8,128)(2,1)} %bitcast.33), calls=%async_computation | async-start | bytes 2097152 | tf_op jit(solution)/shard_map/all_to_all | solution.py:411
  30.7 1.7 collective-permute-start.6
  32.5 20.1 %collective-permute-start.12 = (bf16[64,2048]{1,0:T(8,128)(2,1)}, bf16[64,2048]{1,0:T(8,128)(2,1)S(1)}, u32[]{:S(2)}, u32[]{:S(2)}) collective-permute-start(bf16[64,2048]{1,0:T(8,128)(2,1)} %copy-done.33), channel_id=1, source_target_pairs={{0,2},{2,4},{4,6},{6,0},{1,3},{3,5},{5,7},{7,1},{8,10},{10,12},{12... | collective-permute-start | bytes 786440 | tf_op jit(solution)/shard_map/ppermute | solution.py:379
  35.4 9.1 %collective-permute-start.4 = (bf16[64,2048]{1,0:T(8,128)(2,1)}, bf16[64,2048]{1,0:T(8,128)(2,1)S(1)}, u32[]{:S(2)}, u32[]{:S(2)}) collective-permute-start(bf16[64,2048]{1,0:T(8,128)(2,1)} %copy-done.33), channel_id=1, source_target_pairs={{0,1},{1,0},{2,3},{3,2},{4,5},{5,4},{6,7},{7,6},{8,9},{9,8},{10,11... | collective-permute-start | bytes 786440 | tf_op jit(solution)/shard_map/ppermute | solution.py:378
  35.5 17.1 %collective-permute-start.13 = (bf16[64,2048]{1,0:T(8,128)(2,1)}, bf16[64,2048]{1,0:T(8,128)(2,1)}, u32[]{:S(2)}, u32[]{:S(2)}) collective-permute-start(bf16[64,2048]{1,0:T(8,128)(2,1)} %copy-done.35), channel_id=1, source_target_pairs={{0,6},{2,0},{4,2},{6,4},{1,7},{3,1},{5,3},{7,5},{8,14},{10,8},{12,... | collective-permute-start | bytes 786440 | tf_op jit(solution)/shard_map/ppermute | solution.py:380
  35.6 9.0 %collective-permute-start.7 = (bf16[64,2048]{1,0:T(8,128)(2,1)}, bf16[64,2048]{1,0:T(8,128)(2,1)S(1)}, u32[]{:S(2)}, u32[]{:S(2)}) collective-permute-start(bf16[64,2048]{1,0:T(8,128)(2,1)} %copy-done.35), channel_id=1, source_target_pairs={{0,1},{1,0},{2,3},{3,2},{4,5},{5,4},{6,7},{7,6},{8,9},{9,8},{10,11... | collective-permute-start | bytes 786440 | tf_op jit(solution)/shard_map/ppermute | solution.py:378
  36.1 8.5 %collective-permute-start.5 = (bf16[64,2048]{1,0:T(8,128)(2,1)}, bf16[64,2048]{1,0:T(8,128)(2,1)S(1)}, u32[]{:S(2)}, u32[]{:S(2)}) collective-permute-start(bf16[64,2048]{1,0:T(8,128)(2,1)} %collective-permute-done.1.refs_1_), channel_id=1, source_target_pairs={{0,1},{1,0},{2,3},{3,2},{4,5},{5,4},{6,7},{7,6},{8,9},{9,8},{10,11... | collective-permute-start | bytes 786440 | tf_op jit(solution)/shard_map/ppermute | solution.py:378
  45.8 9.6 %copy-start = (bf16[256,2048]{1,0:T(8,128)(2,1)S(1)}, bf16[256,2048]{1,0:T(8,128)(2,1)}, u32[]{:S(2)}) copy-start(bf16[256,2048]{1,0:T(8,128)(2,1)} %wa.5) | copy-start | bytes 3145732
  45.8 10.1 %copy-start.52 = (s32[16]{0:T(128)S(1)}, s32[16]{0:T(128)}, u32[]{:S(2)}) copy-start(s32[16]{0:T(128)} %param.23) | copy-start | bytes 196
  52.6 2.1 collective-permute-start.14
  53.7 1.9 collective-permute-start.15
  53.8 46.0 %collective-permute-start.20 = (bf16[2048,512]{1,0:T(8,128)(2,1)}, bf16[2048,512]{1,0:T(8,128)(2,1)}, u32[]{:S(2)}, u32[]{:S(2)}) collective-permute-start(bf16[2048,512]{1,0:T(8,128)(2,1)} %bitcast.16.refs_0_), channel_id=1, source_target_pairs={{0,1},{1,0},{2,3},{3,2},{4,5},{5,4},{6,7},{7,6},{8,9},{9,8},{10,11... | collective-permute-start | bytes 6291464 | tf_op jit(solution)/shard_map/ppermute | solution.py:378
  54.2 45.6 %collective-permute-start.21 = (bf16[2048,512]{1,0:T(8,128)(2,1)}, bf16[2048,512]{1,0:T(8,128)(2,1)}, u32[]{:S(2)}, u32[]{:S(2)}) collective-permute-start(bf16[2048,512]{1,0:T(8,128)(2,1)} %bitcast.17.refs_1_), channel_id=1, source_target_pairs={{0,1},{1,0},{2,3},{3,2},{4,5},{5,4},{6,7},{7,6},{8,9},{9,8},{10,11... | collective-permute-start | bytes 6291464 | tf_op jit(solution)/shard_map/ppermute | solution.py:378
  54.3 45.5 %collective-permute-start.22 = (bf16[512,2048]{1,0:T(8,128)(2,1)}, bf16[512,2048]{1,0:T(8,128)(2,1)}, u32[]{:S(2)}, u32[]{:S(2)}) collective-permute-start(bf16[512,2048]{1,0:T(8,128)(2,1)} %bitcast.18.refs_2_), channel_id=1, source_target_pairs={{0,1},{1,0},{2,3},{3,2},{4,5},{5,4},{6,7},{7,6},{8,9},{9,8},{10,11... | collective-permute-start | bytes 6291464 | tf_op jit(solution)/shard_map/ppermute | solution.py:378
  55.4 14.0 %collective-permute-start.17 = (bf16[256,2048]{1,0:T(8,128)(2,1)S(1)}, bf16[256,2048]{1,0:T(8,128)(2,1)S(1)}, u32[]{:S(2)}, u32[]{:S(2)}) collective-permute-start(bf16[256,2048]{1,0:T(8,128)(2,1)S(1)} %copy-done), channel_id=1, source_target_pairs={{0,1},{1,0},{2,3},{3,2},{4,5},{5,4},{6,7},{7,6},{8,9},{9,8},{10,11... | collective-permute-start | bytes 3145736 | tf_op jit(solution)/shard_map/ppermute | solution.py:378
  55.6 13.8 %collective-permute-start.16 = (bf16[1024,512]{1,0:T(8,128)(2,1)S(1)}, bf16[1024,512]{1,0:T(8,128)(2,1)}, u32[]{:S(2)}, u32[]{:S(2)}) collective-permute-start(bf16[1024,512]{1,0:T(8,128)(2,1)S(1)} %bitcast.28), channel_id=1, source_target_pairs={{0,1},{1,0},{2,3},{3,2},{4,5},{5,4},{6,7},{7,6},{8,9},{9,8},{10,11... | collective-permute-start | bytes 3145736 | tf_op jit(solution)/shard_map/ppermute | solution.py:378
  73.4 8.4 %collective-permute-start.18 = (bf16[64,2048]{1,0:T(8,128)(2,1)S(1)}, bf16[64,2048]{1,0:T(8,128)(2,1)S(1)}, u32[]{:S(2)}, u32[]{:S(2)}) collective-permute-start(bf16[64,2048]{1,0:T(8,128)(2,1)S(1)} %get-tuple-element.60), channel_id=1, source_target_pairs={{0,2},{2,4},{4,6},{6,0},{1,3},{3,5},{5,7},{7,1},{8,10},{10,12},{12... | collective-permute-start | bytes 786440 | tf_op jit(solution)/shard_map/ppermute | solution.py:379
  75.1 8.3 %collective-permute-start.19 = (bf16[64,2048]{1,0:T(8,128)(2,1)S(1)}, bf16[64,2048]{1,0:T(8,128)(2,1)S(1)}, u32[]{:S(2)}, u32[]{:S(2)}) collective-permute-start(bf16[64,2048]{1,0:T(8,128)(2,1)S(1)} %get-tuple-element.61), channel_id=1, source_target_pairs={{0,6},{2,0},{4,2},{6,4},{1,7},{3,1},{5,3},{7,5},{8,14},{10,8},{12,... | collective-permute-start | bytes 786440 | tf_op jit(solution)/shard_map/ppermute | solution.py:380
  85.1 14.7 %collective-permute-start.23 = (bf16[128,2048]{1,0:T(8,128)(2,1)}, bf16[128,2048]{1,0:T(8,128)(2,1)}, u32[]{:S(2)}, u32[]{:S(2)}) collective-permute-start(bf16[128,2048]{1,0:T(8,128)(2,1)} %get-tuple-element.67), channel_id=1, source_target_pairs={{0,2},{2,4},{4,6},{6,0},{1,3},{3,5},{5,7},{7,1},{8,10},{10,12},{12... | collective-permute-start | bytes 1572872 | tf_op jit(solution)/shard_map/ppermute | solution.py:379
  87.5 13.1 %collective-permute-start.24 = (bf16[128,2048]{1,0:T(8,128)(2,1)}, bf16[128,2048]{1,0:T(8,128)(2,1)}, u32[]{:S(2)}, u32[]{:S(2)}) collective-permute-start(bf16[128,2048]{1,0:T(8,128)(2,1)} %get-tuple-element.68), channel_id=1, source_target_pairs={{0,6},{2,0},{4,2},{6,4},{1,7},{3,1},{5,3},{7,5},{8,14},{10,8},{12,... | collective-permute-start | bytes 1572872 | tf_op jit(solution)/shard_map/ppermute | solution.py:380
  190.3 75.9 %copy-start.29 = (bf16[256,1024]{1,0:T(8,128)(2,1)S(1)}, bf16[256,1024]{1,0:T(8,128)(2,1)}, u32[]{:S(2)}) copy-start(bf16[256,1024]{1,0:T(8,128)(2,1)} %copy-done.28) | copy-start | bytes 1572868
  190.3 75.9 %copy-start.46 = (bf16[256,128]{1,0:T(8,128)(2,1)S(1)}, bf16[256,128]{1,0:T(8,128)(2,1)}, u32[]{:S(2)}) copy-start(bf16[256,128]{1,0:T(8,128)(2,1)} %copy-done.45) | copy-start | bytes 196612
  190.3 75.8 %all-to-all-start.2 = ((bf16[64,16,2304]{2,1,0:T(8,128)(2,1)}), bf16[64,16,2304]{2,1,0:T(8,128)(2,1)}, u32[]{:S(2)}, u32[]{:S(2)}) async-start(bf16[64,16,2304]{2,1,0:T(8,128)(2,1)} %bitcast.41), calls=%async_computation.2 | async-start | bytes 9437184 | tf_op jit(solution)/shard_map/all_to_all | solution.py:503
  (48 other events, 117.1 us)
where the time goes:
time: 275 us; the launch traced here: 273 us
  waiting for transfers between devices  80.1 us (29%)
  blocking collectives  62.2 us (23%)
  Pallas kernels  62.1 us (23%)
  starting transfers between devices  34.5 us (13%)
  local copies, waits for them, and re-layouts  29.5 us (11%)
  other arithmetic  3.8 us (1%)
    all_to_all x1, waiting for transfers between devices, exchange(): lax.all_to_all(v.reshape(experts, 2 * SUB, v.shape[1]), ('x', 'y', 'z'),...  63.1 us
    all_to_all x1, blocking collectives, exchange(): lax.all_to_all(v.reshape(experts, 2 * SUB, v.shape[1]), ('x', 'y', 'z'),...  62.2 us
    unnamed x109, local copies, waits for them, and re-layouts  28.8 us
    pallas_call x1, Pallas kernels, ffn(): pl.pallas_call(ffn_kernel, grid=(wide // step,), out_shape=shape((wide, p...  22.7 us
    ppermute x5, waiting for transfers between devices, layer(): to_down = lambda v: lax.ppermute(v, 'z', down)  12.8 us
    all_to_all x1, starting transfers between devices, exchange(): lax.all_to_all(v.reshape(experts, 2 * SUB, v.shape[1]), ('x', 'y', 'z'),...  12 us
    ppermute x5, starting transfers between devices, layer(): to_up = lambda v: lax.ppermute(v, 'z', up)  11.3 us
    pallas_call x3, Pallas kernels, projections(): call(lambda *refs: qkv_kernel(len(pieces), *refs), (shape((count // 2, 2...  10.7 us
  transfers between devices with their start and end apart: 27, of which 8 were waited for; matrix products, arithmetic and copies ran while one was open for 2% of the time, Pallas kernels for 10%

commit v1 on v0

--- a/solution.py
+++ b/solution.py
@@ -31,6 +31,14 @@
         kernel, out_shape=out_shape, in_specs=[vmem()] * n_in, out_specs=outs,
         compiler_params=limit(mib), **kw
     )
+
+
+def near(a):
+    return pltpu.with_memory_space_constraint(a, pltpu.VMEM)
+
+
+def away(a):
+    return pltpu.with_memory_space_constraint(a, pltpu.HBM)
 
 
 def shape(dims, dtype):
@@ -114,51 +122,57 @@
 
 
 def qkv_kernel(count, *refs):
-    pieces = refs[:count]
-    wq, wk, wv = refs[count : count + 2], refs[count + 2 : count + 4], refs[count + 4 : count + 6]
-    cos_ref, sin_ref, q_ref, k_ref, v_ref, x_ref = refs[count + 6 :]
+    pieces, weights, refs = refs[:count], refs[count : count + 6], refs[count + 6 :]
+    cos_ref, sin_ref, q_ref, k_ref, v_ref, x_ref, w_ref, x_sem, w_sem = refs
     at = 0
-    for piece in pieces:
-        x_ref[at : at + piece.shape[0], :] = piece[...]
-        at += piece.shape[0]
-    local = wq[0].shape[1]
-    for side in range(2):
-        for w_ref, o_ref in ((wk[side], k_ref), (wq[side], q_ref)):
-            rows = o_ref.shape[0]
-            mixed = dot(x_ref[:rows, :], w_ref[...])
-            for h in range(local // HD):
-                v = mixed[:, h * HD : (h + 1) * HD]
-                turned = v * cos_ref[:rows, :] + pltpu.roll(v, HD // 2, 1) * sin_ref[:rows, :]
-                col = side * local + h * HD
-                o_ref[:, col : col + HD] = turned.astype(BF)
-        v_ref[:, side * local : (side + 1) * local] = dot(x_ref[...], wv[side][...]).astype(BF)
-
-
-def attend(scale, q_ref, keys, values, pre_refs, bias_ref, o_ref):
+    copies = []
+    for i, piece in enumerate(pieces):
+        n = piece.shape[0]
+        copies.append(pltpu.make_async_copy(piece, x_ref.at[at : at + n], x_sem.at[i]))
+        at += n
+    loads = [pltpu.make_async_copy(w, w_ref.at[i], w_sem.at[i]) for i, w in enumerate(weights)]
+    loads[0].start()
+    for copy in copies:
+        copy.start()
+    for load in loads[1:]:
+        load.start()
+    for copy in copies:
+        copy.wait()
+    local = w_ref.shape[2]
+    for i, load in enumerate(loads):
+        load.wait()
+        o_ref = (k_ref, q_ref, v_ref)[i // 2]
+        rows = o_ref.shape[0]
+        mixed = dot(x_ref[:rows, :], w_ref[i])
+        col = i % 2 * local
+        if o_ref is v_ref:
+            o_ref[:, col : col + local] = mixed.astype(BF)
+            continue
+        for h in range(local // HD):
+            v = mixed[:, h * HD : (h + 1) * HD]
+            turned = v * cos_ref[:rows, :] + pltpu.roll(v, HD // 2, 1) * sin_ref[:rows, :]
+            o_ref[:, col + h * HD : col + (h + 1) * HD] = turned.astype(BF)
+
+
+def attend(scale, q_ref, k_ref, v_ref, pre_refs, bias_ref, o_ref, first):
     local = pre_refs[0].shape[1] // 2
+    rows = o_ref.shape[0]
     nt = (((1,), (1,)), ((), ()))
     for h in range(q_ref.shape[1] // HD):
         side, col = divmod(h * HD, local)
         pre_ref = pre_refs[side]
         cols = slice(h * HD, (h + 1) * HD)
-        q = q_ref[:, cols]
-        scores = [
-            lax.dot_general(q, pre_ref[:, col : col + HD], nt, preferred_element_type=F32)
-        ]
-        at = 0
-        for k_ref in keys:
-            n = k_ref.shape[0]
-            s = lax.dot_general(q, k_ref[:, cols], nt, preferred_element_type=F32)
-            scores.append(s + bias_ref[:, at : at + n])
-            at += n
-        top = jnp.max(scores[0], axis=-1, keepdims=True)
-        for s in scores[1:]:
-            top = jnp.maximum(top, jnp.max(s, axis=-1, keepdims=True))
-        raised = [jnp.exp2((s - top) * scale) for s in scores]
-        total = sum(jnp.sum(e, axis=-1, keepdims=True) for e in raised)
-        out = dot(raised[0].astype(BF), pre_ref[:, local + col : local + col + HD])
-        for e, v_ref in zip(raised[1:], values):
-            out += dot(e.astype(BF), v_ref[:, cols])
+        q = q_ref[first : first + rows, cols]
+        s1 = lax.dot_general(q, pre_ref[:, col : col + HD], nt, preferred_element_type=F32)
+        s2 = lax.dot_general(q, k_ref[:, cols], nt, preferred_element_type=F32) + bias_ref[...]
+        top = jnp.maximum(
+            jnp.max(s1, axis=-1, keepdims=True), jnp.max(s2, axis=-1, keepdims=True)
+        )
+        e1 = jnp.exp2((s1 - top) * scale)
+        e2 = jnp.exp2((s2 - top) * scale)
+        total = jnp.sum(e1, axis=-1, keepdims=True) + jnp.sum(e2, axis=-1, keepdims=True)
+        out = dot(e1.astype(BF), pre_ref[:, local + col : local + col + HD])
+        out += dot(e2.astype(BF), v_ref[:, cols])
         o_ref[:, cols] = (out / total).astype(BF)
 
 
@@ -167,20 +181,20 @@
     return dot(a_ref[:, :local], wa_ref[...]) + dot(a_ref[:, local:], wb_ref[...])
 
 
-def attn_far_kernel(scale, q, k0, k1, k2, v0, v1, v2, pa, pb, bias, wa, wb, o1, o2, tmp):
-    attend(scale, q, (k0, k1, k2), (v0, v1, v2), (pa, pb), bias, tmp)
+def attn_far_kernel(scale, first, q, k, v, pa, pb, bias, wa, wb, o1, o2, tmp):
+    attend(scale, q, k, v, (pa, pb), bias, tmp, first)
     total = project(tmp, wa, wb).astype(BF)
     rows = o1.shape[0]
     o1[...] = total[:rows]
     o2[...] = total[rows:]
 
 
-def attn_near_kernel(scale, q, k0, k1, k2, v0, v1, v2, pa, pb, bias, o):
-    attend(scale, q, (k0, k1, k2), (v0, v1, v2), (pa, pb), bias, o)
-
-
-def attn_own_kernel(scale, q, k0, k1, k2, v0, v1, v2, pa, pb, bias, wa, wb, o, tmp):
-    attend(scale, q, (k0, k1, k2), (v0, v1, v2), (pa, pb), bias, tmp)
+def attn_near_kernel(scale, first, q, k, v, pa, pb, bias, o):
+    attend(scale, q, k, v, (pa, pb), bias, o, first)
+
+
+def attn_own_kernel(scale, first, q, k, v, pa, pb, bias, wa, wb, o, tmp):
+    attend(scale, q, k, v, (pa, pb), bias, tmp, first)
     o[...] = project(tmp, wa, wb)
 
 
@@ -233,7 +247,7 @@
     return pl.pallas_call(
         dispatch_kernel,
         grid=(SUB + 1,),
-        out_shape=(shape((rows, width), BF), shape((wide, width + part), BF)),
+        out_shape=(pltpu.HBM((rows, width), BF), pltpu.HBM((wide, width + part), BF)),
         in_specs=[whole(a) for a in args],
         out_specs=(whole(tokens), pl.BlockSpec((wide, part), lambda b: (0, b))),
         scratch_shapes=[
@@ -380,10 +394,10 @@
     to_down = lambda v: lax.ppermute(v, "z", down)
     half = rows // 2
 
-    part = shape((half, width), BF)
-    normed, first, last = call(norm_kernel, (shape((rows, width), BF), part, part), 2, name="norm")(
-        tokens, attn_gain[None]
-    )
+    part = pltpu.HBM((half, width), BF)
+    normed, first, last = call(
+        norm_kernel, (pltpu.HBM((rows, width), BF), part, part), 2, name="norm"
+    )(away(tokens), away(attn_gain[None]))
     low0 = to_up(first)
     high1 = to_down(last)
     low1 = to_up(last)
@@ -393,16 +407,17 @@
     far1 = to_down(high1)
     near_a = (low0, low1, high0, high1)
     near_b = tuple(swap(v) for v in near_a)
-
+    far_b = swap(far0), swap(far1)
+
+    wk = (w_key, swap(w_key))
+    wq = (w_query, swap(w_query))
+    wv = (w_value, swap(w_value))
     out_b = swap(w_out)
-    wq = (w_query, swap(w_query))
-    wk = (w_key, swap(w_key))
-    wv = (w_value, swap(w_value))
 
     spread = prefix_cache.shape[1]
     outgoing = pl.pallas_call(
         prefix_kernel,
-        out_shape=shape((reqs * spread, 2 * local), BF),
+        out_shape=pltpu.HBM((reqs * spread, 2 * local), BF),
         in_specs=[pl.BlockSpec(memory_space=pltpu.SMEM), vmem()],
         out_specs=vmem(),
         compiler_params=limit(16),
@@ -414,27 +429,10 @@
     own_w = (w_gate[0], w_up[0], w_down[0])
     other_w = tuple(swap(w) for w in own_w)
 
-    blocks = 2 * experts
-    wide = blocks * SUB
-    table, wm, wx = call(
-        route_kernel,
-        [
-            shape((wide + blocks, rows), BF), shape((2 * rows, wide), BF),
-            shape((2 * rows, blocks), BF),
-        ],
-        3,
-        name="route",
-    )(routes, routes.T, route_weights)
-
     mine, yours = core * rows, (1 - core) * rows
     z_low, z_high, z_far = (z + zs - 1) % zs, (z + 1) % zs, (z + 2) % zs
     starts = jnp.stack(
-        [
-            z * 2 * rows + mine, z * 2 * rows + yours,
-            z_low * 2 * rows + mine, z_high * 2 * rows + mine,
-            z_low * 2 * rows + yours, z_high * 2 * rows + yours,
-            z_far * 2 * rows + mine, z_far * 2 * rows + yours,
-        ]
+        [chip * 2 * rows + who for who in (mine, yours) for chip in (z, z_low, z_high, z_far)]
     )
     place = (starts[:, None] + jnp.arange(rows, dtype=jnp.int32)).reshape(-1)
     spots = (PREFIX + place).astype(F32)
@@ -447,54 +445,76 @@
     length = lengths[req]
     bias = jnp.where(place < length, 0.0, -1e30)[None, :]
 
-    def projections(pieces, first, count, name):
-        return call(
-            lambda *refs: qkv_kernel(len(pieces), *refs),
-            (
-                shape((count // 2, 2 * local), BF),
-                shape((count, 2 * local), BF),
-                shape((count, 2 * local), BF),
-            ),
-            len(pieces) + 8,
-            scratch_shapes=[pltpu.VMEM((count, width), BF)],
-            name=name,
-        )(*pieces, *wq, *wk, *wv, cosine[first : first + count], sine[first : first + count])
-
-    q0, k0, v0 = projections((normed, own_b), 0, 2 * rows, "qkv_own")
-    *near_b, k0 = lax.optimization_barrier((*near_b, k0))
-    q1, k1, v1 = projections((*near_a, *near_b), 2 * rows, 4 * rows, "qkv_near")
-    far0, far1, k1 = lax.optimization_barrier((far0, far1, k1))
-    q2, k2, v2 = projections((far0, far1, swap(far0), swap(far1)), 6 * rows, 2 * rows, "qkv_far")
-    cache = (k0, k1, k2, v0, v1, v2, pre_a, pre_b, bias)
+    live = jnp.clip(length - (z * 2 + core) * rows, 0, rows).astype(jnp.int32)[None]
+    routes, cosine, sine, bias, live = lax.optimization_barrier(
+        (routes, cosine, sine, bias, live)
+    )
+
+    blocks = 2 * experts
+    wide = blocks * SUB
+    table, wm, wx = call(
+        route_kernel,
+        [
+            pltpu.HBM((wide + blocks, rows), BF), pltpu.HBM((2 * rows, wide), BF),
+            pltpu.HBM((2 * rows, blocks), BF),
+        ],
+        3,
+        name="route",
+    )(routes, routes.T, route_weights)
+
+    far_b, table = lax.optimization_barrier((far_b, table))
+
+    slots = 2 * zs * rows
+    pieces = (normed, *near_a, far0, far1, own_b, *near_b, *far_b)
+    q, k, v = pl.pallas_call(
+        lambda *refs: qkv_kernel(len(pieces), *refs),
+        out_shape=(
+            pltpu.VMEM((slots // 2, 2 * local), BF),
+            pltpu.VMEM((slots, 2 * local), BF),
+            pltpu.VMEM((slots, 2 * local), BF),
+        ),
+        in_specs=[pl.BlockSpec(memory_space=pl.ANY)] * (len(pieces) + 6) + [vmem()] * 2,
+        out_specs=(vmem(),) * 3,
+        scratch_shapes=[
+            pltpu.VMEM((slots, width), BF),
+            pltpu.VMEM((6, width, local), BF),
+            pltpu.SemaphoreType.DMA((len(pieces),)),
+            pltpu.SemaphoreType.DMA((6,)),
+        ],
+        compiler_params=limit(24),
+        name="qkv",
+    )(*map(away, (*pieces, *wk, *wq, *wv, cosine, sine)))
+    cache = (near(q), near(k), near(v), pre_a, pre_b, bias)
     scale = math.log2(math.e) / math.sqrt(HD)
     tmp = [pltpu.VMEM((rows, 2 * local), BF)]
 
-    far1, far2 = call(
-        functools.partial(attn_far_kernel, scale),
+    sum1, sum2 = call(
+        functools.partial(attn_far_kernel, scale, 3 * rows),
         [shape((half, width), BF)] * 2,
-        12,
+        8,
         scratch_shapes=tmp,
         name="attn_far",
-    )(q2, *cache, w_out, out_b)
-    got1 = to_up(far1)
-    got2 = to_down(far2)
-    near = call(
-        functools.partial(attn_near_kernel, scale), shape((2 * rows, 2 * local), BF), 10,
+    )(*cache, w_out, out_b)
+    got1 = to_up(sum1)
+    got2 = to_down(sum2)
+    around = call(
+        functools.partial(attn_near_kernel, scale, rows),
+        shape((2 * rows, 2 * local), BF),
+        6,
         name="attn_near",
-    )(q1, *cache)
+    )(*cache)
     to_low, to_high = call(
         proj_near_kernel, [shape((rows, width), BF)] * 2, 5, name="proj_near"
-    )(near, w_out, out_b, got1, got2)
-    to_low, to_high, q0 = lax.optimization_barrier((to_low, to_high, q0))
+    )(around, w_out, out_b, got1, got2)
     b1 = to_up(to_high)
     b2 = to_down(to_low)
     own = call(
-        functools.partial(attn_own_kernel, scale),
+        functools.partial(attn_own_kernel, scale, 0),
         shape((rows, width), F32),
-        12,
+        8,
         scratch_shapes=tmp,
         name="attn_own",
-    )(q0, *cache, w_out, out_b)
+    )(*cache, w_out, out_b)
     own, other_w = lax.optimization_barrier((own, other_w))
 
     hidden, send = dispatch(tokens, own, b1, b2, moe_gain[None], table)
@@ -505,7 +525,6 @@
         ).reshape(v.shape)
 
     back = exchange(ffn(exchange(send), own_w, other_w))
-    live = jnp.clip(length - (z * 2 + core) * rows, 0, rows).astype(jnp.int32)[None]
     return combine(live, back, wm, wx, hidden)
 
 

time: 275 us -> 271 us (0.985)
  the two profiles are of different devices: /device:TPU:82 before, /device:TPU:24 now
where the time goes in v1:
time: 271 us; the launch traced here: 268 us
  blocking collectives  129 us (48%)
  Pallas kernels  67.5 us (25%)
  waiting for transfers between devices  38.6 us (14%)
  starting transfers between devices  24.1 us (9%)
  local copies, waits for them, and re-layouts  4.29 us (2%)
  other arithmetic  4.01 us (1%)
    all_to_all x2, blocking collectives, exchange(): lax.all_to_all(v.reshape(experts, 2 * SUB, v.shape[1]), ('x', 'y', 'z'),...  129 us
    pallas_call x1, Pallas kernels, ffn(): pl.pallas_call(ffn_kernel, grid=(wide // step,), out_shape=shape((wide, p...  21.2 us
    ppermute x5, waiting for transfers between devices, layer(): to_up = lambda v: lax.ppermute(v, 'z', up)  21.2 us
    pallas_call x1, Pallas kernels, layer(): pl.pallas_call(lambda *refs: qkv_kernel(len(pieces), *refs), out_shape=(p...  17 us
    ppermute x5, starting transfers between devices, layer(): to_down = lambda v: lax.ppermute(v, 'z', down)  14.2 us
    all_to_all x1, waiting for transfers between devices, layer(): lax.all_to_all(outgoing, ('x', 'y'), split_axis=0, concat_axis=0, tiled=T...  9.53 us
    all_to_all x1, starting transfers between devices, layer(): lax.all_to_all(outgoing, ('x', 'y'), split_axis=0, concat_axis=0, tiled=T...  7.17 us
    pallas_call x1, Pallas kernels, dispatch(): pl.pallas_call(dispatch_kernel, grid=(SUB + 1,), out_shape=(pltpu.HBM((ro...  6.22 us
  transfers between devices with their start and end apart: 26, of which 11 were waited for; matrix products, arithmetic and copies ran while one was open for 2% of the time, Pallas kernels for 12%

profile of v1, /device:TPU:24, one launch (start us, length us, event | category | flops | bytes accessed | tf_op | source)
XLA Modules:
  0.0 268.3 jit_solution(10538968884856639670)
XLA Ops:
  0.0 2.2 norm.1
  2.2 4.0 %collective-permute-start.2 = (bf16[64,2048]{1,0:T(8,128)(2,1)}, bf16[64,2048]{1,0:T(8,128)(2,1)S(1)}, u32[]{:S(2)}, u32[]{:S(2)}) collective-permute-start(bf16[64,2048]{1,0:T(8,128)(2,1)} %get-tuple-element.34), channel_id=1, source_target_pairs={{0,6},{2,0},{4,2},{6,4},{1,7},{3,1},{5,3},{7,5},{8,14},{10,8},{12,... | collective-permute-start | bytes 786440 | tf_op jit(solution)/shard_map/ppermute | solution.py:394
  6.2 3.2 %collective-permute-start.3 = (bf16[64,2048]{1,0:T(8,128)(2,1)}, bf16[64,2048]{1,0:T(8,128)(2,1)}, u32[]{:S(2)}, u32[]{:S(2)}) collective-permute-start(bf16[64,2048]{1,0:T(8,128)(2,1)} %get-tuple-element.35), channel_id=1, source_target_pairs={{0,6},{2,0},{4,2},{6,4},{1,7},{3,1},{5,3},{7,5},{8,14},{10,8},{12,... | collective-permute-start | bytes 786440 | tf_op jit(solution)/shard_map/ppermute | solution.py:394
  9.4 3.8 %collective-permute-done.2.refs_3_ = bf16[64,2048]{1,0:T(8,128)(2,1)S(1)} collective-permute-done((bf16[64,2048]{1,0:T(8,128)(2,1)}, bf16[64,2048]{1,0:T(8,128)(2,1)S(1)}, u32[]{:S(2)}, u32[]{:S(2)}) %collective-permute-start.2) | collective-permute-done | bytes 262176 | tf_op jit(solution)/shard_map/ppermute | solution.py:394
  13.2 3.6 %collective-permute-done.refs_1_ = bf16[64,2048]{1,0:T(8,128)(2,1)S(1)} collective-permute-done((bf16[64,2048]{1,0:T(8,128)(2,1)}, bf16[64,2048]{1,0:T(8,128)(2,1)S(1)}, u32[]{:S(2)}, u32[]{:S(2)}) %collective-permute-start) | collective-permute-done | bytes 262176 | tf_op jit(solution)/shard_map/ppermute | solution.py:393
  16.8 0.9 collective-permute-done.3.refs_4_
  17.7 3.3 %collective-permute-done.1.refs_2_ = bf16[64,2048]{1,0:T(8,128)(2,1)S(1)} collective-permute-done((bf16[64,2048]{1,0:T(8,128)(2,1)}, bf16[64,2048]{1,0:T(8,128)(2,1)S(1)}, u32[]{:S(2)}, u32[]{:S(2)}) %collective-permute-start.1) | collective-permute-done | bytes 262176 | tf_op jit(solution)/shard_map/ppermute | solution.py:393
  22.0 4.7 %collective-permute-done.4.refs_5_ = bf16[64,2048]{1,0:T(8,128)(2,1)S(1)} collective-permute-done((bf16[64,2048]{1,0:T(8,128)(2,1)S(1)}, bf16[64,2048]{1,0:T(8,128)(2,1)S(1)}, u32[]{:S(2)}, u32[]{:S(2)}) %collective-permute-start.4) | collective-permute-done | bytes 262176 | tf_op jit(solution)/shard_map/ppermute | solution.py:393
  28.0 1.1 copy.20
  29.1 0.7 copy-done.11
  29.9 1.6 prefix.1
  31.5 7.2 %all-to-all-start = ((bf16[16,64,512]{2,1,0:T(8,128)(2,1)}), bf16[16,64,512]{2,1,0:T(8,128)(2,1)S(1)}, u32[]{:S(2)}, u32[]{:S(2)}) async-start(bf16[16,64,512]{2,1,0:T(8,128)(2,1)} %bitcast.49), calls=%async_computation | async-start | bytes 2097152 | tf_op jit(solution)/shard_map/all_to_all | solution.py:426
  38.7 1.7 collective-permute-done.8.refs_9_
  41.0 1.2 collective-permute-done.11.refs_12_
  44.2 9.5 %all-to-all-done = bf16[16,64,512]{2,1,0:T(8,128)(2,1)S(1)} async-done(((bf16[16,64,512]{2,1,0:T(8,128)(2,1)}), bf16[16,64,512]{2,1,0:T(8,128)(2,1)S(1)}, u32[]{:S(2)}, u32[]{:S(2)}) %all-to-all-start) | async-done | bytes 1048608 | tf_op jit(solution)/shard_map/all_to_all | solution.py:426
  55.3 1.9 fusion
  57.2 1.3 pad_maximum_fusion
  59.3 1.6 route.1
  61.0 17.0 %qkv.1 = (bf16[512,512]{1,0:T(8,128)(2,1)S(1)}, bf16[1024,512]{1,0:T(8,128)(2,1)S(1)}, bf16[1024,512]{1,0:T(8,128)(2,1)S(1)}) custom-call(bf16[128,2048]{1,0:T(8,128)(2,1)} %get-tuple-element.33.refs_0_, bf16[64,2048]{1,0:T(8,128)(2,1)} %copy-done.14, bf16[64,2048]{1,0:T(8,128)(2,1)} %copy-done.15, bf16[64,2048]{1,0:T(8,128)(2,1)} %copy-done.13, ...), custom_call_target="tpu_custom_call" | custom-call | tf_op jit(solution)/shard_map/qkv/pallas_call | solution.py:469
  78.0 3.8 %attn_far.1 = (bf16[64,2048]{1,0:T(8,128)(2,1)S(1)}, bf16[64,2048]{1,0:T(8,128)(2,1)S(1)}) custom-call(bf16[512,512]{1,0:T(8,128)(2,1)S(1)} %get-tuple-element.42.q, bf16[1024,512]{1,0:T(8,128)(2,1)S(1)} %get-tuple-element.43.k, bf16[1024,512]{1,0:T(8,128)(2,1)S(1)} %get-tuple-element.44.v, bf16[1024,512]{1,0:T(8,128)(2,1)S(1)} %bitcast.31, ...), custom_call_target="tpu_custom_call" | custom-call | tf_op jit(solution)/shard_map/attn_far/pallas_call | solution.py:491
  81.9 3.2 %collective-permute-start.22 = (bf16[64,2048]{1,0:T(8,128)(2,1)S(1)}, bf16[64,2048]{1,0:T(8,128)(2,1)S(1)}, u32[]{:S(2)}, u32[]{:S(2)}) collective-permute-start(bf16[64,2048]{1,0:T(8,128)(2,1)S(1)} %get-tuple-element.48), channel_id=1, source_target_pairs={{0,6},{2,0},{4,2},{6,4},{1,7},{3,1},{5,3},{7,5},{8,14},{10,8},{12,... | collective-permute-start | bytes 786440 | tf_op jit(solution)/shard_map/ppermute | solution.py:394
  85.1 4.7 %attn_near.1.a_ref = bf16[256,512]{1,0:T(8,128)(2,1)S(1)} custom-call(bf16[512,512]{1,0:T(8,128)(2,1)S(1)} %get-tuple-element.42.q, bf16[1024,512]{1,0:T(8,128)(2,1)S(1)} %get-tuple-element.43.k, bf16[1024,512]{1,0:T(8,128)(2,1)S(1)} %get-tuple-element.44.v, bf16[1024,512]{1,0:T(8,128)(2,1)S(1)} %bitcast.32, bf16[1024,512]{1,0:T(8,128)(2,1)} %collective-permute-done.16.pb, ...), custom_call_target="tpu_custom_call" | custom-call | tf_op jit(solution)/shard_map/attn_near/pallas_call | solution.py:500
  89.8 2.0 collective-permute-done.21.got1
  91.8 0.7 proj_near.1
  92.7 3.2 %collective-permute-start.24 = (bf16[128,2048]{1,0:T(8,128)(2,1)S(1)}, bf16[128,2048]{1,0:T(8,128)(2,1)S(1)}, u32[]{:S(2)}, u32[]{:S(2)}) collective-permute-start(bf16[128,2048]{1,0:T(8,128)(2,1)S(1)} %get-tuple-element.50), channel_id=1, source_target_pairs={{0,6},{2,0},{4,2},{6,4},{1,7},{3,1},{5,3},{7,5},{8,14},{10,8},{12,... | collective-permute-start | bytes 1572872 | tf_op jit(solution)/shard_map/ppermute | solution.py:394
  95.9 3.8 %attn_own.1.own_ref = f32[128,2048]{1,0:T(8,128)S(1)} custom-call(bf16[512,512]{1,0:T(8,128)(2,1)S(1)} %get-tuple-element.42.q, bf16[1024,512]{1,0:T(8,128)(2,1)S(1)} %get-tuple-element.43.k, bf16[1024,512]{1,0:T(8,128)(2,1)S(1)} %get-tuple-element.44.v, bf16[1024,512]{1,0:T(8,128)(2,1)S(1)} %bitcast.33, bf16[1024,512]{1,0:T(8,128)(2,1)} %collective-permute-done.16.pb, ...), custom_call_target="tpu_custom_call" | custom-call | tf_op jit(solution)/shard_map/attn_own/pallas_call | solution.py:511
  99.7 7.6 %collective-permute-done.23.b1_ref = bf16[128,2048]{1,0:T(8,128)(2,1)S(1)} collective-permute-done((bf16[128,2048]{1,0:T(8,128)(2,1)S(1)}, bf16[128,2048]{1,0:T(8,128)(2,1)S(1)}, u32[]{:S(2)}, u32[]{:S(2)}) %collective-permute-start.23) | collective-permute-done | bytes 524320 | tf_op jit(solution)/shard_map/ppermute | solution.py:393
  107.3 6.2 %dispatch.1 = (bf16[128,2048]{1,0:T(8,128)(2,1)}, bf16[1024,2304]{1,0:T(8,128)(2,1)}) custom-call(bf16[128,2048]{1,0:T(8,128)(2,1)S(1)} %copy-done.1, f32[128,2048]{1,0:T(8,128)S(1)} %attn_own.1.own_ref, bf16[128,2048]{1,0:T(8,128)(2,1)S(1)} %collective-permute-done.23.b1_ref, bf16[128,2048]{1,0:T(8,128)(2,1)S(1)} %collective-permute-done.24.b2_ref, ...), custom_call_target="tpu_custom_call" | custom-call | tf_op jit(solution)/shard_map/dispatch/pallas_call | solution.py:247
  113.6 64.2 %all_to_all.21 = bf16[64,16,2304]{2,1,0:T(8,128)(2,1)} all-to-all(bf16[64,16,2304]{2,1,0:T(8,128)(2,1)} %bitcast.48), channel_id=1, replica_groups=mesh['x'=4,'y'=4,'z'=4,'c'=2] {'x','y','z'}, dimensions={0} | all-to-all | bytes 9437184 | tf_op jit(solution)/shard_map/all_to_all | solution.py:523
  177.7 21.2 %ffn.1 = bf16[1024,2304]{1,0:T(8,128)(2,1)} custom-call(bf16[1024,2304]{1,0:T(8,128)(2,1)} %bitcast.46, bf16[2048,512]{1,0:T(8,128)(2,1)S(1)} %bitcast.36, bf16[2048,512]{1,0:T(8,128)(2,1)S(1)} %bitcast.38, bf16[512,2048]{1,0:T(8,128)(2,1)S(1)} %bitcast.40, bf16[2048,512]{1,0:T(8,128)(2,1)} %collective-permute-done.18.refs_3_, ...), custom_call_target="tpu_custom_call" | custom-call | tf_op jit(solution)/shard_map/ffn/pallas_call | solution.py:319
  199.0 64.5 %all_to_all.22 = bf16[64,16,2304]{2,1,0:T(8,128)(2,1)S(1)} all-to-all(bf16[64,16,2304]{2,1,0:T(8,128)(2,1)} %bitcast.47), channel_id=1, replica_groups=mesh['x'=4,'y'=4,'z'=4,'c'=2] {'x','y','z'}, dimensions={0} | all-to-all | bytes 9437184 | tf_op jit(solution)/shard_map/all_to_all | solution.py:523
  263.6 4.7 %combine.1 = bf16[128,2048]{1,0:T(8,128)(2,1)} custom-call(s32[1]{0:T(128)} %bitcast.11.live_ref, bf16[1024,2304]{1,0:T(8,128)(2,1)S(1)} %bitcast.28, bf16[1024,2304]{1,0:T(8,128)(2,1)S(1)} %bitcast.29, bf16[256,1024]{1,0:T(8,128)(2,1)S(1)} %copy-done.5, bf16[256,128]{1,0:T(8,128)(2,1)S(1)} %copy-done.8, bf16[128,2048]{1,0:T(8,128)(2,1)S(1)} %copy-done.6), custom_call_target="tpu_custom_call" | custom-call | tf_op jit(solution)/shard_map/combine/pallas_call | solution.py:363
  (93 shorter events, 6.8 us)
Async XLA Ops:
  2.2 11.0 %collective-permute-start.2 = (bf16[64,2048]{1,0:T(8,128)(2,1)}, bf16[64,2048]{1,0:T(8,128)(2,1)S(1)}, u32[]{:S(2)}, u32[]{:S(2)}) collective-permute-start(bf16[64,2048]{1,0:T(8,128)(2,1)} %get-tuple-element.34), channel_id=1, source_target_pairs={{0,6},{2,0},{4,2},{6,4},{1,7},{3,1},{5,3},{7,5},{8,14},{10,8},{12,... | collective-permute-start | bytes 786440 | tf_op jit(solution)/shard_map/ppermute | solution.py:394
  6.2 10.6 %collective-permute-start = (bf16[64,2048]{1,0:T(8,128)(2,1)}, bf16[64,2048]{1,0:T(8,128)(2,1)S(1)}, u32[]{:S(2)}, u32[]{:S(2)}) collective-permute-start(bf16[64,2048]{1,0:T(8,128)(2,1)} %get-tuple-element.34), channel_id=1, source_target_pairs={{0,2},{2,4},{4,6},{6,0},{1,3},{3,5},{5,7},{7,1},{8,10},{10,12},{12... | collective-permute-start | bytes 786440 | tf_op jit(solution)/shard_map/ppermute | solution.py:393
  6.2 11.5 %collective-permute-start.3 = (bf16[64,2048]{1,0:T(8,128)(2,1)}, bf16[64,2048]{1,0:T(8,128)(2,1)}, u32[]{:S(2)}, u32[]{:S(2)}) collective-permute-start(bf16[64,2048]{1,0:T(8,128)(2,1)} %get-tuple-element.35), channel_id=1, source_target_pairs={{0,6},{2,0},{4,2},{6,4},{1,7},{3,1},{5,3},{7,5},{8,14},{10,8},{12,... | collective-permute-start | bytes 786440 | tf_op jit(solution)/shard_map/ppermute | solution.py:394
  9.4 11.6 %collective-permute-start.1 = (bf16[64,2048]{1,0:T(8,128)(2,1)}, bf16[64,2048]{1,0:T(8,128)(2,1)S(1)}, u32[]{:S(2)}, u32[]{:S(2)}) collective-permute-start(bf16[64,2048]{1,0:T(8,128)(2,1)} %get-tuple-element.35), channel_id=1, source_target_pairs={{0,2},{2,4},{4,6},{6,0},{1,3},{3,5},{5,7},{7,1},{8,10},{10,12},{12... | collective-permute-start | bytes 786440 | tf_op jit(solution)/shard_map/ppermute | solution.py:393
  13.2 7.8 %collective-permute-start.9 = (bf16[64,2048]{1,0:T(8,128)(2,1)S(1)}, bf16[64,2048]{1,0:T(8,128)(2,1)S(1)}, u32[]{:S(2)}, u32[]{:S(2)}) collective-permute-start(bf16[64,2048]{1,0:T(8,128)(2,1)S(1)} %collective-permute-done.2.refs_3_), channel_id=1, source_target_pairs={{0,1},{1,0},{2,3},{3,2},{4,5},{5,4},{6,7},{7,6},{8,9},{9,8},{10,11... | collective-permute-start | bytes 786440 | tf_op jit(solution)/shard_map/ppermute | solution.py:392
  16.8 4.7 %collective-permute-start.7 = (bf16[64,2048]{1,0:T(8,128)(2,1)S(1)}, bf16[64,2048]{1,0:T(8,128)(2,1)S(1)}, u32[]{:S(2)}, u32[]{:S(2)}) collective-permute-start(bf16[64,2048]{1,0:T(8,128)(2,1)S(1)} %collective-permute-done.refs_1_), channel_id=1, source_target_pairs={{0,1},{1,0},{2,3},{3,2},{4,5},{5,4},{6,7},{7,6},{8,9},{9,8},{10,11... | collective-permute-start | bytes 786440 | tf_op jit(solution)/shard_map/ppermute | solution.py:392
  16.8 9.9 %collective-permute-start.4 = (bf16[64,2048]{1,0:T(8,128)(2,1)S(1)}, bf16[64,2048]{1,0:T(8,128)(2,1)S(1)}, u32[]{:S(2)}, u32[]{:S(2)}) collective-permute-start(bf16[64,2048]{1,0:T(8,128)(2,1)S(1)} %collective-permute-done.refs_1_), channel_id=1, source_target_pairs={{0,2},{2,4},{4,6},{6,0},{1,3},{3,5},{5,7},{7,1},{8,10},{10,12},{12... | collective-permute-start | bytes 786440 | tf_op jit(solution)/shard_map/ppermute | solution.py:393
  17.7 9.0 %collective-permute-start.10 = (bf16[64,2048]{1,0:T(8,128)(2,1)}, bf16[64,2048]{1,0:T(8,128)(2,1)S(1)}, u32[]{:S(2)}, u32[]{:S(2)}) collective-permute-start(bf16[64,2048]{1,0:T(8,128)(2,1)} %collective-permute-done.3.refs_4_), channel_id=1, source_target_pairs={{0,1},{1,0},{2,3},{3,2},{4,5},{5,4},{6,7},{7,6},{8,9},{9,8},{10,11... | collective-permute-start | bytes 786440 | tf_op jit(solution)/shard_map/ppermute | solution.py:392
  21.0 21.7 %collective-permute-start.14 = (bf16[2048,256]{1,0:T(8,128)(2,1)}, bf16[2048,256]{1,0:T(8,128)(2,1)S(1)}, u32[]{:S(2)}, u32[]{:S(2)}) collective-permute-start(bf16[2048,256]{1,0:T(8,128)(2,1)} %refs_16_.1), channel_id=1, source_target_pairs={{0,1},{1,0},{2,3},{3,2},{4,5},{5,4},{6,7},{7,6},{8,9},{9,8},{10,11... | collective-permute-start | bytes 3145736 | tf_op jit(solution)/shard_map/ppermute | solution.py:392
  21.0 22.7 %collective-permute-start.13 = (bf16[2048,256]{1,0:T(8,128)(2,1)}, bf16[2048,256]{1,0:T(8,128)(2,1)}, u32[]{:S(2)}, u32[]{:S(2)}) collective-permute-start(bf16[2048,256]{1,0:T(8,128)(2,1)} %refs_14_.1), channel_id=1, source_target_pairs={{0,1},{1,0},{2,3},{3,2},{4,5},{5,4},{6,7},{7,6},{8,9},{9,8},{10,11... | collective-permute-start | bytes 3145736 | tf_op jit(solution)/shard_map/ppermute | solution.py:392
  21.5 17.1 %collective-permute-start.5 = (bf16[64,2048]{1,0:T(8,128)(2,1)}, bf16[64,2048]{1,0:T(8,128)(2,1)}, u32[]{:S(2)}, u32[]{:S(2)}) collective-permute-start(bf16[64,2048]{1,0:T(8,128)(2,1)} %collective-permute-done.3.refs_4_), channel_id=1, source_target_pairs={{0,6},{2,0},{4,2},{6,4},{1,7},{3,1},{5,3},{7,5},{8,14},{10,8},{12,... | collective-permute-start | bytes 786440 | tf_op jit(solution)/shard_map/ppermute | solution.py:394
  26.7 27.0 %collective-permute-start.15 = (bf16[2048,256]{1,0:T(8,128)(2,1)}, bf16[2048,256]{1,0:T(8,128)(2,1)}, u32[]{:S(2)}, u32[]{:S(2)}) collective-permute-start(bf16[2048,256]{1,0:T(8,128)(2,1)} %refs_18_.1), channel_id=1, source_target_pairs={{0,1},{1,0},{2,3},{3,2},{4,5},{5,4},{6,7},{7,6},{8,9},{9,8},{10,11... | collective-permute-start | bytes 3145736 | tf_op jit(solution)/shard_map/ppermute | solution.py:392
  27.6 13.0 %collective-permute-start.6 = (bf16[128,2048]{1,0:T(8,128)(2,1)}, bf16[128,2048]{1,0:T(8,128)(2,1)}, u32[]{:S(2)}, u32[]{:S(2)}) collective-permute-start(bf16[128,2048]{1,0:T(8,128)(2,1)} %get-tuple-element.33.refs_0_), channel_id=1, source_target_pairs={{0,1},{1,0},{2,3},{3,2},{4,5},{5,4},{6,7},{7,6},{8,9},{9,8},{10,11... | collective-permute-start | bytes 1572872 | tf_op jit(solution)/shard_map/ppermute | solution.py:392
  31.5 22.2 %all-to-all-start = ((bf16[16,64,512]{2,1,0:T(8,128)(2,1)}), bf16[16,64,512]{2,1,0:T(8,128)(2,1)S(1)}, u32[]{:S(2)}, u32[]{:S(2)}) async-start(bf16[16,64,512]{2,1,0:T(8,128)(2,1)} %bitcast.49), calls=%async_computation | async-start | bytes 2097152 | tf_op jit(solution)/shard_map/all_to_all | solution.py:426
  38.6 1.8 collective-permute-start.8
  40.5 1.7 collective-permute-start.11
  40.6 2.0 collective-permute-start.12
  42.2 57.5 %collective-permute-start.18 = (bf16[2048,512]{1,0:T(8,128)(2,1)}, bf16[2048,512]{1,0:T(8,128)(2,1)}, u32[]{:S(2)}, u32[]{:S(2)}) collective-permute-start(bf16[2048,512]{1,0:T(8,128)(2,1)} %bitcast.35), channel_id=1, source_target_pairs={{0,1},{1,0},{2,3},{3,2},{4,5},{5,4},{6,7},{7,6},{8,9},{9,8},{10,11... | collective-permute-start | bytes 6291464 | tf_op jit(solution)/shard_map/ppermute | solution.py:392
  42.6 57.1 %collective-permute-start.19 = (bf16[2048,512]{1,0:T(8,128)(2,1)}, bf16[2048,512]{1,0:T(8,128)(2,1)}, u32[]{:S(2)}, u32[]{:S(2)}) collective-permute-start(bf16[2048,512]{1,0:T(8,128)(2,1)} %bitcast.37), channel_id=1, source_target_pairs={{0,1},{1,0},{2,3},{3,2},{4,5},{5,4},{6,7},{7,6},{8,9},{9,8},{10,11... | collective-permute-start | bytes 6291464 | tf_op jit(solution)/shard_map/ppermute | solution.py:392
  42.7 57.0 %collective-permute-start.20 = (bf16[512,2048]{1,0:T(8,128)(2,1)}, bf16[512,2048]{1,0:T(8,128)(2,1)}, u32[]{:S(2)}, u32[]{:S(2)}) collective-permute-start(bf16[512,2048]{1,0:T(8,128)(2,1)} %bitcast.39), channel_id=1, source_target_pairs={{0,1},{1,0},{2,3},{3,2},{4,5},{5,4},{6,7},{7,6},{8,9},{9,8},{10,11... | collective-permute-start | bytes 6291464 | tf_op jit(solution)/shard_map/ppermute | solution.py:392
  43.7 34.3 %collective-permute-start.17 = (bf16[256,2048]{1,0:T(8,128)(2,1)S(1)}, bf16[256,2048]{1,0:T(8,128)(2,1)S(1)}, u32[]{:S(2)}, u32[]{:S(2)}) collective-permute-start(bf16[256,2048]{1,0:T(8,128)(2,1)S(1)} %copy-done), channel_id=1, source_target_pairs={{0,1},{1,0},{2,3},{3,2},{4,5},{5,4},{6,7},{7,6},{8,9},{9,8},{10,11... | collective-permute-start | bytes 3145736 | tf_op jit(solution)/shard_map/ppermute | solution.py:392
  53.7 24.3 %collective-permute-start.16 = (bf16[1024,512]{1,0:T(8,128)(2,1)S(1)}, bf16[1024,512]{1,0:T(8,128)(2,1)}, u32[]{:S(2)}, u32[]{:S(2)}) collective-permute-start(bf16[1024,512]{1,0:T(8,128)(2,1)S(1)} %bitcast.30), channel_id=1, source_target_pairs={{0,1},{1,0},{2,3},{3,2},{4,5},{5,4},{6,7},{7,6},{8,9},{9,8},{10,11... | collective-permute-start | bytes 3145736 | tf_op jit(solution)/shard_map/ppermute | solution.py:392
  81.8 10.0 %collective-permute-start.21 = (bf16[64,2048]{1,0:T(8,128)(2,1)S(1)}, bf16[64,2048]{1,0:T(8,128)(2,1)S(1)}, u32[]{:S(2)}, u32[]{:S(2)}) collective-permute-start(bf16[64,2048]{1,0:T(8,128)(2,1)S(1)} %get-tuple-element.47), channel_id=1, source_target_pairs={{0,2},{2,4},{4,6},{6,0},{1,3},{3,5},{5,7},{7,1},{8,10},{10,12},{12... | collective-permute-start | bytes 786440 | tf_op jit(solution)/shard_map/ppermute | solution.py:393
  81.9 9.9 %collective-permute-start.22 = (bf16[64,2048]{1,0:T(8,128)(2,1)S(1)}, bf16[64,2048]{1,0:T(8,128)(2,1)S(1)}, u32[]{:S(2)}, u32[]{:S(2)}) collective-permute-start(bf16[64,2048]{1,0:T(8,128)(2,1)S(1)} %get-tuple-element.48), channel_id=1, source_target_pairs={{0,6},{2,0},{4,2},{6,4},{1,7},{3,1},{5,3},{7,5},{8,14},{10,8},{12,... | collective-permute-start | bytes 786440 | tf_op jit(solution)/shard_map/ppermute | solution.py:394
  92.6 14.8 %collective-permute-start.23 = (bf16[128,2048]{1,0:T(8,128)(2,1)S(1)}, bf16[128,2048]{1,0:T(8,128)(2,1)S(1)}, u32[]{:S(2)}, u32[]{:S(2)}) collective-permute-start(bf16[128,2048]{1,0:T(8,128)(2,1)S(1)} %get-tuple-element.49), channel_id=1, source_target_pairs={{0,2},{2,4},{4,6},{6,0},{1,3},{3,5},{5,7},{7,1},{8,10},{10,12},{12... | collective-permute-start | bytes 1572872 | tf_op jit(solution)/shard_map/ppermute | solution.py:393
  92.7 14.6 %collective-permute-start.24 = (bf16[128,2048]{1,0:T(8,128)(2,1)S(1)}, bf16[128,2048]{1,0:T(8,128)(2,1)S(1)}, u32[]{:S(2)}, u32[]{:S(2)}) collective-permute-start(bf16[128,2048]{1,0:T(8,128)(2,1)S(1)} %get-tuple-element.50), channel_id=1, source_target_pairs={{0,6},{2,0},{4,2},{6,4},{1,7},{3,1},{5,3},{7,5},{8,14},{10,8},{12,... | collective-permute-start | bytes 1572872 | tf_op jit(solution)/shard_map/ppermute | solution.py:394
  113.5 64.2 %copy-start.2 = (bf16[1,2048,512]{2,1,0:T(8,128)(2,1)S(1)}, bf16[1,2048,512]{2,1,0:T(8,128)(2,1)}, u32[]{:S(2)}) copy-start(bf16[1,2048,512]{2,1,0:T(8,128)(2,1)} %param.25) | copy-start | bytes 6291460
  113.5 64.2 %copy-start.3 = (bf16[1,2048,512]{2,1,0:T(8,128)(2,1)S(1)}, bf16[1,2048,512]{2,1,0:T(8,128)(2,1)}, u32[]{:S(2)}) copy-start(bf16[1,2048,512]{2,1,0:T(8,128)(2,1)} %param.26) | copy-start | bytes 6291460
  113.6 64.2 %copy-start.4 = (bf16[1,512,2048]{2,1,0:T(8,128)(2,1)S(1)}, bf16[1,512,2048]{2,1,0:T(8,128)(2,1)}, u32[]{:S(2)}) copy-start(bf16[1,512,2048]{2,1,0:T(8,128)(2,1)} %param.27) | copy-start | bytes 6291460
  199.0 64.6 %copy-start.5 = (bf16[256,1024]{1,0:T(8,128)(2,1)S(1)}, bf16[256,1024]{1,0:T(8,128)(2,1)}, u32[]{:S(2)}) copy-start(bf16[256,1024]{1,0:T(8,128)(2,1)} %get-tuple-element.56.wm_ref) | copy-start | bytes 1572868
  199.0 64.6 %copy-start.6 = (bf16[128,2048]{1,0:T(8,128)(2,1)S(1)}, bf16[128,2048]{1,0:T(8,128)(2,1)}, u32[]{:S(2)}) copy-start(bf16[128,2048]{1,0:T(8,128)(2,1)} %get-tuple-element.58.h_ref) | copy-start | bytes 1572868
  199.0 64.6 %copy-start.8 = (bf16[256,128]{1,0:T(8,128)(2,1)S(1)}, bf16[256,128]{1,0:T(8,128)(2,1)}, u32[]{:S(2)}) copy-start(bf16[256,128]{1,0:T(8,128)(2,1)} %get-tuple-element.57.wx_ref) | copy-start | bytes 196612
  (19 other events, 187.7 us)

commit v2 on v1

--- a/solution.py
+++ b/solution.py
@@ -130,28 +130,33 @@
         n = piece.shape[0]
         copies.append(pltpu.make_async_copy(piece, x_ref.at[at : at + n], x_sem.at[i]))
         at += n
-    loads = [pltpu.make_async_copy(w, w_ref.at[i], w_sem.at[i]) for i, w in enumerate(weights)]
-    loads[0].start()
+    local = w_ref.shape[2] // 2
+    loads = [
+        pltpu.make_async_copy(
+            w, w_ref.at[i // 2, :, i % 2 * local : (i % 2 + 1) * local], w_sem.at[i]
+        )
+        for i, w in enumerate(weights)
+    ]
+    for load in loads[:2]:
+        load.start()
     for copy in copies:
         copy.start()
-    for load in loads[1:]:
+    for load in loads[2:]:
         load.start()
     for copy in copies:
         copy.wait()
-    local = w_ref.shape[2]
-    for i, load in enumerate(loads):
-        load.wait()
-        o_ref = (k_ref, q_ref, v_ref)[i // 2]
+    for i, o_ref in enumerate((k_ref, q_ref, v_ref)):
+        loads[2 * i].wait()
+        loads[2 * i + 1].wait()
         rows = o_ref.shape[0]
         mixed = dot(x_ref[:rows, :], w_ref[i])
-        col = i % 2 * local
         if o_ref is v_ref:
-            o_ref[:, col : col + local] = mixed.astype(BF)
+            o_ref[...] = mixed.astype(BF)
             continue
-        for h in range(local // HD):
+        for h in range(2 * local // HD):
             v = mixed[:, h * HD : (h + 1) * HD]
             turned = v * cos_ref[:rows, :] + pltpu.roll(v, HD // 2, 1) * sin_ref[:rows, :]
-            o_ref[:, col + h * HD : col + (h + 1) * HD] = turned.astype(BF)
+            o_ref[:, h * HD : (h + 1) * HD] = turned.astype(BF)
 
 
 def attend(scale, q_ref, k_ref, v_ref, pre_refs, bias_ref, o_ref, first):
@@ -189,8 +194,14 @@
     o2[...] = total[rows:]
 
 
-def attn_near_kernel(scale, first, q, k, v, pa, pb, bias, o):
-    attend(scale, q, k, v, (pa, pb), bias, o, first)
+def attn_near_kernel(
+    scale, first, q, k, v, pa, pb, bias, wa, wb, low_free, low_need, high_need, high_free, tmp
+):
+    attend(scale, q, k, v, (pa, pb), bias, tmp, first)
+    total = project(tmp, wa, wb)
+    n = low_free.shape[0]
+    for i, o_ref in enumerate((low_free, low_need, high_need, high_free)):
+        o_ref[...] = total[i * n : (i + 1) * n].astype(o_ref.dtype)
 
 
 def attn_own_kernel(scale, first, q, k, v, pa, pb, bias, wa, wb, o, tmp):
@@ -198,83 +209,95 @@
     o[...] = project(tmp, wa, wb)
 
 
-def proj_near_kernel(a_ref, wa, wb, got1, got2, low_ref, high_ref):
-    total = project(a_ref, wa, wb)
-    rows = low_ref.shape[0]
-    half = rows // 2
-    low_ref[:half, :] = total[:half].astype(BF)
-    low_ref[half:, :] = (total[half:rows] + got2[...].astype(F32)).astype(BF)
-    high_ref[:half, :] = (total[rows : rows + half] + got1[...].astype(F32)).astype(BF)
-    high_ref[half:, :] = total[rows + half :].astype(BF)
-
-
-def dispatch_kernel(t_ref, own_ref, b1_ref, b2_ref, g_ref, d_ref, h_ref, o_ref, normed, extra):
-    b = pl.program_id(0)
-    part = o_ref.shape[1]
+def add_kernel(a_ref, a_got, b_ref, b_got, a_out, b_out):
+    a_out[...] = (a_ref[...] + a_got[...].astype(F32)).astype(BF)
+    b_out[...] = (b_ref[...] + b_got[...].astype(F32)).astype(BF)
+
+
+def dispatch_kernel(
+    t_ref, own_ref, a1, a2, b1, b2, g_ref, d_ref, h_ref, o_ref, normed, extra
+):
+    step = pl.program_id(0)
+    part = normed.shape[2]
+    group = o_ref.shape[1] // part
     wide = o_ref.shape[0]
     blocks = wide // SUB
 
-    @pl.when(b == 0)
+    @pl.when(step == 0)
     def _():
-        attn_out = own_ref[...] + b1_ref[...].astype(F32) + b2_ref[...].astype(F32)
-        hidden = (t_ref[...].astype(F32) + attn_out).astype(BF)
-        h_ref[...] = hidden
-        rows = rms(hidden.astype(F32), g_ref[...]).astype(BF)
-        for i in range(SUB):
-            normed[i] = rows[:, i * part : (i + 1) * part]
-
-    @pl.when(b < SUB)
-    def _():
-        x = normed[b]
-        o_ref[...] = dot(d_ref[:wide, :], x).astype(BF)
-        more = dot(d_ref[wide:, :], x)
-        for i in range(part // 128):
-            extra[i, pl.ds(b, blocks, stride=SUB), :] = more[:, i * 128 : (i + 1) * 128]
-
-    @pl.when(b == SUB)
-    def _():
-        for i in range(part // 128):
-            o_ref[:, i * 128 : (i + 1) * 128] = extra[i].astype(BF)
-
-
-def dispatch(tokens, own, b1, b2, gain, table):
+        half = a1.shape[0]
+        for at, x, y in ((0, a1, a2), (half, b1, b2)):
+            here = slice(at, at + half)
+            attn_out = own_ref[here, :] + x[...].astype(F32) + y[...].astype(F32)
+            hidden = (t_ref[here, :].astype(F32) + attn_out).astype(BF)
+            h_ref[here, :] = hidden
+            rows = rms(hidden.astype(F32), g_ref[...]).astype(BF)
+            for i in range(SUB):
+                normed[i, here, :] = rows[:, i * part : (i + 1) * part]
+
+    for i in range(group):
+        b = step * group + i
+
+        def columns(b=b, i=i):
+            x = normed[b]
+            o_ref[:, i * part : (i + 1) * part] = dot(d_ref[:wide, :], x).astype(BF)
+            more = dot(d_ref[wide:, :], x)
+            for n in range(part // 128):
+                extra[n, pl.ds(b, blocks, stride=SUB), :] = more[:, n * 128 : (n + 1) * 128]
+
+        if i < group - 1:
+            columns()
+            continue
+        pl.when(b < SUB)(columns)
+
+        @pl.when(b == SUB)
+        def _():
+            for n in range(part // 128):
+                o_ref[:, i * part + n * 128 : i * part + (n + 1) * 128] = extra[n].astype(BF)
+
+
+def dispatch(tokens, *rest):
+    args = (tokens, *rest)
+    table = rest[-1]
     rows, width = tokens.shape
     part = width // SUB
-    blocks = table.shape[0] // (SUB + 1)
-    wide = blocks * SUB
+    group = 3
+    wide = table.shape[0] // (SUB + 1) * SUB
     whole = lambda a: pl.BlockSpec(a.shape, lambda b: (0, 0))
-    args = (tokens, own, b1, b2, gain, table)
     return pl.pallas_call(
         dispatch_kernel,
-        grid=(SUB + 1,),
+        grid=((SUB + 1) // group,),
         out_shape=(pltpu.HBM((rows, width), BF), pltpu.HBM((wide, width + part), BF)),
         in_specs=[whole(a) for a in args],
-        out_specs=(whole(tokens), pl.BlockSpec((wide, part), lambda b: (0, b))),
+        out_specs=(whole(tokens), pl.BlockSpec((wide, group * part), lambda b: (0, b))),
         scratch_shapes=[
             pltpu.VMEM((SUB, rows, part), BF), pltpu.VMEM((part // 128, wide, 128), F32),
         ],
-        compiler_params=limit(20),
+        compiler_params=limit(24),
         name="dispatch",
     )(*args)
 
 
 def ffn_kernel(x_ref, *refs):
-    sources, (o_ref, wg, wu, wd, rows_ref, extra, sem) = refs[:6], refs[6:]
+    sources, (o_ref, wgu, wd, rows_ref, act, extra, sem) = refs[:6], refs[6:]
     j = pl.program_id(0)
     width = rows_ref.shape[1]
     part = width // SUB
     wide = x_ref.shape[0]
     blocks = wide // SUB
-    copies = [
-        pltpu.make_async_copy(source, target.at[h], sem.at[h, i])
-        for h in range(2)
-        for i, (source, target) in enumerate(zip(sources[3 * h : 3 * h + 3], (wg, wu, wd)))
-    ]
+    hidden = act.shape[1] // 2
+    copies = []
+    for h in range(2):
+        targets = (
+            wgu.at[h, :, :hidden], wgu.at[h, :, hidden:], wd.at[h * hidden : (h + 1) * hidden]
+        )
+        for i, target in enumerate(targets):
+            copies.append(pltpu.make_async_copy(sources[3 * h + i], target, sem.at[h, i]))
 
     @pl.when(j == 0)
     def _():
-        for copy in copies:
-            copy.start()
+        for i in (0, 1, 3, 4, 2, 5):
+            copies[i].start()
 
     rows_ref[:wide, :] = x_ref[:, :width]
     for i in range(part // 128):
@@ -283,7 +306,6 @@
         for i in range(part // 128):
             col = b * part + i * 128
             rows_ref[wide:, col : col + 128] = extra[i, pl.ds(b, blocks, stride=SUB), :].astype(BF)
-    total = None
     for h in range(2):
 
         @pl.when(j == 0)
@@ -291,16 +313,17 @@
             copies[3 * h].wait()
             copies[3 * h + 1].wait()
 
-        gate = dot(rows_ref[...], wg[h])
-        upper = dot(rows_ref[...], wu[h])
-        act = (gate / (1.0 + jnp.exp(-gate)) * upper).astype(BF)
-
-        @pl.when(j == 0)
-        def _():
-            copies[3 * h + 2].wait()
-
-        out = dot(act, wd[h])
-        total = out if total is None else total + out
+        both = dot(rows_ref[...], wgu[h])
+        gate = both[:, :hidden]
+        silu = 0.5 * gate * (1.0 + jnp.tanh(0.5 * gate))
+        act[:, h * hidden : (h + 1) * hidden] = (silu * both[:, hidden:]).astype(BF)
+
+    @pl.when(j == 0)
+    def _():
+        copies[2].wait()
+        copies[5].wait()
+
+    total = dot(act[...], wd[...])
     o_ref[:, :width] = total[:wide].astype(BF)
     for b in range(SUB):
         for i in range(part // 128):
@@ -323,10 +346,10 @@
         in_specs=[block] + [pl.BlockSpec(memory_space=pltpu.HBM)] * 6,
         out_specs=block,
         scratch_shapes=[
-            pltpu.VMEM((2, width, hidden), BF),
-            pltpu.VMEM((2, width, hidden), BF),
-            pltpu.VMEM((2, hidden, width), BF),
+            pltpu.VMEM((2, width, 2 * hidden), BF),
+            pltpu.VMEM((2 * hidden, width), BF),
             pltpu.VMEM((rows, width), BF),
+            pltpu.VMEM((rows, 2 * hidden), BF),
             pltpu.VMEM((width // SUB // 128, step, 128), F32),
             pltpu.SemaphoreType.DMA((2, 3)),
         ],
@@ -342,12 +365,16 @@
 
     @pl.when(b == 0)
     def _():
-        for i in range(part // 128):
+        for i in range(x_ref.shape[1] // 128):
             extra[i] = x_ref[:, i * 128 : (i + 1) * 128].astype(F32)
 
-    more = jnp.concatenate(
-        [extra[i, pl.ds(b, blocks, stride=SUB), :] for i in range(part // 128)], axis=1
-    ).astype(BF)
+    each = x_ref.shape[1]
+    more = [
+        extra[i, pl.ds(b * (part // each) + n, blocks, stride=SUB), :]
+        for n in range(part // each)
+        for i in range(each // 128)
+    ]
+    more = jnp.concatenate(more, axis=1).astype(BF)
     both = dot(wm_ref[...], r_ref[...]) + dot(wx_ref[...], more)
     out = h_ref[...].astype(F32) + both[:rows] + both[rows:]
     row = lax.broadcasted_iota(jnp.int32, out.shape, 0)
@@ -356,20 +383,20 @@
 
 def combine(live, back, wm, wx, hidden):
     rows, width = hidden.shape
-    part = width // SUB
+    part = 2 * width // SUB
     wide = back.shape[0]
     whole = lambda a: pl.BlockSpec(a.shape, lambda b: (0, 0))
     cols = lambda n: pl.BlockSpec((n, part), lambda b: (0, b))
     return pl.pallas_call(
         combine_kernel,
-        grid=(SUB,),
+        grid=(SUB // 2,),
         out_shape=shape((rows, width), BF),
         in_specs=[
             pl.BlockSpec(memory_space=pltpu.SMEM), cols(wide),
-            pl.BlockSpec((wide, part), lambda b: (0, SUB)), whole(wm), whole(wx), cols(rows),
+            pl.BlockSpec((wide, part // 2), lambda b: (0, SUB)), whole(wm), whole(wx), cols(rows),
         ],
         out_specs=cols(rows),
-        scratch_shapes=[pltpu.VMEM((part // 128, wide, 128), F32)],
+        scratch_shapes=[pltpu.VMEM((part // 256, wide, 128), F32)],
         compiler_params=limit(20),
         name="combine",
     )(live, back, back, wm, wx, hidden)
@@ -477,7 +504,7 @@
         out_specs=(vmem(),) * 3,
         scratch_shapes=[
             pltpu.VMEM((slots, width), BF),
-            pltpu.VMEM((6, width, local), BF),
+            pltpu.VMEM((3, width, 2 * local), BF),
             pltpu.SemaphoreType.DMA((len(pieces),)),
             pltpu.SemaphoreType.DMA((6,)),
         ],
@@ -497,17 +524,22 @@
     )(*cache, w_out, out_b)
     got1 = to_up(sum1)
     got2 = to_down(sum2)
-    around = call(
+    part = shape((half, width), BF)
+    wide_part = shape((half, width), F32)
+    low_free, low_need, high_need, high_free = call(
         functools.partial(attn_near_kernel, scale, rows),
-        shape((2 * rows, 2 * local), BF),
-        6,
+        [part, wide_part, wide_part, part],
+        8,
+        scratch_shapes=[pltpu.VMEM((2 * rows, 2 * local), BF)],
         name="attn_near",
-    )(*cache)
-    to_low, to_high = call(
-        proj_near_kernel, [shape((rows, width), BF)] * 2, 5, name="proj_near"
-    )(around, w_out, out_b, got1, got2)
-    b1 = to_up(to_high)
-    b2 = to_down(to_low)
+    )(*cache, w_out, out_b)
+    low_free = to_down(low_free)
+    high_free = to_up(high_free)
+    low_need, high_need = call(add_kernel, [part] * 2, 4, name="add")(
+        low_need, got2, high_need, got1
+    )
+    low_need = to_down(low_need)
+    high_need = to_up(high_need)
     own = call(
         functools.partial(attn_own_kernel, scale, 0),
         shape((rows, width), F32),
@@ -517,7 +549,9 @@
     )(*cache, w_out, out_b)
     own, other_w = lax.optimization_barrier((own, other_w))
 
-    hidden, send = dispatch(tokens, own, b1, b2, moe_gain[None], table)
+    hidden, send = dispatch(
+        tokens, own, high_need, low_free, high_free, low_need, moe_gain[None], table
+    )
 
     def exchange(v):
         return lax.all_to_all(
@@ -535,6 +569,7 @@
     )
     req, exp = ("x", "y"), ("z", "c")
     every = req + exp
+
     return jax.shard_map(
         layer,
         mesh=grid,

time: 271 us -> 266 us (0.982)
  Pallas kernels: 67.5 us -> 58.7 us
    pallas_call x1, Pallas kernels: 17 us -> 11.5 us  [layer(): pl.pallas_call(lambda *refs: qkv_kernel(len(pieces), *refs), out_shape=(p...]
    all_to_all x1, waiting for transfers between devices: 9.53 us -> 13.8 us  [layer(): lax.all_to_all(outgoing, ('x', 'y'), split_axis=0, concat_axis=0, tiled=T...]
    ppermute x5 -> x6, waiting for transfers between devices: 4.67 us -> 8.59 us  [layer(): to_down = lambda v: lax.ppermute(v, 'z', down)]
    ppermute x15, waiting for transfers between devices: 3.23 us -> 0.04 us  [layer(): swap = lambda v: lax.ppermute(v, 'c', [(0, 1), (1, 0)])]
    pallas_call x4, Pallas kernels: 16.3 us -> 13.1 us  [the longest x1 5.33 us: layer(): call(functools.partial(attn_near_kernel, scale, rows), [part, wide_part,...]
    ppermute x5 -> x6, waiting for transfers between devices: 21.2 us -> 18.8 us  [layer(): to_up = lambda v: lax.ppermute(v, 'z', up)]
    ppermute x5 -> x6, starting transfers between devices: 14.2 us -> 16.1 us  [layer(): to_down = lambda v: lax.ppermute(v, 'z', down)]
  transfers between devices with their start and end apart: 26 -> 28, of which waited for: 11 -> 10; matrix products, arithmetic and copies ran while one was open for 2% -> 2% of each run, Pallas kernels for 12% -> 11%
where the time goes in v2:
time: 266 us; the launch traced here: 262 us
  blocking collectives  127 us (48%)
  Pallas kernels  58.7 us (22%)
  waiting for transfers between devices  41.3 us (16%)
  starting transfers between devices  26.2 us (10%)
  local copies, waits for them, and re-layouts  4.26 us (2%)
  other arithmetic  4.02 us (2%)
    all_to_all x2, blocking collectives, exchange(): lax.all_to_all(v.reshape(experts, 2 * SUB, v.shape[1]), ('x', 'y', 'z'),...  127 us
    pallas_call x1, Pallas kernels, ffn(): pl.pallas_call(ffn_kernel, grid=(wide // step,), out_shape=shape((wide, p...  21.1 us
    ppermute x6, waiting for transfers between devices, layer(): to_up = lambda v: lax.ppermute(v, 'z', up)  18.8 us
    ppermute x6, starting transfers between devices, layer(): to_down = lambda v: lax.ppermute(v, 'z', down)  16.1 us
    all_to_all x1, waiting for transfers between devices, layer(): lax.all_to_all(outgoing, ('x', 'y'), split_axis=0, concat_axis=0, tiled=T...  13.8 us
    pallas_call x1, Pallas kernels, layer(): pl.pallas_call(lambda *refs: qkv_kernel(len(pieces), *refs), out_shape=(p...  11.5 us
    ppermute x6, waiting for transfers between devices, layer(): to_down = lambda v: lax.ppermute(v, 'z', down)  8.59 us
    all_to_all x1, starting transfers between devices, layer(): lax.all_to_all(outgoing, ('x', 'y'), split_axis=0, concat_axis=0, tiled=T...  7.17 us
  transfers between devices with their start and end apart: 28, of which 10 were waited for; matrix products, arithmetic and copies ran while one was open for 2% of the time, Pallas kernels for 11%

profile of v2, /device:TPU:24, one launch (start us, length us, event | category | flops | bytes accessed | tf_op | source)
XLA Modules:
  0.0 262.5 jit_solution(770336110598816597)
XLA Ops:
  0.0 2.2 norm.1
  2.2 4.0 %collective-permute-start.2 = (bf16[64,2048]{1,0:T(8,128)(2,1)}, bf16[64,2048]{1,0:T(8,128)(2,1)S(1)}, u32[]{:S(2)}, u32[]{:S(2)}) collective-permute-start(bf16[64,2048]{1,0:T(8,128)(2,1)} %get-tuple-element.38), channel_id=1, source_target_pairs={{0,6},{2,0},{4,2},{6,4},{1,7},{3,1},{5,3},{7,5},{8,14},{10,8},{12,... | collective-permute-start | bytes 786440 | tf_op jit(solution)/shard_map/ppermute | solution.py:421
  6.2 3.2 %collective-permute-start.3 = (bf16[64,2048]{1,0:T(8,128)(2,1)}, bf16[64,2048]{1,0:T(8,128)(2,1)S(1)}, u32[]{:S(2)}, u32[]{:S(2)}) collective-permute-start(bf16[64,2048]{1,0:T(8,128)(2,1)} %get-tuple-element.39), channel_id=1, source_target_pairs={{0,6},{2,0},{4,2},{6,4},{1,7},{3,1},{5,3},{7,5},{8,14},{10,8},{12,... | collective-permute-start | bytes 786440 | tf_op jit(solution)/shard_map/ppermute | solution.py:421
  9.5 3.8 %collective-permute-done.2.refs_3_ = bf16[64,2048]{1,0:T(8,128)(2,1)S(1)} collective-permute-done((bf16[64,2048]{1,0:T(8,128)(2,1)}, bf16[64,2048]{1,0:T(8,128)(2,1)S(1)}, u32[]{:S(2)}, u32[]{:S(2)}) %collective-permute-start.2) | collective-permute-done | bytes 262176 | tf_op jit(solution)/shard_map/ppermute | solution.py:421
  13.2 3.6 %collective-permute-done.refs_1_ = bf16[64,2048]{1,0:T(8,128)(2,1)S(1)} collective-permute-done((bf16[64,2048]{1,0:T(8,128)(2,1)}, bf16[64,2048]{1,0:T(8,128)(2,1)S(1)}, u32[]{:S(2)}, u32[]{:S(2)}) %collective-permute-start) | collective-permute-done | bytes 262176 | tf_op jit(solution)/shard_map/ppermute | solution.py:420
  16.8 0.9 collective-permute-done.3.refs_4_
  17.7 3.3 %collective-permute-done.1.refs_2_ = bf16[64,2048]{1,0:T(8,128)(2,1)S(1)} collective-permute-done((bf16[64,2048]{1,0:T(8,128)(2,1)}, bf16[64,2048]{1,0:T(8,128)(2,1)S(1)}, u32[]{:S(2)}, u32[]{:S(2)}) %collective-permute-start.1) | collective-permute-done | bytes 262176 | tf_op jit(solution)/shard_map/ppermute | solution.py:420
  21.9 4.9 %collective-permute-done.4.refs_5_ = bf16[64,2048]{1,0:T(8,128)(2,1)} collective-permute-done((bf16[64,2048]{1,0:T(8,128)(2,1)S(1)}, bf16[64,2048]{1,0:T(8,128)(2,1)}, u32[]{:S(2)}, u32[]{:S(2)}) %collective-permute-start.4) | collective-permute-done | bytes 262176 | tf_op jit(solution)/shard_map/ppermute | solution.py:420
  27.4 2.6 collective-permute-done.5.refs_6_
  31.5 1.1 copy.20
  33.4 1.6 prefix.1
  35.0 7.2 %all-to-all-start = ((bf16[16,64,512]{2,1,0:T(8,128)(2,1)}), bf16[16,64,512]{2,1,0:T(8,128)(2,1)S(1)}, u32[]{:S(2)}, u32[]{:S(2)}) async-start(bf16[16,64,512]{2,1,0:T(8,128)(2,1)} %bitcast.49), calls=%async_computation | async-start | bytes 2097152 | tf_op jit(solution)/shard_map/all_to_all | solution.py:453
  42.9 0.9 copy-done.12
  43.8 13.8 %all-to-all-done = bf16[16,64,512]{2,1,0:T(8,128)(2,1)S(1)} async-done(((bf16[16,64,512]{2,1,0:T(8,128)(2,1)}), bf16[16,64,512]{2,1,0:T(8,128)(2,1)S(1)}, u32[]{:S(2)}, u32[]{:S(2)}) %all-to-all-start) | async-done | bytes 1048608 | tf_op jit(solution)/shard_map/all_to_all | solution.py:453
  59.3 1.9 fusion
  61.2 1.3 pad_maximum_fusion
  63.3 1.6 route.1
  65.0 11.5 %qkv.1 = (bf16[512,512]{1,0:T(8,128)(2,1)S(1)}, bf16[1024,512]{1,0:T(8,128)(2,1)S(1)}, bf16[1024,512]{1,0:T(8,128)(2,1)S(1)}) custom-call(bf16[128,2048]{1,0:T(8,128)(2,1)} %get-tuple-element.37.refs_0_, bf16[64,2048]{1,0:T(8,128)(2,1)} %copy-done.15, bf16[64,2048]{1,0:T(8,128)(2,1)} %copy-done.17, bf16[64,2048]{1,0:T(8,128)(2,1)} %copy-done.14, ...), custom_call_target="tpu_custom_call" | custom-call | tf_op jit(solution)/shard_map/qkv/pallas_call | solution.py:496
  76.5 3.8 %attn_far.1 = (bf16[64,2048]{1,0:T(8,128)(2,1)S(1)}, bf16[64,2048]{1,0:T(8,128)(2,1)S(1)}) custom-call(bf16[512,512]{1,0:T(8,128)(2,1)S(1)} %get-tuple-element.46.q, bf16[1024,512]{1,0:T(8,128)(2,1)S(1)} %get-tuple-element.47.k, bf16[1024,512]{1,0:T(8,128)(2,1)S(1)} %get-tuple-element.48.v, bf16[1024,512]{1,0:T(8,128)(2,1)S(1)} %bitcast.31, ...), custom_call_target="tpu_custom_call" | custom-call | tf_op jit(solution)/shard_map/attn_far/pallas_call | solution.py:518
  80.3 2.0 collective-permute-start.21
  82.4 5.3 %attn_near.1 = (bf16[64,2048]{1,0:T(8,128)(2,1)S(1)}, f32[64,2048]{1,0:T(8,128)S(1)}, f32[64,2048]{1,0:T(8,128)S(1)}, bf16[64,2048]{1,0:T(8,128)(2,1)S(1)}) custom-call(bf16[512,512]{1,0:T(8,128)(2,1)S(1)} %get-tuple-element.46.q, bf16[1024,512]{1,0:T(8,128)(2,1)S(1)} %get-tuple-element.47.k, bf16[1024,512]{1,0:T(8,128)(2,1)S(1)} %get-tuple-element.48.v, ...), custom_call_target="tpu_custom_call" | custom-call | tf_op jit(solution)/shard_map/attn_near/pallas_call | solution.py:529
  87.7 1.3 collective-permute-done.21.a_got
  89.1 3.1 %collective-permute-start.24 = (bf16[64,2048]{1,0:T(8,128)(2,1)S(1)}, bf16[64,2048]{1,0:T(8,128)(2,1)S(1)}, u32[]{:S(2)}, u32[]{:S(2)}) collective-permute-start(bf16[64,2048]{1,0:T(8,128)(2,1)S(1)} %get-tuple-element.56), channel_id=1, source_target_pairs={{0,6},{2,0},{4,2},{6,4},{1,7},{3,1},{5,3},{7,5},{8,14},{10,8},{12,... | collective-permute-start | bytes 786440 | tf_op jit(solution)/shard_map/ppermute | solution.py:421
  92.4 3.3 %collective-permute-start.26 = (bf16[64,2048]{1,0:T(8,128)(2,1)S(1)}, bf16[64,2048]{1,0:T(8,128)(2,1)S(1)}, u32[]{:S(2)}, u32[]{:S(2)}) collective-permute-start(bf16[64,2048]{1,0:T(8,128)(2,1)S(1)} %get-tuple-element.58), channel_id=1, source_target_pairs={{0,6},{2,0},{4,2},{6,4},{1,7},{3,1},{5,3},{7,5},{8,14},{10,8},{12,... | collective-permute-start | bytes 786440 | tf_op jit(solution)/shard_map/ppermute | solution.py:421
  95.7 3.8 %attn_own.1.own_ref = f32[128,2048]{1,0:T(8,128)S(1)} custom-call(bf16[512,512]{1,0:T(8,128)(2,1)S(1)} %get-tuple-element.46.q, bf16[1024,512]{1,0:T(8,128)(2,1)S(1)} %get-tuple-element.47.k, bf16[1024,512]{1,0:T(8,128)(2,1)S(1)} %get-tuple-element.48.v, bf16[1024,512]{1,0:T(8,128)(2,1)S(1)} %bitcast.33, bf16[1024,512]{1,0:T(8,128)(2,1)} %collective-permute-done.16.pb, ...), custom_call_target="tpu_custom_call" | custom-call | tf_op jit(solution)/shard_map/attn_own/pallas_call | solution.py:543
  99.6 3.0 %collective-permute-done.25.b1 = bf16[64,2048]{1,0:T(8,128)(2,1)S(1)} collective-permute-done((bf16[64,2048]{1,0:T(8,128)(2,1)S(1)}, bf16[64,2048]{1,0:T(8,128)(2,1)S(1)}, u32[]{:S(2)}, u32[]{:S(2)}) %collective-permute-start.25) | collective-permute-done | bytes 262176 | tf_op jit(solution)/shard_map/ppermute | solution.py:420
  102.6 4.0 %collective-permute-done.23.a1 = bf16[64,2048]{1,0:T(8,128)(2,1)S(1)} collective-permute-done((bf16[64,2048]{1,0:T(8,128)(2,1)S(1)}, bf16[64,2048]{1,0:T(8,128)(2,1)S(1)}, u32[]{:S(2)}, u32[]{:S(2)}) %collective-permute-start.23) | collective-permute-done | bytes 262176 | tf_op jit(solution)/shard_map/ppermute | solution.py:420
  106.6 4.3 %dispatch.1 = (bf16[128,2048]{1,0:T(8,128)(2,1)}, bf16[1024,2304]{1,0:T(8,128)(2,1)}) custom-call(bf16[128,2048]{1,0:T(8,128)(2,1)S(1)} %copy-done.1, f32[128,2048]{1,0:T(8,128)S(1)} %attn_own.1.own_ref, bf16[64,2048]{1,0:T(8,128)(2,1)S(1)} %collective-permute-done.23.a1, bf16[64,2048]{1,0:T(8,128)(2,1)S(1)} %collective-permute-done.24.a2, ...), custom_call_target="tpu_custom_call" | custom-call | tf_op jit(solution)/shard_map/dispatch/pallas_call | solution.py:267
  111.0 63.3 %all_to_all.21 = bf16[64,16,2304]{2,1,0:T(8,128)(2,1)} all-to-all(bf16[64,16,2304]{2,1,0:T(8,128)(2,1)} %bitcast.48), channel_id=1, replica_groups=mesh['x'=4,'y'=4,'z'=4,'c'=2] {'x','y','z'}, dimensions={0} | all-to-all | bytes 9437184 | tf_op jit(solution)/shard_map/all_to_all | solution.py:557
  174.3 21.1 %ffn.1 = bf16[1024,2304]{1,0:T(8,128)(2,1)} custom-call(bf16[1024,2304]{1,0:T(8,128)(2,1)} %bitcast.46, bf16[2048,512]{1,0:T(8,128)(2,1)S(1)} %bitcast.36, bf16[2048,512]{1,0:T(8,128)(2,1)S(1)} %bitcast.38, bf16[512,2048]{1,0:T(8,128)(2,1)S(1)} %bitcast.40, bf16[2048,512]{1,0:T(8,128)(2,1)} %collective-permute-done.18.refs_3_, ...), custom_call_target="tpu_custom_call" | custom-call | tf_op jit(solution)/shard_map/ffn/pallas_call | solution.py:342
  195.5 63.6 %all_to_all.22 = bf16[64,16,2304]{2,1,0:T(8,128)(2,1)S(1)} all-to-all(bf16[64,16,2304]{2,1,0:T(8,128)(2,1)} %bitcast.47), channel_id=1, replica_groups=mesh['x'=4,'y'=4,'z'=4,'c'=2] {'x','y','z'}, dimensions={0} | all-to-all | bytes 9437184 | tf_op jit(solution)/shard_map/all_to_all | solution.py:557
  259.1 3.4 %combine.1 = bf16[128,2048]{1,0:T(8,128)(2,1)} custom-call(s32[1]{0:T(128)} %bitcast.11.live_ref, bf16[1024,2304]{1,0:T(8,128)(2,1)S(1)} %bitcast.28, bf16[1024,2304]{1,0:T(8,128)(2,1)S(1)} %bitcast.29, bf16[256,1024]{1,0:T(8,128)(2,1)S(1)} %copy-done.5, bf16[256,128]{1,0:T(8,128)(2,1)S(1)} %copy-done.8, bf16[128,2048]{1,0:T(8,128)(2,1)S(1)} %copy-done.6), custom_call_target="tpu_custom_call" | custom-call | tf_op jit(solution)/shard_map/combine/pallas_call | solution.py:390
  (95 shorter events, 6.6 us)
Async XLA Ops:
  2.2 11.0 %collective-permute-start.2 = (bf16[64,2048]{1,0:T(8,128)(2,1)}, bf16[64,2048]{1,0:T(8,128)(2,1)S(1)}, u32[]{:S(2)}, u32[]{:S(2)}) collective-permute-start(bf16[64,2048]{1,0:T(8,128)(2,1)} %get-tuple-element.38), channel_id=1, source_target_pairs={{0,6},{2,0},{4,2},{6,4},{1,7},{3,1},{5,3},{7,5},{8,14},{10,8},{12,... | collective-permute-start | bytes 786440 | tf_op jit(solution)/shard_map/ppermute | solution.py:421
  6.2 10.6 %collective-permute-start = (bf16[64,2048]{1,0:T(8,128)(2,1)}, bf16[64,2048]{1,0:T(8,128)(2,1)S(1)}, u32[]{:S(2)}, u32[]{:S(2)}) collective-permute-start(bf16[64,2048]{1,0:T(8,128)(2,1)} %get-tuple-element.38), channel_id=1, source_target_pairs={{0,2},{2,4},{4,6},{6,0},{1,3},{3,5},{5,7},{7,1},{8,10},{10,12},{12... | collective-permute-start | bytes 786440 | tf_op jit(solution)/shard_map/ppermute | solution.py:420
  6.2 11.5 %collective-permute-start.3 = (bf16[64,2048]{1,0:T(8,128)(2,1)}, bf16[64,2048]{1,0:T(8,128)(2,1)S(1)}, u32[]{:S(2)}, u32[]{:S(2)}) collective-permute-start(bf16[64,2048]{1,0:T(8,128)(2,1)} %get-tuple-element.39), channel_id=1, source_target_pairs={{0,6},{2,0},{4,2},{6,4},{1,7},{3,1},{5,3},{7,5},{8,14},{10,8},{12,... | collective-permute-start | bytes 786440 | tf_op jit(solution)/shard_map/ppermute | solution.py:421
  9.5 11.6 %collective-permute-start.1 = (bf16[64,2048]{1,0:T(8,128)(2,1)}, bf16[64,2048]{1,0:T(8,128)(2,1)S(1)}, u32[]{:S(2)}, u32[]{:S(2)}) collective-permute-start(bf16[64,2048]{1,0:T(8,128)(2,1)} %get-tuple-element.39), channel_id=1, source_target_pairs={{0,2},{2,4},{4,6},{6,0},{1,3},{3,5},{5,7},{7,1},{8,10},{10,12},{12... | collective-permute-start | bytes 786440 | tf_op jit(solution)/shard_map/ppermute | solution.py:420
  13.2 7.8 %collective-permute-start.9 = (bf16[64,2048]{1,0:T(8,128)(2,1)S(1)}, bf16[64,2048]{1,0:T(8,128)(2,1)S(1)}, u32[]{:S(2)}, u32[]{:S(2)}) collective-permute-start(bf16[64,2048]{1,0:T(8,128)(2,1)S(1)} %collective-permute-done.2.refs_3_), channel_id=1, source_target_pairs={{0,1},{1,0},{2,3},{3,2},{4,5},{5,4},{6,7},{7,6},{8,9},{9,8},{10,11... | collective-permute-start | bytes 786440 | tf_op jit(solution)/shard_map/ppermute | solution.py:419
  16.8 4.7 %collective-permute-start.7 = (bf16[64,2048]{1,0:T(8,128)(2,1)S(1)}, bf16[64,2048]{1,0:T(8,128)(2,1)S(1)}, u32[]{:S(2)}, u32[]{:S(2)}) collective-permute-start(bf16[64,2048]{1,0:T(8,128)(2,1)S(1)} %collective-permute-done.refs_1_), channel_id=1, source_target_pairs={{0,1},{1,0},{2,3},{3,2},{4,5},{5,4},{6,7},{7,6},{8,9},{9,8},{10,11... | collective-permute-start | bytes 786440 | tf_op jit(solution)/shard_map/ppermute | solution.py:419
  16.8 10.0 %collective-permute-start.4 = (bf16[64,2048]{1,0:T(8,128)(2,1)S(1)}, bf16[64,2048]{1,0:T(8,128)(2,1)}, u32[]{:S(2)}, u32[]{:S(2)}) collective-permute-start(bf16[64,2048]{1,0:T(8,128)(2,1)S(1)} %collective-permute-done.refs_1_), channel_id=1, source_target_pairs={{0,2},{2,4},{4,6},{6,0},{1,3},{3,5},{5,7},{7,1},{8,10},{10,12},{12... | collective-permute-start | bytes 786440 | tf_op jit(solution)/shard_map/ppermute | solution.py:420
  17.7 25.0 %collective-permute-start.14 = (bf16[2048,256]{1,0:T(8,128)(2,1)}, bf16[2048,256]{1,0:T(8,128)(2,1)S(1)}, u32[]{:S(2)}, u32[]{:S(2)}) collective-permute-start(bf16[2048,256]{1,0:T(8,128)(2,1)} %refs_16_.1), channel_id=1, source_target_pairs={{0,1},{1,0},{2,3},{3,2},{4,5},{5,4},{6,7},{7,6},{8,9},{9,8},{10,11... | collective-permute-start | bytes 3145736 | tf_op jit(solution)/shard_map/ppermute | solution.py:419
  21.0 9.5 %collective-permute-start.6 = (bf16[128,2048]{1,0:T(8,128)(2,1)}, bf16[128,2048]{1,0:T(8,128)(2,1)S(1)}, u32[]{:S(2)}, u32[]{:S(2)}) collective-permute-start(bf16[128,2048]{1,0:T(8,128)(2,1)} %get-tuple-element.37.refs_0_), channel_id=1, source_target_pairs={{0,1},{1,0},{2,3},{3,2},{4,5},{5,4},{6,7},{7,6},{8,9},{9,8},{10,11... | collective-permute-start | bytes 1572872 | tf_op jit(solution)/shard_map/ppermute | solution.py:419
  21.0 5.8 %collective-permute-start.10 = (bf16[64,2048]{1,0:T(8,128)(2,1)S(1)}, bf16[64,2048]{1,0:T(8,128)(2,1)S(1)}, u32[]{:S(2)}, u32[]{:S(2)}) collective-permute-start(bf16[64,2048]{1,0:T(8,128)(2,1)S(1)} %collective-permute-done.3.refs_4_), channel_id=1, source_target_pairs={{0,1},{1,0},{2,3},{3,2},{4,5},{5,4},{6,7},{7,6},{8,9},{9,8},{10,11... | collective-permute-start | bytes 786440 | tf_op jit(solution)/shard_map/ppermute | solution.py:419
  21.5 8.4 %collective-permute-start.5 = (bf16[64,2048]{1,0:T(8,128)(2,1)S(1)}, bf16[64,2048]{1,0:T(8,128)(2,1)}, u32[]{:S(2)}, u32[]{:S(2)}) collective-permute-start(bf16[64,2048]{1,0:T(8,128)(2,1)S(1)} %collective-permute-done.3.refs_4_), channel_id=1, source_target_pairs={{0,6},{2,0},{4,2},{6,4},{1,7},{3,1},{5,3},{7,5},{8,14},{10,8},{12,... | collective-permute-start | bytes 786440 | tf_op jit(solution)/shard_map/ppermute | solution.py:421
  26.9 3.1 %collective-permute-start.8 = (bf16[64,2048]{1,0:T(8,128)(2,1)S(1)}, bf16[64,2048]{1,0:T(8,128)(2,1)S(1)}, u32[]{:S(2)}, u32[]{:S(2)}) collective-permute-start(bf16[64,2048]{1,0:T(8,128)(2,1)S(1)} %collective-permute-done.1.refs_2_), channel_id=1, source_target_pairs={{0,1},{1,0},{2,3},{3,2},{4,5},{5,4},{6,7},{7,6},{8,9},{9,8},{10,11... | collective-permute-start | bytes 786440 | tf_op jit(solution)/shard_map/ppermute | solution.py:419
  26.9 16.9 %collective-permute-start.13 = (bf16[2048,256]{1,0:T(8,128)(2,1)}, bf16[2048,256]{1,0:T(8,128)(2,1)}, u32[]{:S(2)}, u32[]{:S(2)}) collective-permute-start(bf16[2048,256]{1,0:T(8,128)(2,1)} %refs_14_.1), channel_id=1, source_target_pairs={{0,1},{1,0},{2,3},{3,2},{4,5},{5,4},{6,7},{7,6},{8,9},{9,8},{10,11... | collective-permute-start | bytes 3145736 | tf_op jit(solution)/shard_map/ppermute | solution.py:419
  30.0 27.7 %collective-permute-start.15 = (bf16[2048,256]{1,0:T(8,128)(2,1)}, bf16[2048,256]{1,0:T(8,128)(2,1)}, u32[]{:S(2)}, u32[]{:S(2)}) collective-permute-start(bf16[2048,256]{1,0:T(8,128)(2,1)} %refs_18_.1), channel_id=1, source_target_pairs={{0,1},{1,0},{2,3},{3,2},{4,5},{5,4},{6,7},{7,6},{8,9},{9,8},{10,11... | collective-permute-start | bytes 3145736 | tf_op jit(solution)/shard_map/ppermute | solution.py:419
  30.0 12.2 %collective-permute-start.11 = (bf16[64,2048]{1,0:T(8,128)(2,1)}, bf16[64,2048]{1,0:T(8,128)(2,1)}, u32[]{:S(2)}, u32[]{:S(2)}) collective-permute-start(bf16[64,2048]{1,0:T(8,128)(2,1)} %collective-permute-done.4.refs_5_), channel_id=1, source_target_pairs={{0,1},{1,0},{2,3},{3,2},{4,5},{5,4},{6,7},{7,6},{8,9},{9,8},{10,11... | collective-permute-start | bytes 786440 | tf_op jit(solution)/shard_map/ppermute | solution.py:419
  30.7 11.6 %collective-permute-start.12 = (bf16[64,2048]{1,0:T(8,128)(2,1)}, bf16[64,2048]{1,0:T(8,128)(2,1)}, u32[]{:S(2)}, u32[]{:S(2)}) collective-permute-start(bf16[64,2048]{1,0:T(8,128)(2,1)} %collective-permute-done.5.refs_6_), channel_id=1, source_target_pairs={{0,1},{1,0},{2,3},{3,2},{4,5},{5,4},{6,7},{7,6},{8,9},{9,8},{10,11... | collective-permute-start | bytes 786440 | tf_op jit(solution)/shard_map/ppermute | solution.py:419
  35.0 22.7 %all-to-all-start = ((bf16[16,64,512]{2,1,0:T(8,128)(2,1)}), bf16[16,64,512]{2,1,0:T(8,128)(2,1)S(1)}, u32[]{:S(2)}, u32[]{:S(2)}) async-start(bf16[16,64,512]{2,1,0:T(8,128)(2,1)} %bitcast.49), calls=%async_computation | async-start | bytes 2097152 | tf_op jit(solution)/shard_map/all_to_all | solution.py:453
  42.2 50.1 %collective-permute-start.18 = (bf16[2048,512]{1,0:T(8,128)(2,1)}, bf16[2048,512]{1,0:T(8,128)(2,1)}, u32[]{:S(2)}, u32[]{:S(2)}) collective-permute-start(bf16[2048,512]{1,0:T(8,128)(2,1)} %bitcast.35), channel_id=1, source_target_pairs={{0,1},{1,0},{2,3},{3,2},{4,5},{5,4},{6,7},{7,6},{8,9},{9,8},{10,11... | collective-permute-start | bytes 6291464 | tf_op jit(solution)/shard_map/ppermute | solution.py:419
  42.3 50.1 %collective-permute-start.19 = (bf16[2048,512]{1,0:T(8,128)(2,1)}, bf16[2048,512]{1,0:T(8,128)(2,1)}, u32[]{:S(2)}, u32[]{:S(2)}) collective-permute-start(bf16[2048,512]{1,0:T(8,128)(2,1)} %bitcast.37), channel_id=1, source_target_pairs={{0,1},{1,0},{2,3},{3,2},{4,5},{5,4},{6,7},{7,6},{8,9},{9,8},{10,11... | collective-permute-start | bytes 6291464 | tf_op jit(solution)/shard_map/ppermute | solution.py:419
  42.8 56.8 %collective-permute-start.20 = (bf16[512,2048]{1,0:T(8,128)(2,1)}, bf16[512,2048]{1,0:T(8,128)(2,1)}, u32[]{:S(2)}, u32[]{:S(2)}) collective-permute-start(bf16[512,2048]{1,0:T(8,128)(2,1)} %bitcast.39), channel_id=1, source_target_pairs={{0,1},{1,0},{2,3},{3,2},{4,5},{5,4},{6,7},{7,6},{8,9},{9,8},{10,11... | collective-permute-start | bytes 6291464 | tf_op jit(solution)/shard_map/ppermute | solution.py:419
  43.7 32.7 %collective-permute-start.17 = (bf16[256,2048]{1,0:T(8,128)(2,1)S(1)}, bf16[256,2048]{1,0:T(8,128)(2,1)S(1)}, u32[]{:S(2)}, u32[]{:S(2)}) collective-permute-start(bf16[256,2048]{1,0:T(8,128)(2,1)S(1)} %copy-done), channel_id=1, source_target_pairs={{0,1},{1,0},{2,3},{3,2},{4,5},{5,4},{6,7},{7,6},{8,9},{9,8},{10,11... | collective-permute-start | bytes 3145736 | tf_op jit(solution)/shard_map/ppermute | solution.py:419
  57.7 18.8 %collective-permute-start.16 = (bf16[1024,512]{1,0:T(8,128)(2,1)S(1)}, bf16[1024,512]{1,0:T(8,128)(2,1)}, u32[]{:S(2)}, u32[]{:S(2)}) collective-permute-start(bf16[1024,512]{1,0:T(8,128)(2,1)S(1)} %bitcast.30), channel_id=1, source_target_pairs={{0,1},{1,0},{2,3},{3,2},{4,5},{5,4},{6,7},{7,6},{8,9},{9,8},{10,11... | collective-permute-start | bytes 3145736 | tf_op jit(solution)/shard_map/ppermute | solution.py:419
  80.3 8.8 %collective-permute-start.21 = (bf16[64,2048]{1,0:T(8,128)(2,1)S(1)}, bf16[64,2048]{1,0:T(8,128)(2,1)S(1)}, u32[]{:S(2)}, u32[]{:S(2)}) collective-permute-start(bf16[64,2048]{1,0:T(8,128)(2,1)S(1)} %get-tuple-element.52), channel_id=1, source_target_pairs={{0,6},{2,0},{4,2},{6,4},{1,7},{3,1},{5,3},{7,5},{8,14},{10,8},{12,... | collective-permute-start | bytes 786440 | tf_op jit(solution)/shard_map/ppermute | solution.py:421
  82.3 9.9 %collective-permute-start.22 = (bf16[64,2048]{1,0:T(8,128)(2,1)S(1)}, bf16[64,2048]{1,0:T(8,128)(2,1)S(1)}, u32[]{:S(2)}, u32[]{:S(2)}) collective-permute-start(bf16[64,2048]{1,0:T(8,128)(2,1)S(1)} %get-tuple-element.54), channel_id=1, source_target_pairs={{0,2},{2,4},{4,6},{6,0},{1,3},{3,5},{5,7},{7,1},{8,10},{10,12},{12... | collective-permute-start | bytes 786440 | tf_op jit(solution)/shard_map/ppermute | solution.py:420
  89.1 10.5 %collective-permute-start.24 = (bf16[64,2048]{1,0:T(8,128)(2,1)S(1)}, bf16[64,2048]{1,0:T(8,128)(2,1)S(1)}, u32[]{:S(2)}, u32[]{:S(2)}) collective-permute-start(bf16[64,2048]{1,0:T(8,128)(2,1)S(1)} %get-tuple-element.56), channel_id=1, source_target_pairs={{0,6},{2,0},{4,2},{6,4},{1,7},{3,1},{5,3},{7,5},{8,14},{10,8},{12,... | collective-permute-start | bytes 786440 | tf_op jit(solution)/shard_map/ppermute | solution.py:421
  92.2 10.4 %collective-permute-start.25 = (bf16[64,2048]{1,0:T(8,128)(2,1)S(1)}, bf16[64,2048]{1,0:T(8,128)(2,1)S(1)}, u32[]{:S(2)}, u32[]{:S(2)}) collective-permute-start(bf16[64,2048]{1,0:T(8,128)(2,1)S(1)} %get-tuple-element.57), channel_id=1, source_target_pairs={{0,2},{2,4},{4,6},{6,0},{1,3},{3,5},{5,7},{7,1},{8,10},{10,12},{12... | collective-permute-start | bytes 786440 | tf_op jit(solution)/shard_map/ppermute | solution.py:420
  92.3 14.3 %collective-permute-start.23 = (bf16[64,2048]{1,0:T(8,128)(2,1)S(1)}, bf16[64,2048]{1,0:T(8,128)(2,1)S(1)}, u32[]{:S(2)}, u32[]{:S(2)}) collective-permute-start(bf16[64,2048]{1,0:T(8,128)(2,1)S(1)} %get-tuple-element.55), channel_id=1, source_target_pairs={{0,2},{2,4},{4,6},{6,0},{1,3},{3,5},{5,7},{7,1},{8,10},{10,12},{12... | collective-permute-start | bytes 786440 | tf_op jit(solution)/shard_map/ppermute | solution.py:420
  92.4 14.2 %collective-permute-start.26 = (bf16[64,2048]{1,0:T(8,128)(2,1)S(1)}, bf16[64,2048]{1,0:T(8,128)(2,1)S(1)}, u32[]{:S(2)}, u32[]{:S(2)}) collective-permute-start(bf16[64,2048]{1,0:T(8,128)(2,1)S(1)} %get-tuple-element.58), channel_id=1, source_target_pairs={{0,6},{2,0},{4,2},{6,4},{1,7},{3,1},{5,3},{7,5},{8,14},{10,8},{12,... | collective-permute-start | bytes 786440 | tf_op jit(solution)/shard_map/ppermute | solution.py:421
  111.0 63.3 %copy-start.4 = (bf16[1,512,2048]{2,1,0:T(8,128)(2,1)S(1)}, bf16[1,512,2048]{2,1,0:T(8,128)(2,1)}, u32[]{:S(2)}) copy-start(bf16[1,512,2048]{2,1,0:T(8,128)(2,1)} %param.27) | copy-start | bytes 6291460
  195.4 63.7 %copy-start.5 = (bf16[256,1024]{1,0:T(8,128)(2,1)S(1)}, bf16[256,1024]{1,0:T(8,128)(2,1)}, u32[]{:S(2)}) copy-start(bf16[256,1024]{1,0:T(8,128)(2,1)} %get-tuple-element.64.wm_ref) | copy-start | bytes 1572868
  195.4 63.7 %copy-start.6 = (bf16[128,2048]{1,0:T(8,128)(2,1)S(1)}, bf16[128,2048]{1,0:T(8,128)(2,1)}, u32[]{:S(2)}) copy-start(bf16[128,2048]{1,0:T(8,128)(2,1)} %get-tuple-element.66.h_ref) | copy-start | bytes 1572868
  195.5 63.7 %copy-start.8 = (bf16[256,128]{1,0:T(8,128)(2,1)S(1)}, bf16[256,128]{1,0:T(8,128)(2,1)}, u32[]{:S(2)}) copy-start(bf16[256,128]{1,0:T(8,128)(2,1)} %get-tuple-element.65.wx_ref) | copy-start | bytes 196612
  (20 other events, 355.2 us)

commit v3 on v2

--- a/solution.py
+++ b/solution.py
@@ -61,13 +61,20 @@
     last_ref[...] = normed[half:]
 
 
+def facts_kernel(a_ref, b_ref, o_ref):
+    for i in range(a_ref.shape[0]):
+        o_ref[i] = a_ref[i]
+    for i in range(b_ref.shape[0]):
+        o_ref[a_ref.shape[0] + i] = b_ref[i]
+
+
 def slots_of(index):
     block = index // SUB
     return block // 2, (block % 2) * (SUB + 1) + index % SUB
 
 
-def route_kernel(r_ref, rt_ref, w_ref, dt_ref, wm_ref, wx_ref):
-    rows, top = r_ref.shape
+def route_kernel(rt_ref, wt_ref, dt_ref, wm_ref, wx_ref):
+    top, rows = rt_ref.shape
     blocks = wx_ref.shape[1]
     experts = blocks // 2
     wide = blocks * SUB
@@ -77,8 +84,11 @@
     col_i = iota((rows, rows), 1)
     e_t = iota((experts, rows), 0)
     named_t = jnp.zeros((experts, rows), F32)
+    weight_t = jnp.zeros((experts, rows), F32)
     for k in range(top):
-        named_t += one(rt_ref[k : k + 1, :] == e_t)
+        hit = rt_ref[k : k + 1, :] == e_t
+        named_t += one(hit)
+        weight_t += jnp.where(hit, wt_ref[k : k + 1, :], 0.0)
     rank_t = dot(named_t.astype(BF), one(row_i < col_i).astype(BF))
     rank_t = jnp.where(named_t > 0.5, rank_t, -1.0).astype(BF)
     expert, _ = slots_of(iota((wide, experts), 0))
@@ -89,13 +99,8 @@
     spread = one(block // 2 == iota((blocks, experts), 1)).astype(BF)
     slot = (iota((blocks, rows), 0) % 2) * (SUB + 1) + SUB
     dt_ref[wide:, :] = one(dot(spread, rank_t) == slot.astype(F32)).astype(BF)
-    e_n = iota((rows, experts), 1)
-    named = jnp.zeros((rows, experts), F32)
-    weight = jnp.zeros((rows, experts), F32)
-    for k in range(top):
-        hit = r_ref[:, k : k + 1] == e_n
-        named += one(hit)
-        weight += jnp.where(hit, w_ref[:, k : k + 1], 0.0)
+    named = jnp.transpose(named_t)
+    weight = jnp.transpose(weight_t)
     rank = dot(one(col_i < row_i).astype(BF), named.astype(BF))
     rank = jnp.where(named > 0.5, rank, -1.0).astype(BF)
     high = weight.astype(BF)
@@ -143,20 +148,26 @@
         copy.start()
     for load in loads[2:]:
         load.start()
-    for copy in copies:
-        copy.wait()
-    for i, o_ref in enumerate((k_ref, q_ref, v_ref)):
-        loads[2 * i].wait()
-        loads[2 * i + 1].wait()
-        rows = o_ref.shape[0]
-        mixed = dot(x_ref[:rows, :], w_ref[i])
-        if o_ref is v_ref:
-            o_ref[...] = mixed.astype(BF)
-            continue
-        for h in range(2 * local // HD):
-            v = mixed[:, h * HD : (h + 1) * HD]
-            turned = v * cos_ref[:rows, :] + pltpu.roll(v, HD // 2, 1) * sin_ref[:rows, :]
-            o_ref[:, h * HD : (h + 1) * HD] = turned.astype(BF)
+    half = q_ref.shape[0]
+    at, left = 0, list(copies)
+    for rows in (slice(0, half), slice(half, 2 * half)):
+        while at < rows.stop:
+            left.pop(0).wait()
+            at += pieces[len(pieces) - len(left) - 1].shape[0]
+        for i, o_ref in enumerate((k_ref, q_ref, v_ref)):
+            if rows.start == 0:
+                loads[2 * i].wait()
+                loads[2 * i + 1].wait()
+            elif o_ref is q_ref:
+                continue
+            mixed = dot(x_ref[rows, :], w_ref[i])
+            if o_ref is v_ref:
+                o_ref[rows, :] = mixed.astype(BF)
+                continue
+            for h in range(2 * local // HD):
+                v = mixed[:, h * HD : (h + 1) * HD]
+                turned = v * cos_ref[rows, :] + pltpu.roll(v, HD // 2, 1) * sin_ref[rows, :]
+                o_ref[rows, h * HD : (h + 1) * HD] = turned.astype(BF)
 
 
 def attend(scale, q_ref, k_ref, v_ref, pre_refs, bias_ref, o_ref, first):
@@ -278,84 +289,141 @@
     )(*args)
 
 
-def ffn_kernel(x_ref, *refs):
-    sources, (o_ref, wgu, wd, rows_ref, act, extra, sem) = refs[:6], refs[6:]
+def ffn_kernel(group, order_ref, x_hbm, *refs):
+    sources = refs[:6]
+    o_hbm, x_ref, o_ref, wgu, wd, rows_ref, act, extra, w_sem, x_sem, o_sem = refs[6:]
     j = pl.program_id(0)
+    senders, each = x_hbm.shape[:2]
     width = rows_ref.shape[1]
     part = width // SUB
-    wide = x_ref.shape[0]
+    wide = group * each
     blocks = wide // SUB
     hidden = act.shape[1] // 2
+    steps = (order_ref[senders] + group - 1) // group
     copies = []
     for h in range(2):
         targets = (
             wgu.at[h, :, :hidden], wgu.at[h, :, hidden:], wd.at[h * hidden : (h + 1) * hidden]
         )
         for i, target in enumerate(targets):
-            copies.append(pltpu.make_async_copy(sources[3 * h + i], target, sem.at[h, i]))
+            copies.append(pltpu.make_async_copy(sources[3 * h + i], target, w_sem.at[h, i]))
+
+    def moves(step, inward):
+        slot = step % 2
+        out = []
+        for s in range(group):
+            sender = order_ref[step * group + s]
+            here = pl.ds(s * each, each)
+            if inward:
+                ends = x_hbm.at[sender], x_ref.at[slot, here]
+            else:
+                ends = o_ref.at[slot, here], o_hbm.at[sender]
+            out.append(pltpu.make_async_copy(*ends, (x_sem if inward else o_sem).at[slot, s]))
+        return out
+
+    def start(step, inward):
+        for move in moves(step, inward):
+            move.start()
+
+    def wait(step, inward):
+        for move in moves(step, inward):
+            move.wait()
 
     @pl.when(j == 0)
     def _():
-        for i in (0, 1, 3, 4, 2, 5):
+        copies[0].start()
+        copies[1].start()
+        start(0, True)
+        for i in (3, 4, 2, 5):
             copies[i].start()
 
-    rows_ref[:wide, :] = x_ref[:, :width]
-    for i in range(part // 128):
-        extra[i] = x_ref[:, width + i * 128 : width + (i + 1) * 128].astype(F32)
-    for b in range(SUB):
+    @pl.when(j + 1 < steps)
+    def _():
+        start(j + 1, True)
+
+    @pl.when(j < steps)
+    def _():
+        slot = j % 2
+        wait(j, True)
+        rows_ref[:wide, :] = x_ref[slot, :, :width]
         for i in range(part // 128):
-            col = b * part + i * 128
-            rows_ref[wide:, col : col + 128] = extra[i, pl.ds(b, blocks, stride=SUB), :].astype(BF)
-    for h in range(2):
+            extra[i] = x_ref[slot, :, width + i * 128 : width + (i + 1) * 128].astype(F32)
+        for b in range(SUB):
+            for i in range(part // 128):
+                col = b * part + i * 128
+                rows_ref[wide:, col : col + 128] = extra[i, pl.ds(b, blocks, stride=SUB), :].astype(
+                    BF
+                )
+        for h in range(2):
+
+            @pl.when(j == 0)
+            def _():
+                copies[3 * h].wait()
+                copies[3 * h + 1].wait()
+
+            both = dot(rows_ref[...], wgu[h])
+            gate = both[:, :hidden]
+            silu = 0.5 * gate * (1.0 + jnp.tanh(0.5 * gate))
+            act[:, h * hidden : (h + 1) * hidden] = (silu * both[:, hidden:]).astype(BF)
 
         @pl.when(j == 0)
         def _():
-            copies[3 * h].wait()
-            copies[3 * h + 1].wait()
-
-        both = dot(rows_ref[...], wgu[h])
-        gate = both[:, :hidden]
-        silu = 0.5 * gate * (1.0 + jnp.tanh(0.5 * gate))
-        act[:, h * hidden : (h + 1) * hidden] = (silu * both[:, hidden:]).astype(BF)
-
-    @pl.when(j == 0)
+            copies[2].wait()
+            copies[5].wait()
+
+        @pl.when(j >= 2)
+        def _():
+            wait(j - 2, False)
+
+        total = dot(act[...], wd[...])
+        o_ref[slot, :, :width] = total[:wide].astype(BF)
+        for b in range(SUB):
+            for i in range(part // 128):
+                col = b * part + i * 128
+                extra[i, pl.ds(b, blocks, stride=SUB), :] = total[wide:, col : col + 128]
+        for i in range(part // 128):
+            o_ref[slot, :, width + i * 128 : width + (i + 1) * 128] = extra[i].astype(BF)
+        start(j, False)
+
+    @pl.when(j == pl.num_programs(0) - 1)
     def _():
-        copies[2].wait()
-        copies[5].wait()
-
-    total = dot(act[...], wd[...])
-    o_ref[:, :width] = total[:wide].astype(BF)
-    for b in range(SUB):
-        for i in range(part // 128):
-            col = b * part + i * 128
-            extra[i, pl.ds(b, blocks, stride=SUB), :] = total[wide:, col : col + 128]
-    for i in range(part // 128):
-        o_ref[:, width + i * 128 : width + (i + 1) * 128] = extra[i].astype(BF)
-
-
-def ffn(x, w0, w1):
-    wide, packed = x.shape
+        @pl.when(steps >= 2)
+        def _():
+            wait(steps - 2, False)
+
+        @pl.when(steps >= 1)
+        def _():
+            wait(steps - 1, False)
+
+
+def ffn(order, x, w0, w1):
+    senders, each, packed = x.shape
     width, hidden = w0[0].shape
-    step = 256
-    rows = step + step // SUB
-    block = pl.BlockSpec((step, packed), lambda j: (j, 0))
+    group = 16
+    wide = group * each
+    rows = wide + wide // SUB
+    any_space = pl.BlockSpec(memory_space=pl.ANY)
     return pl.pallas_call(
-        ffn_kernel,
-        grid=(wide // step,),
-        out_shape=shape((wide, packed), BF),
-        in_specs=[block] + [pl.BlockSpec(memory_space=pltpu.HBM)] * 6,
-        out_specs=block,
+        functools.partial(ffn_kernel, group),
+        grid=(senders // group,),
+        out_shape=pltpu.HBM(x.shape, BF),
+        in_specs=[pl.BlockSpec(memory_space=pltpu.SMEM)] + [any_space] * 7,
+        out_specs=any_space,
         scratch_shapes=[
+            pltpu.VMEM((2, wide, packed), BF),
+            pltpu.VMEM((2, wide, packed), BF),
             pltpu.VMEM((2, width, 2 * hidden), BF),
             pltpu.VMEM((2 * hidden, width), BF),
             pltpu.VMEM((rows, width), BF),
             pltpu.VMEM((rows, 2 * hidden), BF),
-            pltpu.VMEM((width // SUB // 128, step, 128), F32),
+            pltpu.VMEM((width // SUB // 128, wide, 128), F32),
             pltpu.SemaphoreType.DMA((2, 3)),
+            pltpu.SemaphoreType.DMA((2, group)),
+            pltpu.SemaphoreType.DMA((2, group)),
         ],
         compiler_params=limit(40),
         name="ffn",
-    )(x, *w0, *w1)
+    )(order, *map(away, (x, *w0, *w1)))
 
 
 def combine_kernel(live_ref, r_ref, x_ref, wm_ref, wx_ref, h_ref, o_ref, extra):
@@ -432,9 +500,18 @@
     own_b = swap(normed)
     far0 = to_up(low0)
     far1 = to_down(high1)
+    smem = pl.BlockSpec(memory_space=pltpu.SMEM)
+    facts = pl.pallas_call(
+        facts_kernel,
+        out_shape=shape((reqs + 2,), jnp.int32),
+        in_specs=[smem] * 2,
+        out_specs=smem,
+        compiler_params=limit(2),
+        name="facts",
+    )(lengths, jnp.stack([z, core]))
+    lengths, z, core = facts[:reqs], facts[reqs], facts[reqs + 1]
     near_a = (low0, low1, high0, high1)
     near_b = tuple(swap(v) for v in near_a)
-    far_b = swap(far0), swap(far1)
 
     wk = (w_key, swap(w_key))
     wq = (w_query, swap(w_query))
@@ -473,23 +550,23 @@
     bias = jnp.where(place < length, 0.0, -1e30)[None, :]
 
     live = jnp.clip(length - (z * 2 + core) * rows, 0, rows).astype(jnp.int32)[None]
-    routes, cosine, sine, bias, live = lax.optimization_barrier(
-        (routes, cosine, sine, bias, live)
-    )
-
-    blocks = 2 * experts
-    wide = blocks * SUB
-    table, wm, wx = call(
-        route_kernel,
-        [
-            pltpu.HBM((wide + blocks, rows), BF), pltpu.HBM((2 * rows, wide), BF),
-            pltpu.HBM((2 * rows, blocks), BF),
-        ],
-        3,
-        name="route",
-    )(routes, routes.T, route_weights)
-
-    far_b, table = lax.optimization_barrier((far_b, table))
+    sender = jnp.arange(experts, dtype=jnp.int32)
+    each = jnp.broadcast_to(lengths[:, None], (reqs, zs)).reshape(-1)
+    full = each > (sender % zs * 2 + core) * rows
+    before = sender[None, :] < sender[:, None]
+    count = jnp.sum(full.astype(jnp.int32))
+    rank = jnp.where(
+        full,
+        jnp.sum((before & full[None, :]).astype(jnp.int32), axis=1),
+        count + jnp.sum((before & ~full[None, :]).astype(jnp.int32), axis=1),
+    )
+    order = jnp.sum(jnp.where(rank[None, :] == sender[:, None], sender[None, :], 0), axis=1)
+    order = jnp.concatenate([order, count[None]])
+    far0, far1, cosine, sine, bias, live, order = lax.optimization_barrier(
+        (far0, far1, cosine, sine, bias, live, order)
+    )
+    far_b = swap(far0), swap(far1)
+
 
     slots = 2 * zs * rows
     pieces = (normed, *near_a, far0, far1, own_b, *near_b, *far_b)
@@ -549,16 +626,27 @@
     )(*cache, w_out, out_b)
     own, other_w = lax.optimization_barrier((own, other_w))
 
+    blocks = 2 * experts
+    wide = blocks * SUB
+    table, wm, wx = call(
+        route_kernel,
+        [
+            pltpu.HBM((wide + blocks, rows), BF), pltpu.HBM((2 * rows, wide), BF),
+            pltpu.HBM((2 * rows, blocks), BF),
+        ],
+        2,
+        name="route",
+    )(away(routes.T), away(route_weights.T))
+
     hidden, send = dispatch(
-        tokens, own, high_need, low_free, high_free, low_need, moe_gain[None], table
+        tokens, own, high_need, low_free, high_free, low_need, moe_gain[None], away(table)
     )
 
     def exchange(v):
-        return lax.all_to_all(
-            v.reshape(experts, 2 * SUB, v.shape[1]), ("x", "y", "z"), 0, 0, tiled=True
-        ).reshape(v.shape)
-
-    back = exchange(ffn(exchange(send), own_w, other_w))
+        return lax.all_to_all(v, ("x", "y", "z"), 0, 0, tiled=True)
+
+    got = exchange(send.reshape(experts, 2 * SUB, send.shape[1]))
+    back = exchange(ffn(order, got, own_w, other_w)).reshape(send.shape)
     return combine(live, back, wm, wx, hidden)
 
 

time: 266 us -> 259 us (0.974)
  waiting for transfers between devices: 41.3 us -> 25.8 us
  between operations: 0.95 us -> 6.1 us
  starting transfers between devices: 26.2 us -> 30.8 us
  other arithmetic: 4.02 us -> 7.48 us
  Pallas kernels: 58.7 us -> 55.8 us
    ppermute x6, waiting for transfers between devices: 18.8 us -> 9.24 us  [layer(): to_up = lambda v: lax.ppermute(v, 'z', up)]
    ppermute x6, waiting for transfers between devices: 8.59 us -> 2.19 us  [layer(): to_down = lambda v: lax.ppermute(v, 'z', down)]
    ppermute x6, starting transfers between devices: 16.1 us -> 19.9 us  [layer(): to_down = lambda v: lax.ppermute(v, 'z', down)]
    pallas_call x1 -> x2, Pallas kernels: 21.1 us -> 21.2 us  [the longest x1 20.1 us: ffn(): pl.pallas_call(functools.partial(ffn_kernel, group), grid=(senders // gro...]
  transfers between devices with their start and end apart: 28 -> 28, of which waited for: 10 -> 5; matrix products, arithmetic and copies ran while one was open for 2% -> 4% of each run, Pallas kernels for 11% -> 10%
where the time goes in v3:
time: 259 us; the launch traced here: 256 us
  blocking collectives  127 us (49%)
  Pallas kernels  55.8 us (22%)
  starting transfers between devices  30.8 us (12%)
  waiting for transfers between devices  25.8 us (10%)
  other arithmetic  7.48 us (3%)
  between operations  6.1 us (2%)
  local copies, waits for them, and re-layouts  3.36 us (1%)
    all_to_all x2, blocking collectives, exchange(): return lax.all_to_all(v, ('x', 'y', 'z'), 0, 0, tiled=True)  127 us
    pallas_call x1, Pallas kernels, ffn(): pl.pallas_call(functools.partial(ffn_kernel, group), grid=(senders // gro...  20.1 us
    ppermute x6, starting transfers between devices, layer(): to_down = lambda v: lax.ppermute(v, 'z', down)  19.9 us
    all_to_all x1, waiting for transfers between devices, layer(): lax.all_to_all(outgoing, ('x', 'y'), split_axis=0, concat_axis=0, tiled=T...  14.3 us
    pallas_call x1, Pallas kernels, layer(): pl.pallas_call(lambda *refs: qkv_kernel(len(pieces), *refs), out_shape=(p...  10.3 us
    ppermute x6, waiting for transfers between devices, layer(): to_up = lambda v: lax.ppermute(v, 'z', up)  9.24 us
    all_to_all x1, starting transfers between devices, layer(): lax.all_to_all(outgoing, ('x', 'y'), split_axis=0, concat_axis=0, tiled=T...  7.18 us
    pallas_call x1, Pallas kernels, dispatch(): pl.pallas_call(dispatch_kernel, grid=((SUB + 1) // group,), out_shape=(pl...  5.4 us
  transfers between devices with their start and end apart: 28, of which 5 were waited for; matrix products, arithmetic and copies ran while one was open for 4% of the time, Pallas kernels for 10%

profile of v3, /device:TPU:24, one launch (start us, length us, event | category | flops | bytes accessed | tf_op | source)
XLA Modules:
  0.0 255.9 jit_solution(9277004338498121219)
XLA Ops:
  0.0 2.2 norm.1
  2.2 4.0 %collective-permute-start.5 = (bf16[64,2048]{1,0:T(8,128)(2,1)}, bf16[64,2048]{1,0:T(8,128)(2,1)S(1)}, u32[]{:S(2)}, u32[]{:S(2)}) collective-permute-start(bf16[64,2048]{1,0:T(8,128)(2,1)} %get-tuple-element.35), channel_id=1, source_target_pairs={{0,6},{2,0},{4,2},{6,4},{1,7},{3,1},{5,3},{7,5},{8,14},{10,8},{12,... | collective-permute-start | bytes 786440 | tf_op jit(solution)/shard_map/ppermute | solution.py:489
  6.2 3.3 %collective-permute-start.2 = (bf16[64,2048]{1,0:T(8,128)(2,1)}, bf16[64,2048]{1,0:T(8,128)(2,1)S(1)}, u32[]{:S(2)}, u32[]{:S(2)}) collective-permute-start(bf16[64,2048]{1,0:T(8,128)(2,1)} %get-tuple-element.36), channel_id=1, source_target_pairs={{0,6},{2,0},{4,2},{6,4},{1,7},{3,1},{5,3},{7,5},{8,14},{10,8},{12,... | collective-permute-start | bytes 786440 | tf_op jit(solution)/shard_map/ppermute | solution.py:489
  9.6 0.7 copy-done.7
  10.2 1.1 facts.1
  16.2 1.9 fusion
  18.7 1.3 convert_reduce_fusion.2
  22.1 1.3 pad_maximum_fusion
  23.6 3.1 %collective-permute-start.3 = (bf16[64,2048]{1,0:T(8,128)(2,1)S(1)}, bf16[64,2048]{1,0:T(8,128)(2,1)}, u32[]{:S(2)}, u32[]{:S(2)}) collective-permute-start(bf16[64,2048]{1,0:T(8,128)(2,1)S(1)} %collective-permute-done.2.refs_4_), channel_id=1, source_target_pairs={{0,6},{2,0},{4,2},{6,4},{1,7},{3,1},{5,3},{7,5},{8,14},{10,8},{12,... | collective-permute-start | bytes 786440 | tf_op jit(solution)/shard_map/ppermute | solution.py:489
  26.7 3.4 %collective-permute-done.1.refs_5_ = bf16[64,2048]{1,0:T(8,128)(2,1)S(1)} collective-permute-done((bf16[64,2048]{1,0:T(8,128)(2,1)S(1)}, bf16[64,2048]{1,0:T(8,128)(2,1)S(1)}, u32[]{:S(2)}, u32[]{:S(2)}) %collective-permute-start.1) | collective-permute-done | bytes 262176 | tf_op jit(solution)/shard_map/ppermute | solution.py:488
  30.2 0.7 copy-done.16
  30.9 0.6 pad_add_fusion.1.order_ref
  32.8 0.7 fusion.9
  36.4 1.6 prefix.1
  38.0 7.2 %all-to-all-start = ((bf16[16,64,512]{2,1,0:T(8,128)(2,1)}), bf16[16,64,512]{2,1,0:T(8,128)(2,1)S(1)}, u32[]{:S(2)}, u32[]{:S(2)}) async-start(bf16[16,64,512]{2,1,0:T(8,128)(2,1)} %bitcast.52), calls=%async_computation | async-start | bytes 2097152 | tf_op jit(solution)/shard_map/all_to_all | solution.py:530
  46.3 14.3 %all-to-all-done = bf16[16,64,512]{2,1,0:T(8,128)(2,1)S(1)} async-done(((bf16[16,64,512]{2,1,0:T(8,128)(2,1)}), bf16[16,64,512]{2,1,0:T(8,128)(2,1)S(1)}, u32[]{:S(2)}, u32[]{:S(2)}) %all-to-all-start) | async-done | bytes 1048608 | tf_op jit(solution)/shard_map/all_to_all | solution.py:530
  60.7 10.3 %qkv.1 = (bf16[512,512]{1,0:T(8,128)(2,1)S(1)}, bf16[1024,512]{1,0:T(8,128)(2,1)S(1)}, bf16[1024,512]{1,0:T(8,128)(2,1)S(1)}) custom-call(bf16[128,2048]{1,0:T(8,128)(2,1)} %get-tuple-element.39.refs_0_, bf16[64,2048]{1,0:T(8,128)(2,1)} %copy-done.12, bf16[64,2048]{1,0:T(8,128)(2,1)} %copy-done.13, bf16[64,2048]{1,0:T(8,128)(2,1)} %copy-done.11, ...), custom_call_target="tpu_custom_call" | custom-call | tf_op jit(solution)/shard_map/qkv/pallas_call | solution.py:573
  71.0 2.6 %attn_far.1 = (bf16[64,2048]{1,0:T(8,128)(2,1)S(1)}, bf16[64,2048]{1,0:T(8,128)(2,1)S(1)}) custom-call(bf16[512,512]{1,0:T(8,128)(2,1)S(1)} %get-tuple-element.44.q, bf16[1024,512]{1,0:T(8,128)(2,1)S(1)} %get-tuple-element.45.k, bf16[1024,512]{1,0:T(8,128)(2,1)S(1)} %get-tuple-element.46.v, bf16[1024,512]{1,0:T(8,128)(2,1)S(1)} %bitcast.40, ...), custom_call_target="tpu_custom_call" | custom-call | tf_op jit(solution)/shard_map/attn_far/pallas_call | solution.py:595
  73.6 2.4 collective-permute-start.21
  76.1 4.2 %attn_near.1 = (bf16[64,2048]{1,0:T(8,128)(2,1)S(1)}, f32[64,2048]{1,0:T(8,128)S(1)}, f32[64,2048]{1,0:T(8,128)S(1)}, bf16[64,2048]{1,0:T(8,128)(2,1)S(1)}) custom-call(bf16[512,512]{1,0:T(8,128)(2,1)S(1)} %get-tuple-element.44.q, bf16[1024,512]{1,0:T(8,128)(2,1)S(1)} %get-tuple-element.45.k, bf16[1024,512]{1,0:T(8,128)(2,1)S(1)} %get-tuple-element.46.v, ...), custom_call_target="tpu_custom_call" | custom-call | tf_op jit(solution)/shard_map/attn_near/pallas_call | solution.py:606
  80.2 2.2 collective-permute-done.21.a_got
  82.4 3.6 %collective-permute-start.24 = (bf16[64,2048]{1,0:T(8,128)(2,1)S(1)}, bf16[64,2048]{1,0:T(8,128)(2,1)S(1)}, u32[]{:S(2)}, u32[]{:S(2)}) collective-permute-start(bf16[64,2048]{1,0:T(8,128)(2,1)S(1)} %get-tuple-element.54), channel_id=1, source_target_pairs={{0,6},{2,0},{4,2},{6,4},{1,7},{3,1},{5,3},{7,5},{8,14},{10,8},{12,... | collective-permute-start | bytes 786440 | tf_op jit(solution)/shard_map/ppermute | solution.py:489
  86.2 3.5 %collective-permute-start.26 = (bf16[64,2048]{1,0:T(8,128)(2,1)S(1)}, bf16[64,2048]{1,0:T(8,128)(2,1)S(1)}, u32[]{:S(2)}, u32[]{:S(2)}) collective-permute-start(bf16[64,2048]{1,0:T(8,128)(2,1)S(1)} %get-tuple-element.56), channel_id=1, source_target_pairs={{0,6},{2,0},{4,2},{6,4},{1,7},{3,1},{5,3},{7,5},{8,14},{10,8},{12,... | collective-permute-start | bytes 786440 | tf_op jit(solution)/shard_map/ppermute | solution.py:489
  89.7 2.2 route.1
  91.9 2.6 %attn_own.1.own_ref = f32[128,2048]{1,0:T(8,128)S(1)} custom-call(bf16[512,512]{1,0:T(8,128)(2,1)S(1)} %get-tuple-element.44.q, bf16[1024,512]{1,0:T(8,128)(2,1)S(1)} %get-tuple-element.45.k, bf16[1024,512]{1,0:T(8,128)(2,1)S(1)} %get-tuple-element.46.v, bf16[1024,512]{1,0:T(8,128)(2,1)S(1)} %bitcast.42, bf16[1024,512]{1,0:T(8,128)(2,1)S(1)} %collective-permute-done.16.pb, ...), custom_call_target="tpu_custom_call" | custom-call | tf_op jit(solution)/shard_map/attn_own/pallas_call | solution.py:620
  94.6 1.8 collective-permute-done.25.b1
  96.4 4.0 %collective-permute-done.23.a1 = bf16[64,2048]{1,0:T(8,128)(2,1)S(1)} collective-permute-done((bf16[64,2048]{1,0:T(8,128)(2,1)S(1)}, bf16[64,2048]{1,0:T(8,128)(2,1)S(1)}, u32[]{:S(2)}, u32[]{:S(2)}) %collective-permute-start.23) | collective-permute-done | bytes 262176 | tf_op jit(solution)/shard_map/ppermute | solution.py:488
  100.4 5.4 %dispatch.1 = (bf16[128,2048]{1,0:T(8,128)(2,1)}, bf16[1024,2304]{1,0:T(8,128)(2,1)}) custom-call(bf16[128,2048]{1,0:T(8,128)(2,1)S(1)} %copy-done.1, f32[128,2048]{1,0:T(8,128)S(1)} %attn_own.1.own_ref, bf16[64,2048]{1,0:T(8,128)(2,1)S(1)} %collective-permute-done.23.a1, bf16[64,2048]{1,0:T(8,128)(2,1)S(1)} %collective-permute-done.24.a2, ...), custom_call_target="tpu_custom_call" | custom-call | tf_op jit(solution)/shard_map/dispatch/pallas_call | solution.py:278
  105.8 63.3 %all_to_all.21.x_hbm = bf16[64,16,2304]{2,1,0:T(8,128)(2,1)} all-to-all(bf16[64,16,2304]{2,1,0:T(8,128)(2,1)} %bitcast.51), channel_id=1, replica_groups=mesh['x'=4,'y'=4,'z'=4,'c'=2] {'x','y','z'}, dimensions={0} | all-to-all | bytes 9437184 | tf_op jit(solution)/shard_map/all_to_all | solution.py:646
  169.1 20.1 %ffn.1 = bf16[64,16,2304]{2,1,0:T(8,128)(2,1)} custom-call(s32[65]{0:T(128)S(1)} %pad_add_fusion.1.order_ref, bf16[64,16,2304]{2,1,0:T(8,128)(2,1)} %all_to_all.21.x_hbm, bf16[2048,512]{1,0:T(8,128)(2,1)} %bitcast.54, bf16[2048,512]{1,0:T(8,128)(2,1)} %bitcast.56, bf16[512,2048]{1,0:T(8,128)(2,1)} %bitcast.58, ...), custom_call_target="tpu_custom_call" | custom-call | tf_op jit(solution)/shard_map/ffn/pallas_call | solution.py:406
  189.2 63.4 %all_to_all.22 = bf16[64,16,2304]{2,1,0:T(8,128)(2,1)S(1)} all-to-all(bf16[64,16,2304]{2,1,0:T(8,128)(2,1)} %ffn.1), channel_id=1, replica_groups=mesh['x'=4,'y'=4,'z'=4,'c'=2] {'x','y','z'}, dimensions={0} | all-to-all | bytes 9437184 | tf_op jit(solution)/shard_map/all_to_all | solution.py:646
  252.5 3.4 %combine.1 = bf16[128,2048]{1,0:T(8,128)(2,1)} custom-call(s32[1]{0:T(128)} %bitcast.20.live_ref, bf16[1024,2304]{1,0:T(8,128)(2,1)S(1)} %bitcast.37, bf16[1024,2304]{1,0:T(8,128)(2,1)S(1)} %bitcast.38, bf16[256,1024]{1,0:T(8,128)(2,1)S(1)} %copy-done.2, bf16[256,128]{1,0:T(8,128)(2,1)S(1)} %copy-done.4, bf16[128,2048]{1,0:T(8,128)(2,1)S(1)} %copy-done.3), custom_call_target="tpu_custom_call" | custom-call | tf_op jit(solution)/shard_map/combine/pallas_call | solution.py:458
  (92 shorter events, 7.4 us)
Async XLA Ops:
  2.2 18.2 %collective-permute-start.5 = (bf16[64,2048]{1,0:T(8,128)(2,1)}, bf16[64,2048]{1,0:T(8,128)(2,1)S(1)}, u32[]{:S(2)}, u32[]{:S(2)}) collective-permute-start(bf16[64,2048]{1,0:T(8,128)(2,1)} %get-tuple-element.35), channel_id=1, source_target_pairs={{0,6},{2,0},{4,2},{6,4},{1,7},{3,1},{5,3},{7,5},{8,14},{10,8},{12,... | collective-permute-start | bytes 786440 | tf_op jit(solution)/shard_map/ppermute | solution.py:489
  6.2 13.9 %collective-permute-start = (bf16[64,2048]{1,0:T(8,128)(2,1)}, bf16[64,2048]{1,0:T(8,128)(2,1)S(1)}, u32[]{:S(2)}, u32[]{:S(2)}) collective-permute-start(bf16[64,2048]{1,0:T(8,128)(2,1)} %get-tuple-element.35), channel_id=1, source_target_pairs={{0,2},{2,4},{4,6},{6,0},{1,3},{3,5},{5,7},{7,1},{8,10},{10,12},{12... | collective-permute-start | bytes 786440 | tf_op jit(solution)/shard_map/ppermute | solution.py:488
  6.2 15.2 %collective-permute-start.4 = (bf16[64,2048]{1,0:T(8,128)(2,1)}, bf16[64,2048]{1,0:T(8,128)(2,1)S(1)}, u32[]{:S(2)}, u32[]{:S(2)}) collective-permute-start(bf16[64,2048]{1,0:T(8,128)(2,1)} %get-tuple-element.36), channel_id=1, source_target_pairs={{0,2},{2,4},{4,6},{6,0},{1,3},{3,5},{5,7},{7,1},{8,10},{10,12},{12... | collective-permute-start | bytes 786440 | tf_op jit(solution)/shard_map/ppermute | solution.py:488
  6.2 15.4 %collective-permute-start.2 = (bf16[64,2048]{1,0:T(8,128)(2,1)}, bf16[64,2048]{1,0:T(8,128)(2,1)S(1)}, u32[]{:S(2)}, u32[]{:S(2)}) collective-permute-start(bf16[64,2048]{1,0:T(8,128)(2,1)} %get-tuple-element.36), channel_id=1, source_target_pairs={{0,6},{2,0},{4,2},{6,4},{1,7},{3,1},{5,3},{7,5},{8,14},{10,8},{12,... | collective-permute-start | bytes 786440 | tf_op jit(solution)/shard_map/ppermute | solution.py:489
  16.2 20.1 %copy-start.10 = (bf16[8,64,2,256]{3,2,1,0:T(2,128)(2,1)S(1)}, bf16[8,64,2,256]{3,2,1,0:T(2,128)(2,1)}, u32[]{:S(2)}) copy-start(bf16[8,64,2,256]{3,2,1,0:T(2,128)(2,1)} %param.21) | copy-start | bytes 1572868
  20.2 3.4 %collective-permute-start.7 = (bf16[64,2048]{1,0:T(8,128)(2,1)S(1)}, bf16[64,2048]{1,0:T(8,128)(2,1)S(1)}, u32[]{:S(2)}, u32[]{:S(2)}) collective-permute-start(bf16[64,2048]{1,0:T(8,128)(2,1)S(1)} %collective-permute-done.refs_1_), channel_id=1, source_target_pairs={{0,1},{1,0},{2,3},{3,2},{4,5},{5,4},{6,7},{7,6},{8,9},{9,8},{10,11... | collective-permute-start | bytes 786440 | tf_op jit(solution)/shard_map/ppermute | solution.py:487
  20.3 9.9 %collective-permute-start.1 = (bf16[64,2048]{1,0:T(8,128)(2,1)S(1)}, bf16[64,2048]{1,0:T(8,128)(2,1)S(1)}, u32[]{:S(2)}, u32[]{:S(2)}) collective-permute-start(bf16[64,2048]{1,0:T(8,128)(2,1)S(1)} %collective-permute-done.refs_1_), channel_id=1, source_target_pairs={{0,2},{2,4},{4,6},{6,0},{1,3},{3,5},{5,7},{7,1},{8,10},{10,12},{12... | collective-permute-start | bytes 786440 | tf_op jit(solution)/shard_map/ppermute | solution.py:488
  20.4 3.1 %collective-permute-start.9 = (bf16[64,2048]{1,0:T(8,128)(2,1)S(1)}, bf16[64,2048]{1,0:T(8,128)(2,1)S(1)}, u32[]{:S(2)}, u32[]{:S(2)}) collective-permute-start(bf16[64,2048]{1,0:T(8,128)(2,1)S(1)} %collective-permute-done.5.refs_3_), channel_id=1, source_target_pairs={{0,1},{1,0},{2,3},{3,2},{4,5},{5,4},{6,7},{7,6},{8,9},{9,8},{10,11... | collective-permute-start | bytes 786440 | tf_op jit(solution)/shard_map/ppermute | solution.py:487
  21.4 14.0 %collective-permute-start.6 = (bf16[128,2048]{1,0:T(8,128)(2,1)}, bf16[128,2048]{1,0:T(8,128)(2,1)S(1)}, u32[]{:S(2)}, u32[]{:S(2)}) collective-permute-start(bf16[128,2048]{1,0:T(8,128)(2,1)} %get-tuple-element.39.refs_0_), channel_id=1, source_target_pairs={{0,1},{1,0},{2,3},{3,2},{4,5},{5,4},{6,7},{7,6},{8,9},{9,8},{10,11... | collective-permute-start | bytes 1572872 | tf_op jit(solution)/shard_map/ppermute | solution.py:487
  21.6 24.2 %collective-permute-start.14 = (bf16[2048,256]{1,0:T(8,128)(2,1)}, bf16[2048,256]{1,0:T(8,128)(2,1)}, u32[]{:S(2)}, u32[]{:S(2)}) collective-permute-start(bf16[2048,256]{1,0:T(8,128)(2,1)} %refs_16_.1), channel_id=1, source_target_pairs={{0,1},{1,0},{2,3},{3,2},{4,5},{5,4},{6,7},{7,6},{8,9},{9,8},{10,11... | collective-permute-start | bytes 3145736 | tf_op jit(solution)/shard_map/ppermute | solution.py:487
  23.5 11.8 %collective-permute-start.10 = (bf16[64,2048]{1,0:T(8,128)(2,1)S(1)}, bf16[64,2048]{1,0:T(8,128)(2,1)}, u32[]{:S(2)}, u32[]{:S(2)}) collective-permute-start(bf16[64,2048]{1,0:T(8,128)(2,1)S(1)} %collective-permute-done.2.refs_4_), channel_id=1, source_target_pairs={{0,1},{1,0},{2,3},{3,2},{4,5},{5,4},{6,7},{7,6},{8,9},{9,8},{10,11... | collective-permute-start | bytes 786440 | tf_op jit(solution)/shard_map/ppermute | solution.py:487
  23.6 9.9 %collective-permute-start.3 = (bf16[64,2048]{1,0:T(8,128)(2,1)S(1)}, bf16[64,2048]{1,0:T(8,128)(2,1)}, u32[]{:S(2)}, u32[]{:S(2)}) collective-permute-start(bf16[64,2048]{1,0:T(8,128)(2,1)S(1)} %collective-permute-done.2.refs_4_), channel_id=1, source_target_pairs={{0,6},{2,0},{4,2},{6,4},{1,7},{3,1},{5,3},{7,5},{8,14},{10,8},{12,... | collective-permute-start | bytes 786440 | tf_op jit(solution)/shard_map/ppermute | solution.py:489
  30.2 3.3 %collective-permute-start.8 = (bf16[64,2048]{1,0:T(8,128)(2,1)S(1)}, bf16[64,2048]{1,0:T(8,128)(2,1)}, u32[]{:S(2)}, u32[]{:S(2)}) collective-permute-start(bf16[64,2048]{1,0:T(8,128)(2,1)S(1)} %collective-permute-done.4.refs_2_), channel_id=1, source_target_pairs={{0,1},{1,0},{2,3},{3,2},{4,5},{5,4},{6,7},{7,6},{8,9},{9,8},{10,11... | collective-permute-start | bytes 786440 | tf_op jit(solution)/shard_map/ppermute | solution.py:487
  33.5 12.5 %collective-permute-start.13 = (bf16[2048,256]{1,0:T(8,128)(2,1)S(1)}, bf16[2048,256]{1,0:T(8,128)(2,1)}, u32[]{:S(2)}, u32[]{:S(2)}) collective-permute-start(bf16[2048,256]{1,0:T(8,128)(2,1)S(1)} %copy-done.8), channel_id=1, source_target_pairs={{0,1},{1,0},{2,3},{3,2},{4,5},{5,4},{6,7},{7,6},{8,9},{9,8},{10,11... | collective-permute-start | bytes 3145736 | tf_op jit(solution)/shard_map/ppermute | solution.py:487
  33.5 27.1 %collective-permute-start.15 = (bf16[2048,256]{1,0:T(8,128)(2,1)}, bf16[2048,256]{1,0:T(8,128)(2,1)}, u32[]{:S(2)}, u32[]{:S(2)}) collective-permute-start(bf16[2048,256]{1,0:T(8,128)(2,1)} %refs_18_.1), channel_id=1, source_target_pairs={{0,1},{1,0},{2,3},{3,2},{4,5},{5,4},{6,7},{7,6},{8,9},{9,8},{10,11... | collective-permute-start | bytes 3145736 | tf_op jit(solution)/shard_map/ppermute | solution.py:487
  35.3 9.9 %collective-permute-start.11 = (bf16[64,2048]{1,0:T(8,128)(2,1)}, bf16[64,2048]{1,0:T(8,128)(2,1)}, u32[]{:S(2)}, u32[]{:S(2)}) collective-permute-start(bf16[64,2048]{1,0:T(8,128)(2,1)} %copy-done.16), channel_id=1, source_target_pairs={{0,1},{1,0},{2,3},{3,2},{4,5},{5,4},{6,7},{7,6},{8,9},{9,8},{10,11... | collective-permute-start | bytes 786440 | tf_op jit(solution)/shard_map/ppermute | solution.py:487
  35.5 9.8 %collective-permute-start.12 = (bf16[64,2048]{1,0:T(8,128)(2,1)}, bf16[64,2048]{1,0:T(8,128)(2,1)}, u32[]{:S(2)}, u32[]{:S(2)}) collective-permute-start(bf16[64,2048]{1,0:T(8,128)(2,1)} %collective-permute-done.3.refs_6_), channel_id=1, source_target_pairs={{0,1},{1,0},{2,3},{3,2},{4,5},{5,4},{6,7},{7,6},{8,9},{9,8},{10,11... | collective-permute-start | bytes 786440 | tf_op jit(solution)/shard_map/ppermute | solution.py:487
  38.0 22.6 %all-to-all-start = ((bf16[16,64,512]{2,1,0:T(8,128)(2,1)}), bf16[16,64,512]{2,1,0:T(8,128)(2,1)S(1)}, u32[]{:S(2)}, u32[]{:S(2)}) async-start(bf16[16,64,512]{2,1,0:T(8,128)(2,1)} %bitcast.52), calls=%async_computation | async-start | bytes 2097152 | tf_op jit(solution)/shard_map/all_to_all | solution.py:530
  45.2 40.9 %collective-permute-start.18 = (bf16[2048,512]{1,0:T(8,128)(2,1)}, bf16[2048,512]{1,0:T(8,128)(2,1)}, u32[]{:S(2)}, u32[]{:S(2)}) collective-permute-start(bf16[2048,512]{1,0:T(8,128)(2,1)} %bitcast.53), channel_id=1, source_target_pairs={{0,1},{1,0},{2,3},{3,2},{4,5},{5,4},{6,7},{7,6},{8,9},{9,8},{10,11... | collective-permute-start | bytes 6291464 | tf_op jit(solution)/shard_map/ppermute | solution.py:487
  45.3 40.9 %collective-permute-start.19 = (bf16[2048,512]{1,0:T(8,128)(2,1)}, bf16[2048,512]{1,0:T(8,128)(2,1)}, u32[]{:S(2)}, u32[]{:S(2)}) collective-permute-start(bf16[2048,512]{1,0:T(8,128)(2,1)} %bitcast.55), channel_id=1, source_target_pairs={{0,1},{1,0},{2,3},{3,2},{4,5},{5,4},{6,7},{7,6},{8,9},{9,8},{10,11... | collective-permute-start | bytes 6291464 | tf_op jit(solution)/shard_map/ppermute | solution.py:487
  45.8 48.8 %collective-permute-start.20 = (bf16[512,2048]{1,0:T(8,128)(2,1)}, bf16[512,2048]{1,0:T(8,128)(2,1)}, u32[]{:S(2)}, u32[]{:S(2)}) collective-permute-start(bf16[512,2048]{1,0:T(8,128)(2,1)} %bitcast.57), channel_id=1, source_target_pairs={{0,1},{1,0},{2,3},{3,2},{4,5},{5,4},{6,7},{7,6},{8,9},{9,8},{10,11... | collective-permute-start | bytes 6291464 | tf_op jit(solution)/shard_map/ppermute | solution.py:487
  45.9 25.0 %collective-permute-start.17 = (bf16[256,2048]{1,0:T(8,128)(2,1)S(1)}, bf16[256,2048]{1,0:T(8,128)(2,1)S(1)}, u32[]{:S(2)}, u32[]{:S(2)}) collective-permute-start(bf16[256,2048]{1,0:T(8,128)(2,1)S(1)} %copy-done), channel_id=1, source_target_pairs={{0,1},{1,0},{2,3},{3,2},{4,5},{5,4},{6,7},{7,6},{8,9},{9,8},{10,11... | collective-permute-start | bytes 3145736 | tf_op jit(solution)/shard_map/ppermute | solution.py:487
  60.7 10.3 %collective-permute-start.16 = (bf16[1024,512]{1,0:T(8,128)(2,1)S(1)}, bf16[1024,512]{1,0:T(8,128)(2,1)S(1)}, u32[]{:S(2)}, u32[]{:S(2)}) collective-permute-start(bf16[1024,512]{1,0:T(8,128)(2,1)S(1)} %bitcast.39), channel_id=1, source_target_pairs={{0,1},{1,0},{2,3},{3,2},{4,5},{5,4},{6,7},{7,6},{8,9},{9,8},{10,11... | collective-permute-start | bytes 3145736 | tf_op jit(solution)/shard_map/ppermute | solution.py:487
  73.6 8.8 %collective-permute-start.21 = (bf16[64,2048]{1,0:T(8,128)(2,1)S(1)}, bf16[64,2048]{1,0:T(8,128)(2,1)S(1)}, u32[]{:S(2)}, u32[]{:S(2)}) collective-permute-start(bf16[64,2048]{1,0:T(8,128)(2,1)S(1)} %get-tuple-element.50), channel_id=1, source_target_pairs={{0,6},{2,0},{4,2},{6,4},{1,7},{3,1},{5,3},{7,5},{8,14},{10,8},{12,... | collective-permute-start | bytes 786440 | tf_op jit(solution)/shard_map/ppermute | solution.py:489
  76.1 9.9 %collective-permute-start.22 = (bf16[64,2048]{1,0:T(8,128)(2,1)S(1)}, bf16[64,2048]{1,0:T(8,128)(2,1)S(1)}, u32[]{:S(2)}, u32[]{:S(2)}) collective-permute-start(bf16[64,2048]{1,0:T(8,128)(2,1)S(1)} %get-tuple-element.52), channel_id=1, source_target_pairs={{0,2},{2,4},{4,6},{6,0},{1,3},{3,5},{5,7},{7,1},{8,10},{10,12},{12... | collective-permute-start | bytes 786440 | tf_op jit(solution)/shard_map/ppermute | solution.py:488
  82.4 12.2 %collective-permute-start.24 = (bf16[64,2048]{1,0:T(8,128)(2,1)S(1)}, bf16[64,2048]{1,0:T(8,128)(2,1)S(1)}, u32[]{:S(2)}, u32[]{:S(2)}) collective-permute-start(bf16[64,2048]{1,0:T(8,128)(2,1)S(1)} %get-tuple-element.54), channel_id=1, source_target_pairs={{0,6},{2,0},{4,2},{6,4},{1,7},{3,1},{5,3},{7,5},{8,14},{10,8},{12,... | collective-permute-start | bytes 786440 | tf_op jit(solution)/shard_map/ppermute | solution.py:489
  86.0 10.4 %collective-permute-start.25 = (bf16[64,2048]{1,0:T(8,128)(2,1)S(1)}, bf16[64,2048]{1,0:T(8,128)(2,1)S(1)}, u32[]{:S(2)}, u32[]{:S(2)}) collective-permute-start(bf16[64,2048]{1,0:T(8,128)(2,1)S(1)} %get-tuple-element.55), channel_id=1, source_target_pairs={{0,2},{2,4},{4,6},{6,0},{1,3},{3,5},{5,7},{7,1},{8,10},{10,12},{12... | collective-permute-start | bytes 786440 | tf_op jit(solution)/shard_map/ppermute | solution.py:488
  86.1 14.3 %collective-permute-start.23 = (bf16[64,2048]{1,0:T(8,128)(2,1)S(1)}, bf16[64,2048]{1,0:T(8,128)(2,1)S(1)}, u32[]{:S(2)}, u32[]{:S(2)}) collective-permute-start(bf16[64,2048]{1,0:T(8,128)(2,1)S(1)} %get-tuple-element.53), channel_id=1, source_target_pairs={{0,2},{2,4},{4,6},{6,0},{1,3},{3,5},{5,7},{7,1},{8,10},{10,12},{12... | collective-permute-start | bytes 786440 | tf_op jit(solution)/shard_map/ppermute | solution.py:488
  86.2 14.2 %collective-permute-start.26 = (bf16[64,2048]{1,0:T(8,128)(2,1)S(1)}, bf16[64,2048]{1,0:T(8,128)(2,1)S(1)}, u32[]{:S(2)}, u32[]{:S(2)}) collective-permute-start(bf16[64,2048]{1,0:T(8,128)(2,1)S(1)} %get-tuple-element.56), channel_id=1, source_target_pairs={{0,6},{2,0},{4,2},{6,4},{1,7},{3,1},{5,3},{7,5},{8,14},{10,8},{12,... | collective-permute-start | bytes 786440 | tf_op jit(solution)/shard_map/ppermute | solution.py:489
  189.1 63.4 %copy-start.2 = (bf16[256,1024]{1,0:T(8,128)(2,1)S(1)}, bf16[256,1024]{1,0:T(8,128)(2,1)}, u32[]{:S(2)}) copy-start(bf16[256,1024]{1,0:T(8,128)(2,1)} %get-tuple-element.62.wm_ref) | copy-start | bytes 1572868
  189.2 63.4 %copy-start.3 = (bf16[128,2048]{1,0:T(8,128)(2,1)S(1)}, bf16[128,2048]{1,0:T(8,128)(2,1)}, u32[]{:S(2)}) copy-start(bf16[128,2048]{1,0:T(8,128)(2,1)} %get-tuple-element.64.h_ref) | copy-start | bytes 1572868
  189.2 63.4 %copy-start.4 = (bf16[256,128]{1,0:T(8,128)(2,1)S(1)}, bf16[256,128]{1,0:T(8,128)(2,1)}, u32[]{:S(2)}) copy-start(bf16[256,128]{1,0:T(8,128)(2,1)} %get-tuple-element.63.wx_ref) | copy-start | bytes 196612
  (14 other events, 154.6 us)

commit v4 on v3

--- a/solution.py
+++ b/solution.py
@@ -3,6 +3,7 @@
 
 import jax
 import jax.numpy as jnp
+import numpy as np
 from jax import lax
 from jax.experimental import pallas as pl
 from jax.experimental.pallas import tpu as pltpu
@@ -25,11 +26,15 @@
     return pltpu.CompilerParams(vmem_limit_bytes=mib << 20)
 
 
-def call(kernel, out_shape, n_in, mib=16, **kw):
+def smem():
+    return pl.BlockSpec(memory_space=pltpu.SMEM)
+
+
+def call(kernel, out_shape, n_in, mib=16, lengths=0, **kw):
     outs = jax.tree.map(lambda _: vmem(), out_shape)
     return pl.pallas_call(
-        kernel, out_shape=out_shape, in_specs=[vmem()] * n_in, out_specs=outs,
-        compiler_params=limit(mib), **kw
+        kernel, out_shape=out_shape, in_specs=[vmem()] * n_in + [smem()] * lengths,
+        out_specs=outs, compiler_params=limit(mib), **kw
     )
 
 
@@ -61,11 +66,24 @@
     last_ref[...] = normed[half:]
 
 
-def facts_kernel(a_ref, b_ref, o_ref):
-    for i in range(a_ref.shape[0]):
-        o_ref[i] = a_ref[i]
-    for i in range(b_ref.shape[0]):
-        o_ref[a_ref.shape[0] + i] = b_ref[i]
+def seat():
+    req = lax.axis_index("x") * lax.axis_size("y") + lax.axis_index("y")
+    return req, lax.axis_index("z"), lax.axis_index("c")
+
+
+def held_blocks():
+    _, z, core = seat()
+    zs = lax.axis_size("z")
+    chips = [lax.rem(z + d, zs) for d in (0, zs - 1, 1, 2)]
+    return [chip * 2 + who for who in (core, 1 - core) for chip in chips]
+
+
+def tables(rows, blocks):
+    freqs = 10000.0 ** (-(np.arange(HD // 2) * 2.0) / HD)
+    freqs = np.concatenate([freqs, freqs])
+    first = (PREFIX + rows * np.arange(blocks))[:, None] * freqs
+    within = np.arange(rows)[:, None] * freqs
+    return [f(a).astype(np.float32) for a in (first, within) for f in (np.cos, np.sin)]
 
 
 def slots_of(index):
@@ -73,8 +91,27 @@
     return block // 2, (block % 2) * (SUB + 1) + index % SUB
 
 
-def route_kernel(rt_ref, wt_ref, dt_ref, wm_ref, wx_ref):
+def route_kernel(zs, len_ref, rt_ref, wt_ref, dt_ref, wm_ref, wx_ref, order_ref):
     top, rows = rt_ref.shape
+    _, _, core = seat()
+    senders = order_ref.shape[0] - 1
+
+    def pick(wanted):
+        def step(s, n):
+            full = len_ref[s // zs] > (s % zs * 2 + core) * rows
+            take = full == wanted
+
+            @pl.when(take)
+            def _():
+                order_ref[n] = s
+
+            return n + take.astype(jnp.int32)
+
+        return step
+
+    count = lax.fori_loop(0, senders, pick(True), jnp.int32(0))
+    order_ref[senders] = count
+    lax.fori_loop(0, senders, pick(False), count)
     blocks = wx_ref.shape[1]
     experts = blocks // 2
     wide = blocks * SUB
@@ -128,7 +165,8 @@
 
 def qkv_kernel(count, *refs):
     pieces, weights, refs = refs[:count], refs[count : count + 6], refs[count + 6 :]
-    cos_ref, sin_ref, q_ref, k_ref, v_ref, x_ref, w_ref, x_sem, w_sem = refs
+    c0_ref, s0_ref, c1_ref, s1_ref, q_ref, k_ref, v_ref, x_ref, w_ref = refs[:9]
+    cos_ref, sin_ref, x_sem, w_sem = refs[9:]
     at = 0
     copies = []
     for i, piece in enumerate(pieces):
@@ -148,6 +186,13 @@
         copy.start()
     for load in loads[2:]:
         load.start()
+    n = c1_ref.shape[0]
+    side = jnp.where(lax.broadcasted_iota(jnp.int32, (n, HD), 1) < HD // 2, -1.0, 1.0)
+    for i, block in enumerate(held_blocks()):
+        c0, s0 = c0_ref[pl.ds(block, 1), :], s0_ref[pl.ds(block, 1), :]
+        here = slice(i * n, (i + 1) * n)
+        cos_ref[here, :] = c0 * c1_ref[...] - s0 * s1_ref[...]
+        sin_ref[here, :] = side * (s0 * c1_ref[...] + c0 * s1_ref[...])
     half = q_ref.shape[0]
     at, left = 0, list(copies)
     for rows in (slice(0, half), slice(half, 2 * half)):
@@ -170,7 +215,14 @@
                 o_ref[rows, h * HD : (h + 1) * HD] = turned.astype(BF)
 
 
-def attend(scale, q_ref, k_ref, v_ref, pre_refs, bias_ref, o_ref, first):
+def attend(scale, q_ref, k_ref, v_ref, pre_refs, len_ref, o_ref, first):
+    req, _, _ = seat()
+    blocks = held_blocks()
+    n = k_ref.shape[0] // len(blocks)
+    lane = lax.broadcasted_iota(jnp.int32, (1, n), 1)
+    bias = jnp.concatenate(
+        [jnp.where(block * n + lane < len_ref[req], 0.0, -1e30) for block in blocks], axis=1
+    )
     local = pre_refs[0].shape[1] // 2
     rows = o_ref.shape[0]
     nt = (((1,), (1,)), ((), ()))
@@ -180,7 +232,7 @@
         cols = slice(h * HD, (h + 1) * HD)
         q = q_ref[first : first + rows, cols]
         s1 = lax.dot_general(q, pre_ref[:, col : col + HD], nt, preferred_element_type=F32)
-        s2 = lax.dot_general(q, k_ref[:, cols], nt, preferred_element_type=F32) + bias_ref[...]
+        s2 = lax.dot_general(q, k_ref[:, cols], nt, preferred_element_type=F32) + bias
         top = jnp.maximum(
             jnp.max(s1, axis=-1, keepdims=True), jnp.max(s2, axis=-1, keepdims=True)
         )
@@ -197,8 +249,8 @@
     return dot(a_ref[:, :local], wa_ref[...]) + dot(a_ref[:, local:], wb_ref[...])
 
 
-def attn_far_kernel(scale, first, q, k, v, pa, pb, bias, wa, wb, o1, o2, tmp):
-    attend(scale, q, k, v, (pa, pb), bias, tmp, first)
+def attn_far_kernel(scale, first, q, k, v, pa, pb, wa, wb, lens, o1, o2, tmp):
+    attend(scale, q, k, v, (pa, pb), lens, tmp, first)
     total = project(tmp, wa, wb).astype(BF)
     rows = o1.shape[0]
     o1[...] = total[:rows]
@@ -206,17 +258,17 @@
 
 
 def attn_near_kernel(
-    scale, first, q, k, v, pa, pb, bias, wa, wb, low_free, low_need, high_need, high_free, tmp
+    scale, first, q, k, v, pa, pb, wa, wb, lens, low_free, low_need, high_need, high_free, tmp
 ):
-    attend(scale, q, k, v, (pa, pb), bias, tmp, first)
+    attend(scale, q, k, v, (pa, pb), lens, tmp, first)
     total = project(tmp, wa, wb)
     n = low_free.shape[0]
     for i, o_ref in enumerate((low_free, low_need, high_need, high_free)):
         o_ref[...] = total[i * n : (i + 1) * n].astype(o_ref.dtype)
 
 
-def attn_own_kernel(scale, first, q, k, v, pa, pb, bias, wa, wb, o, tmp):
-    attend(scale, q, k, v, (pa, pb), bias, tmp, first)
+def attn_own_kernel(scale, first, q, k, v, pa, pb, wa, wb, lens, o, tmp):
+    attend(scale, q, k, v, (pa, pb), lens, tmp, first)
     o[...] = project(tmp, wa, wb)
 
 
@@ -290,9 +342,8 @@
 
 
 def ffn_kernel(group, order_ref, x_hbm, *refs):
-    sources = refs[:6]
-    o_hbm, x_ref, o_ref, wgu, wd, rows_ref, act, extra, w_sem, x_sem, o_sem = refs[6:]
-    j = pl.program_id(0)
+    weights = refs[:3], refs[3:6]
+    o_hbm, x_ref, o_ref, rows_ref, act, extra, x_sem, o_sem = refs[6:]
     senders, each = x_hbm.shape[:2]
     width = rows_ref.shape[1]
     part = width // SUB
@@ -300,13 +351,6 @@
     blocks = wide // SUB
     hidden = act.shape[1] // 2
     steps = (order_ref[senders] + group - 1) // group
-    copies = []
-    for h in range(2):
-        targets = (
-            wgu.at[h, :, :hidden], wgu.at[h, :, hidden:], wd.at[h * hidden : (h + 1) * hidden]
-        )
-        for i, target in enumerate(targets):
-            copies.append(pltpu.make_async_copy(sources[3 * h + i], target, w_sem.at[h, i]))
 
     def moves(step, inward):
         slot = step % 2
@@ -329,21 +373,17 @@
         for move in moves(step, inward):
             move.wait()
 
-    @pl.when(j == 0)
+    @pl.when(steps > 0)
     def _():
-        copies[0].start()
-        copies[1].start()
         start(0, True)
-        for i in (3, 4, 2, 5):
-            copies[i].start()
-
-    @pl.when(j + 1 < steps)
-    def _():
-        start(j + 1, True)
-
-    @pl.when(j < steps)
-    def _():
+
+    def body(j, carry):
         slot = j % 2
+
+        @pl.when(j + 1 < steps)
+        def _():
+            start(j + 1, True)
+
         wait(j, True)
         rows_ref[:wide, :] = x_ref[slot, :, :width]
         for i in range(part // 128):
@@ -354,28 +394,18 @@
                 rows_ref[wide:, col : col + 128] = extra[i, pl.ds(b, blocks, stride=SUB), :].astype(
                     BF
                 )
-        for h in range(2):
-
-            @pl.when(j == 0)
-            def _():
-                copies[3 * h].wait()
-                copies[3 * h + 1].wait()
-
-            both = dot(rows_ref[...], wgu[h])
-            gate = both[:, :hidden]
+        for h, (g_ref, u_ref, _) in enumerate(weights):
+            gate = dot(rows_ref[...], g_ref[...])
             silu = 0.5 * gate * (1.0 + jnp.tanh(0.5 * gate))
-            act[:, h * hidden : (h + 1) * hidden] = (silu * both[:, hidden:]).astype(BF)
-
-        @pl.when(j == 0)
-        def _():
-            copies[2].wait()
-            copies[5].wait()
+            upper = dot(rows_ref[...], u_ref[...])
+            act[:, h * hidden : (h + 1) * hidden] = (silu * upper).astype(BF)
 
         @pl.when(j >= 2)
         def _():
             wait(j - 2, False)
 
-        total = dot(act[...], wd[...])
+        total = dot(act[:, :hidden], weights[0][2][...])
+        total += dot(act[:, hidden:], weights[1][2][...])
         o_ref[slot, :, :width] = total[:wide].astype(BF)
         for b in range(SUB):
             for i in range(part // 128):
@@ -384,20 +414,21 @@
         for i in range(part // 128):
             o_ref[slot, :, width + i * 128 : width + (i + 1) * 128] = extra[i].astype(BF)
         start(j, False)
-
-    @pl.when(j == pl.num_programs(0) - 1)
+        return carry
+
+    lax.fori_loop(0, steps, body, 0)
+
+    @pl.when(steps >= 2)
     def _():
-        @pl.when(steps >= 2)
-        def _():
-            wait(steps - 2, False)
-
-        @pl.when(steps >= 1)
-        def _():
-            wait(steps - 1, False)
+        wait(steps - 2, False)
+
+    @pl.when(steps >= 1)
+    def _():
+        wait(steps - 1, False)
 
 
 def ffn(order, x, w0, w1):
-    senders, each, packed = x.shape
+    _, each, packed = x.shape
     width, hidden = w0[0].shape
     group = 16
     wide = group * each
@@ -405,28 +436,24 @@
     any_space = pl.BlockSpec(memory_space=pl.ANY)
     return pl.pallas_call(
         functools.partial(ffn_kernel, group),
-        grid=(senders // group,),
         out_shape=pltpu.HBM(x.shape, BF),
-        in_specs=[pl.BlockSpec(memory_space=pltpu.SMEM)] + [any_space] * 7,
+        in_specs=[smem(), any_space] + [vmem()] * 6,
         out_specs=any_space,
         scratch_shapes=[
             pltpu.VMEM((2, wide, packed), BF),
             pltpu.VMEM((2, wide, packed), BF),
-            pltpu.VMEM((2, width, 2 * hidden), BF),
-            pltpu.VMEM((2 * hidden, width), BF),
             pltpu.VMEM((rows, width), BF),
             pltpu.VMEM((rows, 2 * hidden), BF),
             pltpu.VMEM((width // SUB // 128, wide, 128), F32),
-            pltpu.SemaphoreType.DMA((2, 3)),
             pltpu.SemaphoreType.DMA((2, group)),
             pltpu.SemaphoreType.DMA((2, group)),
         ],
-        compiler_params=limit(40),
+        compiler_params=limit(24),
         name="ffn",
-    )(order, *map(away, (x, *w0, *w1)))
-
-
-def combine_kernel(live_ref, r_ref, x_ref, wm_ref, wx_ref, h_ref, o_ref, extra):
+    )(order, away(x), *map(near, (*w0, *w1)))
+
+
+def combine_kernel(len_ref, r_ref, x_ref, wm_ref, wx_ref, h_ref, o_ref, extra):
     b = pl.program_id(0)
     rows, part = o_ref.shape
     blocks = r_ref.shape[0] // SUB
@@ -446,10 +473,12 @@
     both = dot(wm_ref[...], r_ref[...]) + dot(wx_ref[...], more)
     out = h_ref[...].astype(F32) + both[:rows] + both[rows:]
     row = lax.broadcasted_iota(jnp.int32, out.shape, 0)
-    o_ref[...] = jnp.where(row < live_ref[0], out, 0.0).astype(BF)
-
-
-def combine(live, back, wm, wx, hidden):
+    req, z, core = seat()
+    live = len_ref[req] - (z * 2 + core) * rows
+    o_ref[...] = jnp.where(row < live, out, 0.0).astype(BF)
+
+
+def combine(lengths, back, wm, wx, hidden):
     rows, width = hidden.shape
     part = 2 * width // SUB
     wide = back.shape[0]
@@ -467,7 +496,7 @@
         scratch_shapes=[pltpu.VMEM((part // 256, wide, 128), F32)],
         compiler_params=limit(20),
         name="combine",
-    )(live, back, back, wm, wx, hidden)
+    )(lengths, back, back, wm, wx, hidden)
 
 
 def layer(
@@ -478,9 +507,6 @@
     zs = lax.axis_size("z")
     reqs = lax.axis_size("x") * lax.axis_size("y")
     experts = reqs * zs
-    z = lax.axis_index("z")
-    core = lax.axis_index("c")
-    req = lax.axis_index("x") * lax.axis_size("y") + lax.axis_index("y")
     local = w_query.shape[1]
     up = [(i, (i + 1) % zs) for i in range(zs)]
     down = [(i, (i - 1) % zs) for i in range(zs)]
@@ -500,16 +526,6 @@
     own_b = swap(normed)
     far0 = to_up(low0)
     far1 = to_down(high1)
-    smem = pl.BlockSpec(memory_space=pltpu.SMEM)
-    facts = pl.pallas_call(
-        facts_kernel,
-        out_shape=shape((reqs + 2,), jnp.int32),
-        in_specs=[smem] * 2,
-        out_specs=smem,
-        compiler_params=limit(2),
-        name="facts",
-    )(lengths, jnp.stack([z, core]))
-    lengths, z, core = facts[:reqs], facts[reqs], facts[reqs + 1]
     near_a = (low0, low1, high0, high1)
     near_b = tuple(swap(v) for v in near_a)
 
@@ -533,38 +549,6 @@
     own_w = (w_gate[0], w_up[0], w_down[0])
     other_w = tuple(swap(w) for w in own_w)
 
-    mine, yours = core * rows, (1 - core) * rows
-    z_low, z_high, z_far = (z + zs - 1) % zs, (z + 1) % zs, (z + 2) % zs
-    starts = jnp.stack(
-        [chip * 2 * rows + who for who in (mine, yours) for chip in (z, z_low, z_high, z_far)]
-    )
-    place = (starts[:, None] + jnp.arange(rows, dtype=jnp.int32)).reshape(-1)
-    spots = (PREFIX + place).astype(F32)
-    freqs = 10000.0 ** (-(jnp.arange(HD // 2, dtype=F32) * 2.0) / HD)
-    angles = spots[:, None] * freqs[None, :]
-    cosine = jnp.cos(angles)
-    sine = jnp.sin(angles)
-    cosine = jnp.concatenate([cosine, cosine], axis=1)
-    sine = jnp.concatenate([-sine, sine], axis=1)
-    length = lengths[req]
-    bias = jnp.where(place < length, 0.0, -1e30)[None, :]
-
-    live = jnp.clip(length - (z * 2 + core) * rows, 0, rows).astype(jnp.int32)[None]
-    sender = jnp.arange(experts, dtype=jnp.int32)
-    each = jnp.broadcast_to(lengths[:, None], (reqs, zs)).reshape(-1)
-    full = each > (sender % zs * 2 + core) * rows
-    before = sender[None, :] < sender[:, None]
-    count = jnp.sum(full.astype(jnp.int32))
-    rank = jnp.where(
-        full,
-        jnp.sum((before & full[None, :]).astype(jnp.int32), axis=1),
-        count + jnp.sum((before & ~full[None, :]).astype(jnp.int32), axis=1),
-    )
-    order = jnp.sum(jnp.where(rank[None, :] == sender[:, None], sender[None, :], 0), axis=1)
-    order = jnp.concatenate([order, count[None]])
-    far0, far1, cosine, sine, bias, live, order = lax.optimization_barrier(
-        (far0, far1, cosine, sine, bias, live, order)
-    )
     far_b = swap(far0), swap(far1)
 
 
@@ -577,28 +561,31 @@
             pltpu.VMEM((slots, 2 * local), BF),
             pltpu.VMEM((slots, 2 * local), BF),
         ),
-        in_specs=[pl.BlockSpec(memory_space=pl.ANY)] * (len(pieces) + 6) + [vmem()] * 2,
+        in_specs=[pl.BlockSpec(memory_space=pl.ANY)] * (len(pieces) + 6) + [vmem()] * 4,
         out_specs=(vmem(),) * 3,
         scratch_shapes=[
             pltpu.VMEM((slots, width), BF),
             pltpu.VMEM((3, width, 2 * local), BF),
+            pltpu.VMEM((slots, HD), F32),
+            pltpu.VMEM((slots, HD), F32),
             pltpu.SemaphoreType.DMA((len(pieces),)),
             pltpu.SemaphoreType.DMA((6,)),
         ],
         compiler_params=limit(24),
         name="qkv",
-    )(*map(away, (*pieces, *wk, *wq, *wv, cosine, sine)))
-    cache = (near(q), near(k), near(v), pre_a, pre_b, bias)
+    )(*map(away, (*pieces, *wk, *wq, *wv, *map(jnp.asarray, tables(rows, 2 * zs)))))
+    cache = (near(q), near(k), near(v), pre_a, pre_b, w_out, out_b, lengths)
     scale = math.log2(math.e) / math.sqrt(HD)
     tmp = [pltpu.VMEM((rows, 2 * local), BF)]
 
     sum1, sum2 = call(
         functools.partial(attn_far_kernel, scale, 3 * rows),
         [shape((half, width), BF)] * 2,
-        8,
+        7,
+        lengths=1,
         scratch_shapes=tmp,
         name="attn_far",
-    )(*cache, w_out, out_b)
+    )(*cache)
     got1 = to_up(sum1)
     got2 = to_down(sum2)
     part = shape((half, width), BF)
@@ -606,10 +593,11 @@
     low_free, low_need, high_need, high_free = call(
         functools.partial(attn_near_kernel, scale, rows),
         [part, wide_part, wide_part, part],
-        8,
+        7,
+        lengths=1,
         scratch_shapes=[pltpu.VMEM((2 * rows, 2 * local), BF)],
         name="attn_near",
-    )(*cache, w_out, out_b)
+    )(*cache)
     low_free = to_down(low_free)
     high_free = to_up(high_free)
     low_need, high_need = call(add_kernel, [part] * 2, 4, name="add")(
@@ -620,24 +608,26 @@
     own = call(
         functools.partial(attn_own_kernel, scale, 0),
         shape((rows, width), F32),
-        8,
+        7,
+        lengths=1,
         scratch_shapes=tmp,
         name="attn_own",
-    )(*cache, w_out, out_b)
+    )(*cache)
     own, other_w = lax.optimization_barrier((own, other_w))
 
     blocks = 2 * experts
     wide = blocks * SUB
-    table, wm, wx = call(
-        route_kernel,
-        [
+    table, wm, wx, order = pl.pallas_call(
+        functools.partial(route_kernel, zs),
+        out_shape=[
             pltpu.HBM((wide + blocks, rows), BF), pltpu.HBM((2 * rows, wide), BF),
-            pltpu.HBM((2 * rows, blocks), BF),
+            pltpu.HBM((2 * rows, blocks), BF), shape((experts + 1,), jnp.int32),
         ],
-        2,
+        in_specs=[smem(), vmem(), vmem()],
+        out_specs=[vmem(), vmem(), vmem(), smem()],
+        compiler_params=limit(16),
         name="route",
-    )(away(routes.T), away(route_weights.T))
-
+    )(lengths, away(routes.T), away(route_weights.T))
     hidden, send = dispatch(
         tokens, own, high_need, low_free, high_free, low_need, moe_gain[None], away(table)
     )
@@ -647,7 +637,7 @@
 
     got = exchange(send.reshape(experts, 2 * SUB, send.shape[1]))
     back = exchange(ffn(order, got, own_w, other_w)).reshape(send.shape)
-    return combine(live, back, wm, wx, hidden)
+    return combine(lengths, back, wm, wx, hidden)
 
 
 def solution(mesh):

time: 259 us -> 255 us (0.985)
  waiting for transfers between devices: 25.8 us -> 37.3 us
  other arithmetic: 7.48 us -> 0 us
  between operations: 6.1 us -> 0.32 us
  starting transfers between devices: 30.8 us -> 26.5 us
    ppermute x6, waiting for transfers between devices: 2.19 us -> 9.13 us  [layer(): to_down = lambda v: lax.ppermute(v, 'z', down)]
    ppermute x6, waiting for transfers between devices: 9.24 us -> 14.8 us  [layer(): to_up = lambda v: lax.ppermute(v, 'z', up)]
    ppermute x6, starting transfers between devices: 19.9 us -> 16.1 us  [layer(): to_down = lambda v: lax.ppermute(v, 'z', down)]
    pallas_call x3 -> x2, Pallas kernels: 23.4 us -> 22.6 us  [the longest x1 18.3 us: ffn(): pl.pallas_call(functools.partial(ffn_kernel, group), out_shape=pltpu.HBM(...]
  transfers between devices with their start and end apart: 28 -> 28, of which waited for: 5 -> 9; matrix products, arithmetic and copies ran while one was open for 4% -> 0% of each run, Pallas kernels for 10% -> 11%
where the time goes in v4:
time: 255 us; the launch traced here: 252 us
  blocking collectives  127 us (50%)
  Pallas kernels  57 us (22%)
  waiting for transfers between devices  37.3 us (15%)
  starting transfers between devices  26.5 us (10%)
  local copies, waits for them, and re-layouts  3.77 us (1%)
    all_to_all x2, blocking collectives, exchange(): return lax.all_to_all(v, ('x', 'y', 'z'), 0, 0, tiled=True)  127 us
    pallas_call x1, Pallas kernels, ffn(): pl.pallas_call(functools.partial(ffn_kernel, group), out_shape=pltpu.HBM(...  18.3 us
    ppermute x6, starting transfers between devices, layer(): to_down = lambda v: lax.ppermute(v, 'z', down)  16.1 us
    ppermute x6, waiting for transfers between devices, layer(): to_up = lambda v: lax.ppermute(v, 'z', up)  14.8 us
    all_to_all x1, waiting for transfers between devices, layer(): lax.all_to_all(outgoing, ('x', 'y'), split_axis=0, concat_axis=0, tiled=T...  13.3 us
    pallas_call x1, Pallas kernels, layer(): pl.pallas_call(lambda *refs: qkv_kernel(len(pieces), *refs), out_shape=(p...  10.1 us
    ppermute x6, waiting for transfers between devices, layer(): to_down = lambda v: lax.ppermute(v, 'z', down)  9.13 us
    all_to_all x1, starting transfers between devices, layer(): lax.all_to_all(outgoing, ('x', 'y'), split_axis=0, concat_axis=0, tiled=T...  7.17 us
  transfers between devices with their start and end apart: 28, of which 9 were waited for; matrix products, arithmetic and copies ran while one was open for 0% of the time, Pallas kernels for 11%

profile of v4, /device:TPU:24, one launch (start us, length us, event | category | flops | bytes accessed | tf_op | source)
XLA Modules:
  0.0 251.8 jit_solution(7003893329731280114)
XLA Ops:
  0.0 2.2 norm.1
  2.2 4.0 %collective-permute-start.2 = (bf16[64,2048]{1,0:T(8,128)(2,1)}, bf16[64,2048]{1,0:T(8,128)(2,1)S(1)}, u32[]{:S(2)}, u32[]{:S(2)}) collective-permute-start(bf16[64,2048]{1,0:T(8,128)(2,1)} %get-tuple-element.31), channel_id=1, source_target_pairs={{0,6},{2,0},{4,2},{6,4},{1,7},{3,1},{5,3},{7,5},{8,14},{10,8},{12,... | collective-permute-start | bytes 786440 | tf_op jit(solution)/shard_map/ppermute | solution.py:515
  6.2 3.2 %collective-permute-start.3 = (bf16[64,2048]{1,0:T(8,128)(2,1)}, bf16[64,2048]{1,0:T(8,128)(2,1)S(1)}, u32[]{:S(2)}, u32[]{:S(2)}) collective-permute-start(bf16[64,2048]{1,0:T(8,128)(2,1)} %get-tuple-element.32), channel_id=1, source_target_pairs={{0,6},{2,0},{4,2},{6,4},{1,7},{3,1},{5,3},{7,5},{8,14},{10,8},{12,... | collective-permute-start | bytes 786440 | tf_op jit(solution)/shard_map/ppermute | solution.py:515
  9.4 3.8 %collective-permute-done.2.refs_3_ = bf16[64,2048]{1,0:T(8,128)(2,1)S(1)} collective-permute-done((bf16[64,2048]{1,0:T(8,128)(2,1)}, bf16[64,2048]{1,0:T(8,128)(2,1)S(1)}, u32[]{:S(2)}, u32[]{:S(2)}) %collective-permute-start.2) | collective-permute-done | bytes 262176 | tf_op jit(solution)/shard_map/ppermute | solution.py:515
  13.2 3.6 %collective-permute-done.refs_1_ = bf16[64,2048]{1,0:T(8,128)(2,1)S(1)} collective-permute-done((bf16[64,2048]{1,0:T(8,128)(2,1)}, bf16[64,2048]{1,0:T(8,128)(2,1)S(1)}, u32[]{:S(2)}, u32[]{:S(2)}) %collective-permute-start) | collective-permute-done | bytes 262176 | tf_op jit(solution)/shard_map/ppermute | solution.py:514
  16.8 0.9 collective-permute-done.3.refs_4_
  17.7 3.3 %collective-permute-done.1.refs_2_ = bf16[64,2048]{1,0:T(8,128)(2,1)S(1)} collective-permute-done((bf16[64,2048]{1,0:T(8,128)(2,1)}, bf16[64,2048]{1,0:T(8,128)(2,1)S(1)}, u32[]{:S(2)}, u32[]{:S(2)}) %collective-permute-start.1) | collective-permute-done | bytes 262176 | tf_op jit(solution)/shard_map/ppermute | solution.py:514
  21.9 4.9 %collective-permute-done.4.refs_5_ = bf16[64,2048]{1,0:T(8,128)(2,1)} collective-permute-done((bf16[64,2048]{1,0:T(8,128)(2,1)S(1)}, bf16[64,2048]{1,0:T(8,128)(2,1)}, u32[]{:S(2)}, u32[]{:S(2)}) %collective-permute-start.4) | collective-permute-done | bytes 262176 | tf_op jit(solution)/shard_map/ppermute | solution.py:514
  27.4 2.6 %collective-permute-done.5.refs_6_ = bf16[64,2048]{1,0:T(8,128)(2,1)} collective-permute-done((bf16[64,2048]{1,0:T(8,128)(2,1)S(1)}, bf16[64,2048]{1,0:T(8,128)(2,1)}, u32[]{:S(2)}, u32[]{:S(2)}) %collective-permute-start.5) | collective-permute-done | bytes 262176 | tf_op jit(solution)/shard_map/ppermute | solution.py:515
  30.7 0.8 copy-done.12
  31.5 0.5 collective-permute-start.12
  32.0 1.1 copy.22
  33.1 0.7 copy-done.10
  33.9 1.6 prefix.1
  35.5 7.2 %all-to-all-start = ((bf16[16,64,512]{2,1,0:T(8,128)(2,1)}), bf16[16,64,512]{2,1,0:T(8,128)(2,1)S(1)}, u32[]{:S(2)}, u32[]{:S(2)}) async-start(bf16[16,64,512]{2,1,0:T(8,128)(2,1)} %bitcast.29), calls=%async_computation | async-start | bytes 2097152 | tf_op jit(solution)/shard_map/all_to_all | solution.py:546
  43.3 0.9 copy-done.11
  44.3 13.3 %all-to-all-done = bf16[16,64,512]{2,1,0:T(8,128)(2,1)S(1)} async-done(((bf16[16,64,512]{2,1,0:T(8,128)(2,1)}), bf16[16,64,512]{2,1,0:T(8,128)(2,1)S(1)}, u32[]{:S(2)}, u32[]{:S(2)}) %all-to-all-start) | async-done | bytes 1048608 | tf_op jit(solution)/shard_map/all_to_all | solution.py:546
  57.6 10.1 %qkv.1 = (bf16[512,512]{1,0:T(8,128)(2,1)S(1)}, bf16[1024,512]{1,0:T(8,128)(2,1)S(1)}, bf16[1024,512]{1,0:T(8,128)(2,1)S(1)}) custom-call(bf16[128,2048]{1,0:T(8,128)(2,1)} %get-tuple-element.30.refs_0_, bf16[64,2048]{1,0:T(8,128)(2,1)} %copy-done.14, bf16[64,2048]{1,0:T(8,128)(2,1)} %copy-done.16, bf16[64,2048]{1,0:T(8,128)(2,1)} %copy-done.13, ...), custom_call_target="tpu_custom_call" | custom-call | tf_op jit(solution)/shard_map/qkv/pallas_call | solution.py:557
  67.7 3.2 %attn_far.1 = (bf16[64,2048]{1,0:T(8,128)(2,1)S(1)}, bf16[64,2048]{1,0:T(8,128)(2,1)S(1)}) custom-call(bf16[512,512]{1,0:T(8,128)(2,1)S(1)} %get-tuple-element.33.q, bf16[1024,512]{1,0:T(8,128)(2,1)S(1)} %get-tuple-element.34.k, bf16[1024,512]{1,0:T(8,128)(2,1)S(1)} %get-tuple-element.35.v, bf16[1024,512]{1,0:T(8,128)(2,1)S(1)} %bitcast.17, ...), custom_call_target="tpu_custom_call" | custom-call | tf_op jit(solution)/shard_map/attn_far/pallas_call | solution.py:581
  71.0 2.0 collective-permute-start.21
  73.1 4.8 %attn_near.1 = (bf16[64,2048]{1,0:T(8,128)(2,1)S(1)}, f32[64,2048]{1,0:T(8,128)S(1)}, f32[64,2048]{1,0:T(8,128)S(1)}, bf16[64,2048]{1,0:T(8,128)(2,1)S(1)}) custom-call(bf16[512,512]{1,0:T(8,128)(2,1)S(1)} %get-tuple-element.33.q, bf16[1024,512]{1,0:T(8,128)(2,1)S(1)} %get-tuple-element.34.k, bf16[1024,512]{1,0:T(8,128)(2,1)S(1)} %get-tuple-element.35.v, ...), custom_call_target="tpu_custom_call" | custom-call | tf_op jit(solution)/shard_map/attn_near/pallas_call | solution.py:593
  77.9 1.9 collective-permute-done.21.a_got
  79.7 3.1 %collective-permute-start.24 = (bf16[64,2048]{1,0:T(8,128)(2,1)S(1)}, bf16[64,2048]{1,0:T(8,128)(2,1)S(1)}, u32[]{:S(2)}, u32[]{:S(2)}) collective-permute-start(bf16[64,2048]{1,0:T(8,128)(2,1)S(1)} %get-tuple-element.42), channel_id=1, source_target_pairs={{0,6},{2,0},{4,2},{6,4},{1,7},{3,1},{5,3},{7,5},{8,14},{10,8},{12,... | collective-permute-start | bytes 786440 | tf_op jit(solution)/shard_map/ppermute | solution.py:515
  83.3 3.3 %collective-permute-start.26 = (bf16[64,2048]{1,0:T(8,128)(2,1)S(1)}, bf16[64,2048]{1,0:T(8,128)(2,1)S(1)}, u32[]{:S(2)}, u32[]{:S(2)}) collective-permute-start(bf16[64,2048]{1,0:T(8,128)(2,1)S(1)} %get-tuple-element.44), channel_id=1, source_target_pairs={{0,6},{2,0},{4,2},{6,4},{1,7},{3,1},{5,3},{7,5},{8,14},{10,8},{12,... | collective-permute-start | bytes 786440 | tf_op jit(solution)/shard_map/ppermute | solution.py:515
  86.6 4.4 %route.1 = (bf16[1152,128]{1,0:T(8,128)(2,1)}, bf16[256,1024]{1,0:T(8,128)(2,1)}, bf16[256,128]{1,0:T(8,128)(2,1)}, s32[65]{0:T(128)S(1)}) custom-call(s32[16]{0:T(128)S(1)} %copy-done.8, s32[8,128]{1,0:T(8,128)} %bitcast.31, f32[8,128]{1,0:T(8,128)} %bitcast.32), custom_call_target="tpu_custom_call" | custom-call | tf_op jit(solution)/shard_map/route/pallas_call | solution.py:620
  91.0 3.2 %attn_own.1.own_ref = f32[128,2048]{1,0:T(8,128)S(1)} custom-call(bf16[512,512]{1,0:T(8,128)(2,1)S(1)} %get-tuple-element.33.q, bf16[1024,512]{1,0:T(8,128)(2,1)S(1)} %get-tuple-element.34.k, bf16[1024,512]{1,0:T(8,128)(2,1)S(1)} %get-tuple-element.35.v, bf16[1024,512]{1,0:T(8,128)(2,1)S(1)} %bitcast.19, bf16[1024,512]{1,0:T(8,128)(2,1)S(1)} %collective-permute-done.16.pb, ...), custom_call_target="tpu_custom_call" | custom-call | tf_op jit(solution)/shard_map/attn_own/pallas_call | solution.py:608
  94.2 3.0 %collective-permute-done.23.a1 = bf16[64,2048]{1,0:T(8,128)(2,1)S(1)} collective-permute-done((bf16[64,2048]{1,0:T(8,128)(2,1)S(1)}, bf16[64,2048]{1,0:T(8,128)(2,1)S(1)}, u32[]{:S(2)}, u32[]{:S(2)}) %collective-permute-start.23) | collective-permute-done | bytes 262176 | tf_op jit(solution)/shard_map/ppermute | solution.py:514
  97.2 5.4 %dispatch.1 = (bf16[128,2048]{1,0:T(8,128)(2,1)}, bf16[1024,2304]{1,0:T(8,128)(2,1)}) custom-call(bf16[128,2048]{1,0:T(8,128)(2,1)S(1)} %copy-done.4, f32[128,2048]{1,0:T(8,128)S(1)} %attn_own.1.own_ref, bf16[64,2048]{1,0:T(8,128)(2,1)S(1)} %collective-permute-done.23.a1, bf16[64,2048]{1,0:T(8,128)(2,1)S(1)} %collective-permute-done.24.a2, ...), custom_call_target="tpu_custom_call" | custom-call | tf_op jit(solution)/shard_map/dispatch/pallas_call | solution.py:330
  102.7 63.3 %all_to_all.21.x_hbm = bf16[64,16,2304]{2,1,0:T(8,128)(2,1)} all-to-all(bf16[64,16,2304]{2,1,0:T(8,128)(2,1)} %bitcast.28), channel_id=1, replica_groups=mesh['x'=4,'y'=4,'z'=4,'c'=2] {'x','y','z'}, dimensions={0} | all-to-all | bytes 9437184 | tf_op jit(solution)/shard_map/all_to_all | solution.py:636
  166.0 18.3 %ffn.1 = bf16[64,16,2304]{2,1,0:T(8,128)(2,1)} custom-call(s32[65]{0:T(128)S(1)} %get-tuple-element.29.order_ref, bf16[64,16,2304]{2,1,0:T(8,128)(2,1)} %all_to_all.21.x_hbm, bf16[2048,512]{1,0:T(8,128)(2,1)S(1)} %bitcast.21, bf16[2048,512]{1,0:T(8,128)(2,1)S(1)} %bitcast.23, bf16[512,2048]{1,0:T(8,128)(2,1)S(1)} %bitcast.25, ...), custom_call_target="tpu_custom_call" | custom-call | tf_op jit(solution)/shard_map/ffn/pallas_call | solution.py:437
  184.3 63.7 %all_to_all.22 = bf16[64,16,2304]{2,1,0:T(8,128)(2,1)S(1)} all-to-all(bf16[64,16,2304]{2,1,0:T(8,128)(2,1)} %ffn.1), channel_id=1, replica_groups=mesh['x'=4,'y'=4,'z'=4,'c'=2] {'x','y','z'}, dimensions={0} | all-to-all | bytes 9437184 | tf_op jit(solution)/shard_map/all_to_all | solution.py:636
  248.0 3.8 %combine.1 = bf16[128,2048]{1,0:T(8,128)(2,1)} custom-call(s32[16]{0:T(128)S(1)} %copy-done.8, bf16[1024,2304]{1,0:T(8,128)(2,1)S(1)} %bitcast.14, bf16[1024,2304]{1,0:T(8,128)(2,1)S(1)} %bitcast.15, bf16[256,1024]{1,0:T(8,128)(2,1)S(1)} %copy-done.5, bf16[256,128]{1,0:T(8,128)(2,1)S(1)} %copy-done.7, bf16[128,2048]{1,0:T(8,128)(2,1)S(1)} %copy-done.6), custom_call_target="tpu_custom_call" | custom-call | tf_op jit(solution)/shard_map/combine/pallas_call | solution.py:487
  (80 shorter events, 3.5 us)
Async XLA Ops:
  2.2 11.0 %collective-permute-start.2 = (bf16[64,2048]{1,0:T(8,128)(2,1)}, bf16[64,2048]{1,0:T(8,128)(2,1)S(1)}, u32[]{:S(2)}, u32[]{:S(2)}) collective-permute-start(bf16[64,2048]{1,0:T(8,128)(2,1)} %get-tuple-element.31), channel_id=1, source_target_pairs={{0,6},{2,0},{4,2},{6,4},{1,7},{3,1},{5,3},{7,5},{8,14},{10,8},{12,... | collective-permute-start | bytes 786440 | tf_op jit(solution)/shard_map/ppermute | solution.py:515
  6.2 10.6 %collective-permute-start = (bf16[64,2048]{1,0:T(8,128)(2,1)}, bf16[64,2048]{1,0:T(8,128)(2,1)S(1)}, u32[]{:S(2)}, u32[]{:S(2)}) collective-permute-start(bf16[64,2048]{1,0:T(8,128)(2,1)} %get-tuple-element.31), channel_id=1, source_target_pairs={{0,2},{2,4},{4,6},{6,0},{1,3},{3,5},{5,7},{7,1},{8,10},{10,12},{12... | collective-permute-start | bytes 786440 | tf_op jit(solution)/shard_map/ppermute | solution.py:514
  6.2 11.5 %collective-permute-start.3 = (bf16[64,2048]{1,0:T(8,128)(2,1)}, bf16[64,2048]{1,0:T(8,128)(2,1)S(1)}, u32[]{:S(2)}, u32[]{:S(2)}) collective-permute-start(bf16[64,2048]{1,0:T(8,128)(2,1)} %get-tuple-element.32), channel_id=1, source_target_pairs={{0,6},{2,0},{4,2},{6,4},{1,7},{3,1},{5,3},{7,5},{8,14},{10,8},{12,... | collective-permute-start | bytes 786440 | tf_op jit(solution)/shard_map/ppermute | solution.py:515
  9.4 11.6 %collective-permute-start.1 = (bf16[64,2048]{1,0:T(8,128)(2,1)}, bf16[64,2048]{1,0:T(8,128)(2,1)S(1)}, u32[]{:S(2)}, u32[]{:S(2)}) collective-permute-start(bf16[64,2048]{1,0:T(8,128)(2,1)} %get-tuple-element.32), channel_id=1, source_target_pairs={{0,2},{2,4},{4,6},{6,0},{1,3},{3,5},{5,7},{7,1},{8,10},{10,12},{12... | collective-permute-start | bytes 786440 | tf_op jit(solution)/shard_map/ppermute | solution.py:514
  13.2 7.8 %collective-permute-start.9 = (bf16[64,2048]{1,0:T(8,128)(2,1)S(1)}, bf16[64,2048]{1,0:T(8,128)(2,1)S(1)}, u32[]{:S(2)}, u32[]{:S(2)}) collective-permute-start(bf16[64,2048]{1,0:T(8,128)(2,1)S(1)} %collective-permute-done.2.refs_3_), channel_id=1, source_target_pairs={{0,1},{1,0},{2,3},{3,2},{4,5},{5,4},{6,7},{7,6},{8,9},{9,8},{10,11... | collective-permute-start | bytes 786440 | tf_op jit(solution)/shard_map/ppermute | solution.py:513
  16.8 4.7 %collective-permute-start.7 = (bf16[64,2048]{1,0:T(8,128)(2,1)S(1)}, bf16[64,2048]{1,0:T(8,128)(2,1)S(1)}, u32[]{:S(2)}, u32[]{:S(2)}) collective-permute-start(bf16[64,2048]{1,0:T(8,128)(2,1)S(1)} %collective-permute-done.refs_1_), channel_id=1, source_target_pairs={{0,1},{1,0},{2,3},{3,2},{4,5},{5,4},{6,7},{7,6},{8,9},{9,8},{10,11... | collective-permute-start | bytes 786440 | tf_op jit(solution)/shard_map/ppermute | solution.py:513
  16.8 10.0 %collective-permute-start.4 = (bf16[64,2048]{1,0:T(8,128)(2,1)S(1)}, bf16[64,2048]{1,0:T(8,128)(2,1)}, u32[]{:S(2)}, u32[]{:S(2)}) collective-permute-start(bf16[64,2048]{1,0:T(8,128)(2,1)S(1)} %collective-permute-done.refs_1_), channel_id=1, source_target_pairs={{0,2},{2,4},{4,6},{6,0},{1,3},{3,5},{5,7},{7,1},{8,10},{10,12},{12... | collective-permute-start | bytes 786440 | tf_op jit(solution)/shard_map/ppermute | solution.py:514
  17.7 25.5 %collective-permute-start.14 = (bf16[2048,256]{1,0:T(8,128)(2,1)}, bf16[2048,256]{1,0:T(8,128)(2,1)S(1)}, u32[]{:S(2)}, u32[]{:S(2)}) collective-permute-start(bf16[2048,256]{1,0:T(8,128)(2,1)} %refs_16_.1), channel_id=1, source_target_pairs={{0,1},{1,0},{2,3},{3,2},{4,5},{5,4},{6,7},{7,6},{8,9},{9,8},{10,11... | collective-permute-start | bytes 3145736 | tf_op jit(solution)/shard_map/ppermute | solution.py:513
  21.0 9.5 %collective-permute-start.6 = (bf16[128,2048]{1,0:T(8,128)(2,1)}, bf16[128,2048]{1,0:T(8,128)(2,1)S(1)}, u32[]{:S(2)}, u32[]{:S(2)}) collective-permute-start(bf16[128,2048]{1,0:T(8,128)(2,1)} %get-tuple-element.30.refs_0_), channel_id=1, source_target_pairs={{0,1},{1,0},{2,3},{3,2},{4,5},{5,4},{6,7},{7,6},{8,9},{9,8},{10,11... | collective-permute-start | bytes 1572872 | tf_op jit(solution)/shard_map/ppermute | solution.py:513
  21.0 5.8 %collective-permute-start.10 = (bf16[64,2048]{1,0:T(8,128)(2,1)S(1)}, bf16[64,2048]{1,0:T(8,128)(2,1)S(1)}, u32[]{:S(2)}, u32[]{:S(2)}) collective-permute-start(bf16[64,2048]{1,0:T(8,128)(2,1)S(1)} %collective-permute-done.3.refs_4_), channel_id=1, source_target_pairs={{0,1},{1,0},{2,3},{3,2},{4,5},{5,4},{6,7},{7,6},{8,9},{9,8},{10,11... | collective-permute-start | bytes 786440 | tf_op jit(solution)/shard_map/ppermute | solution.py:513
  21.5 8.4 %collective-permute-start.5 = (bf16[64,2048]{1,0:T(8,128)(2,1)S(1)}, bf16[64,2048]{1,0:T(8,128)(2,1)}, u32[]{:S(2)}, u32[]{:S(2)}) collective-permute-start(bf16[64,2048]{1,0:T(8,128)(2,1)S(1)} %collective-permute-done.3.refs_4_), channel_id=1, source_target_pairs={{0,6},{2,0},{4,2},{6,4},{1,7},{3,1},{5,3},{7,5},{8,14},{10,8},{12,... | collective-permute-start | bytes 786440 | tf_op jit(solution)/shard_map/ppermute | solution.py:515
  26.8 3.1 %collective-permute-start.8 = (bf16[64,2048]{1,0:T(8,128)(2,1)S(1)}, bf16[64,2048]{1,0:T(8,128)(2,1)S(1)}, u32[]{:S(2)}, u32[]{:S(2)}) collective-permute-start(bf16[64,2048]{1,0:T(8,128)(2,1)S(1)} %collective-permute-done.1.refs_2_), channel_id=1, source_target_pairs={{0,1},{1,0},{2,3},{3,2},{4,5},{5,4},{6,7},{7,6},{8,9},{9,8},{10,11... | collective-permute-start | bytes 786440 | tf_op jit(solution)/shard_map/ppermute | solution.py:513
  26.9 17.4 %collective-permute-start.13 = (bf16[2048,256]{1,0:T(8,128)(2,1)}, bf16[2048,256]{1,0:T(8,128)(2,1)}, u32[]{:S(2)}, u32[]{:S(2)}) collective-permute-start(bf16[2048,256]{1,0:T(8,128)(2,1)} %refs_14_.1), channel_id=1, source_target_pairs={{0,1},{1,0},{2,3},{3,2},{4,5},{5,4},{6,7},{7,6},{8,9},{9,8},{10,11... | collective-permute-start | bytes 3145736 | tf_op jit(solution)/shard_map/ppermute | solution.py:513
  29.9 27.7 %collective-permute-start.15 = (bf16[2048,256]{1,0:T(8,128)(2,1)}, bf16[2048,256]{1,0:T(8,128)(2,1)}, u32[]{:S(2)}, u32[]{:S(2)}) collective-permute-start(bf16[2048,256]{1,0:T(8,128)(2,1)} %refs_18_.1), channel_id=1, source_target_pairs={{0,1},{1,0},{2,3},{3,2},{4,5},{5,4},{6,7},{7,6},{8,9},{9,8},{10,11... | collective-permute-start | bytes 3145736 | tf_op jit(solution)/shard_map/ppermute | solution.py:513
  30.0 12.7 %collective-permute-start.11 = (bf16[64,2048]{1,0:T(8,128)(2,1)}, bf16[64,2048]{1,0:T(8,128)(2,1)}, u32[]{:S(2)}, u32[]{:S(2)}) collective-permute-start(bf16[64,2048]{1,0:T(8,128)(2,1)} %collective-permute-done.4.refs_5_), channel_id=1, source_target_pairs={{0,1},{1,0},{2,3},{3,2},{4,5},{5,4},{6,7},{7,6},{8,9},{9,8},{10,11... | collective-permute-start | bytes 786440 | tf_op jit(solution)/shard_map/ppermute | solution.py:513
  31.5 11.3 %collective-permute-start.12 = (bf16[64,2048]{1,0:T(8,128)(2,1)}, bf16[64,2048]{1,0:T(8,128)(2,1)}, u32[]{:S(2)}, u32[]{:S(2)}) collective-permute-start(bf16[64,2048]{1,0:T(8,128)(2,1)} %collective-permute-done.5.refs_6_), channel_id=1, source_target_pairs={{0,1},{1,0},{2,3},{3,2},{4,5},{5,4},{6,7},{7,6},{8,9},{9,8},{10,11... | collective-permute-start | bytes 786440 | tf_op jit(solution)/shard_map/ppermute | solution.py:513
  35.5 22.2 %all-to-all-start = ((bf16[16,64,512]{2,1,0:T(8,128)(2,1)}), bf16[16,64,512]{2,1,0:T(8,128)(2,1)S(1)}, u32[]{:S(2)}, u32[]{:S(2)}) async-start(bf16[16,64,512]{2,1,0:T(8,128)(2,1)} %bitcast.29), calls=%async_computation | async-start | bytes 2097152 | tf_op jit(solution)/shard_map/all_to_all | solution.py:546
  42.6 40.3 %collective-permute-start.18 = (bf16[2048,512]{1,0:T(8,128)(2,1)}, bf16[2048,512]{1,0:T(8,128)(2,1)}, u32[]{:S(2)}, u32[]{:S(2)}) collective-permute-start(bf16[2048,512]{1,0:T(8,128)(2,1)} %bitcast.20), channel_id=1, source_target_pairs={{0,1},{1,0},{2,3},{3,2},{4,5},{5,4},{6,7},{7,6},{8,9},{9,8},{10,11... | collective-permute-start | bytes 6291464 | tf_op jit(solution)/shard_map/ppermute | solution.py:513
  42.7 40.5 %collective-permute-start.19 = (bf16[2048,512]{1,0:T(8,128)(2,1)}, bf16[2048,512]{1,0:T(8,128)(2,1)}, u32[]{:S(2)}, u32[]{:S(2)}) collective-permute-start(bf16[2048,512]{1,0:T(8,128)(2,1)} %bitcast.22), channel_id=1, source_target_pairs={{0,1},{1,0},{2,3},{3,2},{4,5},{5,4},{6,7},{7,6},{8,9},{9,8},{10,11... | collective-permute-start | bytes 6291464 | tf_op jit(solution)/shard_map/ppermute | solution.py:513
  43.2 51.0 %collective-permute-start.20 = (bf16[512,2048]{1,0:T(8,128)(2,1)}, bf16[512,2048]{1,0:T(8,128)(2,1)}, u32[]{:S(2)}, u32[]{:S(2)}) collective-permute-start(bf16[512,2048]{1,0:T(8,128)(2,1)} %bitcast.24), channel_id=1, source_target_pairs={{0,1},{1,0},{2,3},{3,2},{4,5},{5,4},{6,7},{7,6},{8,9},{9,8},{10,11... | collective-permute-start | bytes 6291464 | tf_op jit(solution)/shard_map/ppermute | solution.py:513
  44.2 23.5 %collective-permute-start.17 = (bf16[256,2048]{1,0:T(8,128)(2,1)S(1)}, bf16[256,2048]{1,0:T(8,128)(2,1)S(1)}, u32[]{:S(2)}, u32[]{:S(2)}) collective-permute-start(bf16[256,2048]{1,0:T(8,128)(2,1)S(1)} %copy-done), channel_id=1, source_target_pairs={{0,1},{1,0},{2,3},{3,2},{4,5},{5,4},{6,7},{7,6},{8,9},{9,8},{10,11... | collective-permute-start | bytes 3145736 | tf_op jit(solution)/shard_map/ppermute | solution.py:513
  57.6 10.1 %collective-permute-start.16 = (bf16[1024,512]{1,0:T(8,128)(2,1)S(1)}, bf16[1024,512]{1,0:T(8,128)(2,1)S(1)}, u32[]{:S(2)}, u32[]{:S(2)}) collective-permute-start(bf16[1024,512]{1,0:T(8,128)(2,1)S(1)} %bitcast.16), channel_id=1, source_target_pairs={{0,1},{1,0},{2,3},{3,2},{4,5},{5,4},{6,7},{7,6},{8,9},{9,8},{10,11... | collective-permute-start | bytes 3145736 | tf_op jit(solution)/shard_map/ppermute | solution.py:513
  71.0 8.8 %collective-permute-start.21 = (bf16[64,2048]{1,0:T(8,128)(2,1)S(1)}, bf16[64,2048]{1,0:T(8,128)(2,1)S(1)}, u32[]{:S(2)}, u32[]{:S(2)}) collective-permute-start(bf16[64,2048]{1,0:T(8,128)(2,1)S(1)} %get-tuple-element.38), channel_id=1, source_target_pairs={{0,6},{2,0},{4,2},{6,4},{1,7},{3,1},{5,3},{7,5},{8,14},{10,8},{12,... | collective-permute-start | bytes 786440 | tf_op jit(solution)/shard_map/ppermute | solution.py:515
  73.0 9.9 %collective-permute-start.22 = (bf16[64,2048]{1,0:T(8,128)(2,1)S(1)}, bf16[64,2048]{1,0:T(8,128)(2,1)S(1)}, u32[]{:S(2)}, u32[]{:S(2)}) collective-permute-start(bf16[64,2048]{1,0:T(8,128)(2,1)S(1)} %get-tuple-element.40), channel_id=1, source_target_pairs={{0,2},{2,4},{4,6},{6,0},{1,3},{3,5},{5,7},{7,1},{8,10},{10,12},{12... | collective-permute-start | bytes 786440 | tf_op jit(solution)/shard_map/ppermute | solution.py:514
  79.7 14.5 %collective-permute-start.24 = (bf16[64,2048]{1,0:T(8,128)(2,1)S(1)}, bf16[64,2048]{1,0:T(8,128)(2,1)S(1)}, u32[]{:S(2)}, u32[]{:S(2)}) collective-permute-start(bf16[64,2048]{1,0:T(8,128)(2,1)S(1)} %get-tuple-element.42), channel_id=1, source_target_pairs={{0,6},{2,0},{4,2},{6,4},{1,7},{3,1},{5,3},{7,5},{8,14},{10,8},{12,... | collective-permute-start | bytes 786440 | tf_op jit(solution)/shard_map/ppermute | solution.py:515
  82.9 11.4 %collective-permute-start.25 = (bf16[64,2048]{1,0:T(8,128)(2,1)S(1)}, bf16[64,2048]{1,0:T(8,128)(2,1)S(1)}, u32[]{:S(2)}, u32[]{:S(2)}) collective-permute-start(bf16[64,2048]{1,0:T(8,128)(2,1)S(1)} %get-tuple-element.43), channel_id=1, source_target_pairs={{0,2},{2,4},{4,6},{6,0},{1,3},{3,5},{5,7},{7,1},{8,10},{10,12},{12... | collective-permute-start | bytes 786440 | tf_op jit(solution)/shard_map/ppermute | solution.py:514
  83.0 14.3 %collective-permute-start.23 = (bf16[64,2048]{1,0:T(8,128)(2,1)S(1)}, bf16[64,2048]{1,0:T(8,128)(2,1)S(1)}, u32[]{:S(2)}, u32[]{:S(2)}) collective-permute-start(bf16[64,2048]{1,0:T(8,128)(2,1)S(1)} %get-tuple-element.41), channel_id=1, source_target_pairs={{0,2},{2,4},{4,6},{6,0},{1,3},{3,5},{5,7},{7,1},{8,10},{10,12},{12... | collective-permute-start | bytes 786440 | tf_op jit(solution)/shard_map/ppermute | solution.py:514
  83.3 14.0 %collective-permute-start.26 = (bf16[64,2048]{1,0:T(8,128)(2,1)S(1)}, bf16[64,2048]{1,0:T(8,128)(2,1)S(1)}, u32[]{:S(2)}, u32[]{:S(2)}) collective-permute-start(bf16[64,2048]{1,0:T(8,128)(2,1)S(1)} %get-tuple-element.44), channel_id=1, source_target_pairs={{0,6},{2,0},{4,2},{6,4},{1,7},{3,1},{5,3},{7,5},{8,14},{10,8},{12,... | collective-permute-start | bytes 786440 | tf_op jit(solution)/shard_map/ppermute | solution.py:515
  102.7 63.3 %copy-start.3 = (bf16[1,512,2048]{2,1,0:T(8,128)(2,1)S(1)}, bf16[1,512,2048]{2,1,0:T(8,128)(2,1)}, u32[]{:S(2)}) copy-start(bf16[1,512,2048]{2,1,0:T(8,128)(2,1)} %param.31) | copy-start | bytes 6291460
  184.3 63.7 %copy-start.5 = (bf16[256,1024]{1,0:T(8,128)(2,1)S(1)}, bf16[256,1024]{1,0:T(8,128)(2,1)}, u32[]{:S(2)}) copy-start(bf16[256,1024]{1,0:T(8,128)(2,1)} %get-tuple-element.50.wm_ref) | copy-start | bytes 1572868
  184.3 63.7 %copy-start.6 = (bf16[128,2048]{1,0:T(8,128)(2,1)S(1)}, bf16[128,2048]{1,0:T(8,128)(2,1)}, u32[]{:S(2)}) copy-start(bf16[128,2048]{1,0:T(8,128)(2,1)} %get-tuple-element.52.h_ref) | copy-start | bytes 1572868
  184.3 63.7 %copy-start.7 = (bf16[256,128]{1,0:T(8,128)(2,1)S(1)}, bf16[256,128]{1,0:T(8,128)(2,1)}, u32[]{:S(2)}) copy-start(bf16[256,128]{1,0:T(8,128)(2,1)} %get-tuple-element.51.wx_ref) | copy-start | bytes 196612
  (17 other events, 266.1 us)

commit v5 on v4

--- a/solution.py
+++ b/solution.py
@@ -215,14 +215,13 @@
                 o_ref[rows, h * HD : (h + 1) * HD] = turned.astype(BF)
 
 
-def attend(scale, q_ref, k_ref, v_ref, pre_refs, len_ref, o_ref, first):
+def attend(scale, q_ref, k_ref, v_ref, pre_refs, len_ref, o_ref, bias_ref, first):
     req, _, _ = seat()
     blocks = held_blocks()
     n = k_ref.shape[0] // len(blocks)
     lane = lax.broadcasted_iota(jnp.int32, (1, n), 1)
-    bias = jnp.concatenate(
-        [jnp.where(block * n + lane < len_ref[req], 0.0, -1e30) for block in blocks], axis=1
-    )
+    for i, block in enumerate(blocks):
+        bias_ref[:, i * n : (i + 1) * n] = jnp.where(block * n + lane < len_ref[req], 0.0, -1e30)
     local = pre_refs[0].shape[1] // 2
     rows = o_ref.shape[0]
     nt = (((1,), (1,)), ((), ()))
@@ -232,7 +231,7 @@
         cols = slice(h * HD, (h + 1) * HD)
         q = q_ref[first : first + rows, cols]
         s1 = lax.dot_general(q, pre_ref[:, col : col + HD], nt, preferred_element_type=F32)
-        s2 = lax.dot_general(q, k_ref[:, cols], nt, preferred_element_type=F32) + bias
+        s2 = lax.dot_general(q, k_ref[:, cols], nt, preferred_element_type=F32) + bias_ref[...]
         top = jnp.maximum(
             jnp.max(s1, axis=-1, keepdims=True), jnp.max(s2, axis=-1, keepdims=True)
         )
@@ -249,8 +248,8 @@
     return dot(a_ref[:, :local], wa_ref[...]) + dot(a_ref[:, local:], wb_ref[...])
 
 
-def attn_far_kernel(scale, first, q, k, v, pa, pb, wa, wb, lens, o1, o2, tmp):
-    attend(scale, q, k, v, (pa, pb), lens, tmp, first)
+def attn_far_kernel(scale, first, q, k, v, pa, pb, wa, wb, lens, o1, o2, tmp, bias):
+    attend(scale, q, k, v, (pa, pb), lens, tmp, bias, first)
     total = project(tmp, wa, wb).astype(BF)
     rows = o1.shape[0]
     o1[...] = total[:rows]
@@ -258,17 +257,18 @@
 
 
 def attn_near_kernel(
-    scale, first, q, k, v, pa, pb, wa, wb, lens, low_free, low_need, high_need, high_free, tmp
+    scale, first, q, k, v, pa, pb, wa, wb, lens, low_free, low_need, high_need, high_free,
+    tmp, bias,
 ):
-    attend(scale, q, k, v, (pa, pb), lens, tmp, first)
+    attend(scale, q, k, v, (pa, pb), lens, tmp, bias, first)
     total = project(tmp, wa, wb)
     n = low_free.shape[0]
     for i, o_ref in enumerate((low_free, low_need, high_need, high_free)):
         o_ref[...] = total[i * n : (i + 1) * n].astype(o_ref.dtype)
 
 
-def attn_own_kernel(scale, first, q, k, v, pa, pb, wa, wb, lens, o, tmp):
-    attend(scale, q, k, v, (pa, pb), lens, tmp, first)
+def attn_own_kernel(scale, first, q, k, v, pa, pb, wa, wb, lens, o, tmp, bias):
+    attend(scale, q, k, v, (pa, pb), lens, tmp, bias, first)
     o[...] = project(tmp, wa, wb)
 
 
@@ -277,74 +277,49 @@
     b_out[...] = (b_ref[...] + b_got[...].astype(F32)).astype(BF)
 
 
-def dispatch_kernel(
-    t_ref, own_ref, a1, a2, b1, b2, g_ref, d_ref, h_ref, o_ref, normed, extra
-):
-    step = pl.program_id(0)
-    part = normed.shape[2]
-    group = o_ref.shape[1] // part
+def dispatch_kernel(t_ref, own_ref, a1, a2, b1, b2, g_ref, d_ref, h_ref, o_ref, normed, extra):
+    half = a1.shape[0]
+    width = t_ref.shape[1]
+    part = width // SUB
     wide = o_ref.shape[0]
     blocks = wide // SUB
-
-    @pl.when(step == 0)
-    def _():
-        half = a1.shape[0]
-        for at, x, y in ((0, a1, a2), (half, b1, b2)):
-            here = slice(at, at + half)
-            attn_out = own_ref[here, :] + x[...].astype(F32) + y[...].astype(F32)
-            hidden = (t_ref[here, :].astype(F32) + attn_out).astype(BF)
-            h_ref[here, :] = hidden
-            rows = rms(hidden.astype(F32), g_ref[...]).astype(BF)
-            for i in range(SUB):
-                normed[i, here, :] = rows[:, i * part : (i + 1) * part]
-
-    for i in range(group):
-        b = step * group + i
-
-        def columns(b=b, i=i):
-            x = normed[b]
-            o_ref[:, i * part : (i + 1) * part] = dot(d_ref[:wide, :], x).astype(BF)
-            more = dot(d_ref[wide:, :], x)
-            for n in range(part // 128):
-                extra[n, pl.ds(b, blocks, stride=SUB), :] = more[:, n * 128 : (n + 1) * 128]
-
-        if i < group - 1:
-            columns()
-            continue
-        pl.when(b < SUB)(columns)
-
-        @pl.when(b == SUB)
-        def _():
-            for n in range(part // 128):
-                o_ref[:, i * part + n * 128 : i * part + (n + 1) * 128] = extra[n].astype(BF)
+    for at, x, y in ((0, a1, a2), (half, b1, b2)):
+        here = slice(at, at + half)
+        attn_out = own_ref[here, :] + x[...].astype(F32) + y[...].astype(F32)
+        hidden = (t_ref[here, :].astype(F32) + attn_out).astype(BF)
+        h_ref[here, :] = hidden
+        normed[here, :] = rms(hidden.astype(F32), g_ref[...]).astype(BF)
+    for b in range(0, SUB, 2):
+        x = normed[:, b * part : (b + 2) * part]
+        o_ref[:, b * part : (b + 2) * part] = dot(d_ref[:wide, :], x).astype(BF)
+        more = dot(d_ref[wide:, :], x)
+        for n in range(2 * part // 128):
+            row, i = divmod(n, part // 128)
+            extra[i, pl.ds(b + row, blocks, stride=SUB), :] = more[:, n * 128 : (n + 1) * 128]
+    for i in range(part // 128):
+        o_ref[:, width + i * 128 : width + (i + 1) * 128] = extra[i].astype(BF)
 
 
 def dispatch(tokens, *rest):
     args = (tokens, *rest)
-    table = rest[-1]
     rows, width = tokens.shape
     part = width // SUB
-    group = 3
-    wide = table.shape[0] // (SUB + 1) * SUB
-    whole = lambda a: pl.BlockSpec(a.shape, lambda b: (0, 0))
-    return pl.pallas_call(
+    wide = rest[-1].shape[0] // (SUB + 1) * SUB
+    return call(
         dispatch_kernel,
-        grid=((SUB + 1) // group,),
-        out_shape=(pltpu.HBM((rows, width), BF), pltpu.HBM((wide, width + part), BF)),
-        in_specs=[whole(a) for a in args],
-        out_specs=(whole(tokens), pl.BlockSpec((wide, group * part), lambda b: (0, b))),
+        (pltpu.HBM((rows, width), BF), pltpu.VMEM((wide, width + part), BF)),
+        len(args),
         scratch_shapes=[
-            pltpu.VMEM((SUB, rows, part), BF), pltpu.VMEM((part // 128, wide, 128), F32),
+            pltpu.VMEM((rows, width), BF), pltpu.VMEM((part // 128, wide, 128), F32),
         ],
-        compiler_params=limit(24),
         name="dispatch",
     )(*args)
 
 
-def ffn_kernel(group, order_ref, x_hbm, *refs):
+def ffn_kernel(group, order_ref, x_ref, *refs):
     weights = refs[:3], refs[3:6]
-    o_hbm, x_ref, o_ref, rows_ref, act, extra, x_sem, o_sem = refs[6:]
-    senders, each = x_hbm.shape[:2]
+    o_ref, rows_ref, act, extra = refs[6:]
+    senders, each = x_ref.shape[:2]
     width = rows_ref.shape[1]
     part = width // SUB
     wide = group * each
@@ -352,42 +327,13 @@
     hidden = act.shape[1] // 2
     steps = (order_ref[senders] + group - 1) // group
 
-    def moves(step, inward):
-        slot = step % 2
-        out = []
+    def body(j, carry):
         for s in range(group):
-            sender = order_ref[step * group + s]
-            here = pl.ds(s * each, each)
-            if inward:
-                ends = x_hbm.at[sender], x_ref.at[slot, here]
-            else:
-                ends = o_ref.at[slot, here], o_hbm.at[sender]
-            out.append(pltpu.make_async_copy(*ends, (x_sem if inward else o_sem).at[slot, s]))
-        return out
-
-    def start(step, inward):
-        for move in moves(step, inward):
-            move.start()
-
-    def wait(step, inward):
-        for move in moves(step, inward):
-            move.wait()
-
-    @pl.when(steps > 0)
-    def _():
-        start(0, True)
-
-    def body(j, carry):
-        slot = j % 2
-
-        @pl.when(j + 1 < steps)
-        def _():
-            start(j + 1, True)
-
-        wait(j, True)
-        rows_ref[:wide, :] = x_ref[slot, :, :width]
-        for i in range(part // 128):
-            extra[i] = x_ref[slot, :, width + i * 128 : width + (i + 1) * 128].astype(F32)
+            x = x_ref.at[order_ref[j * group + s]]
+            here = slice(s * each, (s + 1) * each)
+            rows_ref[here, :] = x[:, :width]
+            for i in range(part // 128):
+                extra[i, here, :] = x[:, width + i * 128 : width + (i + 1) * 128].astype(F32)
         for b in range(SUB):
             for i in range(part // 128):
                 col = b * part + i * 128
@@ -399,104 +345,76 @@
             silu = 0.5 * gate * (1.0 + jnp.tanh(0.5 * gate))
             upper = dot(rows_ref[...], u_ref[...])
             act[:, h * hidden : (h + 1) * hidden] = (silu * upper).astype(BF)
-
-        @pl.when(j >= 2)
-        def _():
-            wait(j - 2, False)
-
         total = dot(act[:, :hidden], weights[0][2][...])
         total += dot(act[:, hidden:], weights[1][2][...])
-        o_ref[slot, :, :width] = total[:wide].astype(BF)
         for b in range(SUB):
             for i in range(part // 128):
                 col = b * part + i * 128
                 extra[i, pl.ds(b, blocks, stride=SUB), :] = total[wide:, col : col + 128]
-        for i in range(part // 128):
-            o_ref[slot, :, width + i * 128 : width + (i + 1) * 128] = extra[i].astype(BF)
-        start(j, False)
+        for s in range(group):
+            o = o_ref.at[order_ref[j * group + s]]
+            here = slice(s * each, (s + 1) * each)
+            o[:, :width] = total[here].astype(BF)
+            for i in range(part // 128):
+                o[:, width + i * 128 : width + (i + 1) * 128] = extra[i, here, :].astype(BF)
         return carry
 
     lax.fori_loop(0, steps, body, 0)
 
-    @pl.when(steps >= 2)
-    def _():
-        wait(steps - 2, False)
-
-    @pl.when(steps >= 1)
-    def _():
-        wait(steps - 1, False)
-
 
 def ffn(order, x, w0, w1):
-    _, each, packed = x.shape
     width, hidden = w0[0].shape
+    each = x.shape[1]
     group = 16
     wide = group * each
     rows = wide + wide // SUB
-    any_space = pl.BlockSpec(memory_space=pl.ANY)
     return pl.pallas_call(
         functools.partial(ffn_kernel, group),
-        out_shape=pltpu.HBM(x.shape, BF),
-        in_specs=[smem(), any_space] + [vmem()] * 6,
-        out_specs=any_space,
+        out_shape=pltpu.VMEM(x.shape, BF),
+        in_specs=[smem()] + [vmem()] * 7,
+        out_specs=vmem(),
         scratch_shapes=[
-            pltpu.VMEM((2, wide, packed), BF),
-            pltpu.VMEM((2, wide, packed), BF),
             pltpu.VMEM((rows, width), BF),
             pltpu.VMEM((rows, 2 * hidden), BF),
             pltpu.VMEM((width // SUB // 128, wide, 128), F32),
-            pltpu.SemaphoreType.DMA((2, group)),
-            pltpu.SemaphoreType.DMA((2, group)),
         ],
-        compiler_params=limit(24),
+        compiler_params=limit(16),
         name="ffn",
-    )(order, away(x), *map(near, (*w0, *w1)))
-
-
-def combine_kernel(len_ref, r_ref, x_ref, wm_ref, wx_ref, h_ref, o_ref, extra):
-    b = pl.program_id(0)
-    rows, part = o_ref.shape
+    )(order, *map(near, (x, *w0, *w1)))
+
+
+def combine_kernel(r_ref, wm_ref, wx_ref, h_ref, len_ref, o_ref, extra):
+    rows, width = o_ref.shape
+    part = width // SUB
     blocks = r_ref.shape[0] // SUB
-
-    @pl.when(b == 0)
-    def _():
-        for i in range(x_ref.shape[1] // 128):
-            extra[i] = x_ref[:, i * 128 : (i + 1) * 128].astype(F32)
-
-    each = x_ref.shape[1]
-    more = [
-        extra[i, pl.ds(b * (part // each) + n, blocks, stride=SUB), :]
-        for n in range(part // each)
-        for i in range(each // 128)
-    ]
-    more = jnp.concatenate(more, axis=1).astype(BF)
-    both = dot(wm_ref[...], r_ref[...]) + dot(wx_ref[...], more)
-    out = h_ref[...].astype(F32) + both[:rows] + both[rows:]
-    row = lax.broadcasted_iota(jnp.int32, out.shape, 0)
     req, z, core = seat()
     live = len_ref[req] - (z * 2 + core) * rows
-    o_ref[...] = jnp.where(row < live, out, 0.0).astype(BF)
+    for i in range(part // 128):
+        extra[i] = r_ref[:, width + i * 128 : width + (i + 1) * 128].astype(F32)
+    for b in range(0, SUB, 2):
+        cols = slice(b * part, (b + 2) * part)
+        more = [
+            extra[i, pl.ds(b + n, blocks, stride=SUB), :]
+            for n in range(2)
+            for i in range(part // 128)
+        ]
+        more = jnp.concatenate(more, axis=1).astype(BF)
+        both = dot(wm_ref[...], r_ref[:, cols]) + dot(wx_ref[...], more)
+        out = h_ref[:, cols].astype(F32) + both[:rows] + both[rows:]
+        row = lax.broadcasted_iota(jnp.int32, out.shape, 0)
+        o_ref[:, cols] = jnp.where(row < live, out, 0.0).astype(BF)
 
 
 def combine(lengths, back, wm, wx, hidden):
-    rows, width = hidden.shape
-    part = 2 * width // SUB
-    wide = back.shape[0]
-    whole = lambda a: pl.BlockSpec(a.shape, lambda b: (0, 0))
-    cols = lambda n: pl.BlockSpec((n, part), lambda b: (0, b))
-    return pl.pallas_call(
+    part = hidden.shape[1] // SUB
+    return call(
         combine_kernel,
-        grid=(SUB // 2,),
-        out_shape=shape((rows, width), BF),
-        in_specs=[
-            pl.BlockSpec(memory_space=pltpu.SMEM), cols(wide),
-            pl.BlockSpec((wide, part // 2), lambda b: (0, SUB)), whole(wm), whole(wx), cols(rows),
-        ],
-        out_specs=cols(rows),
-        scratch_shapes=[pltpu.VMEM((part // 256, wide, 128), F32)],
-        compiler_params=limit(20),
+        shape(hidden.shape, BF),
+        4,
+        lengths=1,
+        scratch_shapes=[pltpu.VMEM((part // 128, back.shape[0], 128), F32)],
         name="combine",
-    )(lengths, back, back, wm, wx, hidden)
+    )(near(back), wm, wx, hidden, lengths)
 
 
 def layer(
@@ -542,7 +460,7 @@
         out_specs=vmem(),
         compiler_params=limit(16),
         name="prefix",
-    )(group_of, jnp.transpose(prefix_cache, (0, 2, 1, 3)))
+    )(away(group_of), jnp.transpose(prefix_cache, (0, 2, 1, 3)))
     pre_a = lax.all_to_all(outgoing, ("x", "y"), split_axis=0, concat_axis=0, tiled=True)
     pre_b = swap(pre_a)
 
@@ -576,7 +494,8 @@
     )(*map(away, (*pieces, *wk, *wq, *wv, *map(jnp.asarray, tables(rows, 2 * zs)))))
     cache = (near(q), near(k), near(v), pre_a, pre_b, w_out, out_b, lengths)
     scale = math.log2(math.e) / math.sqrt(HD)
-    tmp = [pltpu.VMEM((rows, 2 * local), BF)]
+    masks = pltpu.VMEM((1, slots), F32)
+    tmp = [pltpu.VMEM((rows, 2 * local), BF), masks]
 
     sum1, sum2 = call(
         functools.partial(attn_far_kernel, scale, 3 * rows),
@@ -595,7 +514,7 @@
         [part, wide_part, wide_part, part],
         7,
         lengths=1,
-        scratch_shapes=[pltpu.VMEM((2 * rows, 2 * local), BF)],
+        scratch_shapes=[pltpu.VMEM((2 * rows, 2 * local), BF), masks],
         name="attn_near",
     )(*cache)
     low_free = to_down(low_free)
@@ -620,7 +539,7 @@
     table, wm, wx, order = pl.pallas_call(
         functools.partial(route_kernel, zs),
         out_shape=[
-            pltpu.HBM((wide + blocks, rows), BF), pltpu.HBM((2 * rows, wide), BF),
+            pltpu.VMEM((wide + blocks, rows), BF), pltpu.HBM((2 * rows, wide), BF),
             pltpu.HBM((2 * rows, blocks), BF), shape((experts + 1,), jnp.int32),
         ],
         in_specs=[smem(), vmem(), vmem()],
@@ -629,7 +548,7 @@
         name="route",
     )(lengths, away(routes.T), away(route_weights.T))
     hidden, send = dispatch(
-        tokens, own, high_need, low_free, high_free, low_need, moe_gain[None], away(table)
+        tokens, own, high_need, low_free, high_free, low_need, moe_gain[None], near(table)
     )
 
     def exchange(v):

time: 255 us -> 245 us (0.961)
  Pallas kernels: 57 us -> 49.5 us
    pallas_call x4, Pallas kernels: 31.9 us -> 24.2 us  [the longest x1 15.1 us: ffn(): pl.pallas_call(functools.partial(ffn_kernel, group), out_shape=pltpu.VMEM...]
where the time goes in v5:
time: 245 us; the launch traced here: 242 us
  blocking collectives  125 us (51%)
  Pallas kernels  49.5 us (20%)
  waiting for transfers between devices  37.3 us (15%)
  starting transfers between devices  26.5 us (11%)
  local copies, waits for them, and re-layouts  2.99 us (1%)
    all_to_all x2, blocking collectives, exchange(): return lax.all_to_all(v, ('x', 'y', 'z'), 0, 0, tiled=True)  125 us
    ppermute x6, starting transfers between devices, layer(): to_down = lambda v: lax.ppermute(v, 'z', down)  16.1 us
    pallas_call x1, Pallas kernels, ffn(): pl.pallas_call(functools.partial(ffn_kernel, group), out_shape=pltpu.VMEM...  15.1 us
    ppermute x6, waiting for transfers between devices, layer(): to_up = lambda v: lax.ppermute(v, 'z', up)  14.9 us
    all_to_all x1, waiting for transfers between devices, layer(): lax.all_to_all(outgoing, ('x', 'y'), split_axis=0, concat_axis=0, tiled=T...  13.3 us
    pallas_call x1, Pallas kernels, layer(): pl.pallas_call(lambda *refs: qkv_kernel(len(pieces), *refs), out_shape=(p...  10.1 us
    ppermute x6, waiting for transfers between devices, layer(): to_down = lambda v: lax.ppermute(v, 'z', down)  9.09 us
    all_to_all x1, starting transfers between devices, layer(): lax.all_to_all(outgoing, ('x', 'y'), split_axis=0, concat_axis=0, tiled=T...  7.17 us
  transfers between devices with their start and end apart: 28, of which 9 were waited for; matrix products, arithmetic and copies ran while one was open for 0% of the time, Pallas kernels for 11%

profile of v5, /device:TPU:24, one launch (start us, length us, event | category | flops | bytes accessed | tf_op | source)
XLA Modules:
  0.0 241.5 jit_solution(5681055039078273335)
XLA Ops:
  0.0 2.2 norm.1
  2.2 4.0 %collective-permute-start.2 = (bf16[64,2048]{1,0:T(8,128)(2,1)}, bf16[64,2048]{1,0:T(8,128)(2,1)S(1)}, u32[]{:S(2)}, u32[]{:S(2)}) collective-permute-start(bf16[64,2048]{1,0:T(8,128)(2,1)} %get-tuple-element.31), channel_id=1, source_target_pairs={{0,6},{2,0},{4,2},{6,4},{1,7},{3,1},{5,3},{7,5},{8,14},{10,8},{12,... | collective-permute-start | bytes 786440 | tf_op jit(solution)/shard_map/ppermute | solution.py:433
  6.2 3.2 %collective-permute-start.3 = (bf16[64,2048]{1,0:T(8,128)(2,1)}, bf16[64,2048]{1,0:T(8,128)(2,1)S(1)}, u32[]{:S(2)}, u32[]{:S(2)}) collective-permute-start(bf16[64,2048]{1,0:T(8,128)(2,1)} %get-tuple-element.32), channel_id=1, source_target_pairs={{0,6},{2,0},{4,2},{6,4},{1,7},{3,1},{5,3},{7,5},{8,14},{10,8},{12,... | collective-permute-start | bytes 786440 | tf_op jit(solution)/shard_map/ppermute | solution.py:433
  9.4 3.8 %collective-permute-done.2.refs_3_ = bf16[64,2048]{1,0:T(8,128)(2,1)S(1)} collective-permute-done((bf16[64,2048]{1,0:T(8,128)(2,1)}, bf16[64,2048]{1,0:T(8,128)(2,1)S(1)}, u32[]{:S(2)}, u32[]{:S(2)}) %collective-permute-start.2) | collective-permute-done | bytes 262176 | tf_op jit(solution)/shard_map/ppermute | solution.py:433
  13.2 3.6 %collective-permute-done.refs_1_ = bf16[64,2048]{1,0:T(8,128)(2,1)S(1)} collective-permute-done((bf16[64,2048]{1,0:T(8,128)(2,1)}, bf16[64,2048]{1,0:T(8,128)(2,1)S(1)}, u32[]{:S(2)}, u32[]{:S(2)}) %collective-permute-start) | collective-permute-done | bytes 262176 | tf_op jit(solution)/shard_map/ppermute | solution.py:432
  16.8 0.9 collective-permute-done.3.refs_4_
  17.7 3.3 %collective-permute-done.1.refs_2_ = bf16[64,2048]{1,0:T(8,128)(2,1)S(1)} collective-permute-done((bf16[64,2048]{1,0:T(8,128)(2,1)}, bf16[64,2048]{1,0:T(8,128)(2,1)S(1)}, u32[]{:S(2)}, u32[]{:S(2)}) %collective-permute-start.1) | collective-permute-done | bytes 262176 | tf_op jit(solution)/shard_map/ppermute | solution.py:432
  21.9 4.9 %collective-permute-done.4.refs_5_ = bf16[64,2048]{1,0:T(8,128)(2,1)} collective-permute-done((bf16[64,2048]{1,0:T(8,128)(2,1)S(1)}, bf16[64,2048]{1,0:T(8,128)(2,1)}, u32[]{:S(2)}, u32[]{:S(2)}) %collective-permute-start.4) | collective-permute-done | bytes 262176 | tf_op jit(solution)/shard_map/ppermute | solution.py:432
  26.8 0.5 collective-permute-start.13
  27.4 2.6 %collective-permute-done.5.refs_6_ = bf16[64,2048]{1,0:T(8,128)(2,1)} collective-permute-done((bf16[64,2048]{1,0:T(8,128)(2,1)S(1)}, bf16[64,2048]{1,0:T(8,128)(2,1)}, u32[]{:S(2)}, u32[]{:S(2)}) %collective-permute-start.5) | collective-permute-done | bytes 262176 | tf_op jit(solution)/shard_map/ppermute | solution.py:433
  30.6 0.8 copy-done.11
  31.4 0.5 collective-permute-start.12
  31.9 1.1 copy.22
  33.1 1.8 prefix.1
  34.9 7.2 %all-to-all-start = ((bf16[16,64,512]{2,1,0:T(8,128)(2,1)}), bf16[16,64,512]{2,1,0:T(8,128)(2,1)S(1)}, u32[]{:S(2)}, u32[]{:S(2)}) async-start(bf16[16,64,512]{2,1,0:T(8,128)(2,1)} %bitcast.28), calls=%async_computation | async-start | bytes 2097152 | tf_op jit(solution)/shard_map/all_to_all | solution.py:464
  42.8 0.9 copy-done.10
  43.8 13.3 %all-to-all-done = bf16[16,64,512]{2,1,0:T(8,128)(2,1)S(1)} async-done(((bf16[16,64,512]{2,1,0:T(8,128)(2,1)}), bf16[16,64,512]{2,1,0:T(8,128)(2,1)S(1)}, u32[]{:S(2)}, u32[]{:S(2)}) %all-to-all-start) | async-done | bytes 1048608 | tf_op jit(solution)/shard_map/all_to_all | solution.py:464
  57.1 10.1 %qkv.1 = (bf16[512,512]{1,0:T(8,128)(2,1)S(1)}, bf16[1024,512]{1,0:T(8,128)(2,1)S(1)}, bf16[1024,512]{1,0:T(8,128)(2,1)S(1)}) custom-call(bf16[128,2048]{1,0:T(8,128)(2,1)} %get-tuple-element.30.refs_0_, bf16[64,2048]{1,0:T(8,128)(2,1)} %copy-done.13, bf16[64,2048]{1,0:T(8,128)(2,1)} %copy-done.15, bf16[64,2048]{1,0:T(8,128)(2,1)} %copy-done.12, ...), custom_call_target="tpu_custom_call" | custom-call | tf_op jit(solution)/shard_map/qkv/pallas_call | solution.py:475
  67.2 3.2 %attn_far.1 = (bf16[64,2048]{1,0:T(8,128)(2,1)S(1)}, bf16[64,2048]{1,0:T(8,128)(2,1)S(1)}) custom-call(bf16[512,512]{1,0:T(8,128)(2,1)S(1)} %get-tuple-element.33.q, bf16[1024,512]{1,0:T(8,128)(2,1)S(1)} %get-tuple-element.34.k, bf16[1024,512]{1,0:T(8,128)(2,1)S(1)} %get-tuple-element.35.v, bf16[1024,512]{1,0:T(8,128)(2,1)S(1)} %bitcast.16, ...), custom_call_target="tpu_custom_call" | custom-call | tf_op jit(solution)/shard_map/attn_far/pallas_call | solution.py:500
  70.4 2.0 collective-permute-start.21
  72.5 4.8 %attn_near.1 = (bf16[64,2048]{1,0:T(8,128)(2,1)S(1)}, f32[64,2048]{1,0:T(8,128)S(1)}, f32[64,2048]{1,0:T(8,128)S(1)}, bf16[64,2048]{1,0:T(8,128)(2,1)S(1)}) custom-call(bf16[512,512]{1,0:T(8,128)(2,1)S(1)} %get-tuple-element.33.q, bf16[1024,512]{1,0:T(8,128)(2,1)S(1)} %get-tuple-element.34.k, bf16[1024,512]{1,0:T(8,128)(2,1)S(1)} %get-tuple-element.35.v, ...), custom_call_target="tpu_custom_call" | custom-call | tf_op jit(solution)/shard_map/attn_near/pallas_call | solution.py:512
  77.3 1.8 collective-permute-done.21.a_got
  79.2 3.1 %collective-permute-start.24 = (bf16[64,2048]{1,0:T(8,128)(2,1)S(1)}, bf16[64,2048]{1,0:T(8,128)(2,1)S(1)}, u32[]{:S(2)}, u32[]{:S(2)}) collective-permute-start(bf16[64,2048]{1,0:T(8,128)(2,1)S(1)} %get-tuple-element.42), channel_id=1, source_target_pairs={{0,6},{2,0},{4,2},{6,4},{1,7},{3,1},{5,3},{7,5},{8,14},{10,8},{12,... | collective-permute-start | bytes 786440 | tf_op jit(solution)/shard_map/ppermute | solution.py:433
  82.7 3.3 %collective-permute-start.26 = (bf16[64,2048]{1,0:T(8,128)(2,1)S(1)}, bf16[64,2048]{1,0:T(8,128)(2,1)S(1)}, u32[]{:S(2)}, u32[]{:S(2)}) collective-permute-start(bf16[64,2048]{1,0:T(8,128)(2,1)S(1)} %get-tuple-element.44), channel_id=1, source_target_pairs={{0,6},{2,0},{4,2},{6,4},{1,7},{3,1},{5,3},{7,5},{8,14},{10,8},{12,... | collective-permute-start | bytes 786440 | tf_op jit(solution)/shard_map/ppermute | solution.py:433
  86.0 4.4 %route.1 = (bf16[1152,128]{1,0:T(8,128)(2,1)S(1)}, bf16[256,1024]{1,0:T(8,128)(2,1)}, bf16[256,128]{1,0:T(8,128)(2,1)}, s32[65]{0:T(128)S(1)}) custom-call(s32[16]{0:T(128)S(1)} %copy-done.8, s32[8,128]{1,0:T(8,128)} %bitcast.30, f32[8,128]{1,0:T(8,128)} %bitcast.31), custom_call_target="tpu_custom_call" | custom-call | tf_op jit(solution)/shard_map/route/pallas_call | solution.py:539
  90.4 3.2 %attn_own.1.own_ref = f32[128,2048]{1,0:T(8,128)S(1)} custom-call(bf16[512,512]{1,0:T(8,128)(2,1)S(1)} %get-tuple-element.33.q, bf16[1024,512]{1,0:T(8,128)(2,1)S(1)} %get-tuple-element.34.k, bf16[1024,512]{1,0:T(8,128)(2,1)S(1)} %get-tuple-element.35.v, bf16[1024,512]{1,0:T(8,128)(2,1)S(1)} %bitcast.18, bf16[1024,512]{1,0:T(8,128)(2,1)S(1)} %collective-permute-done.16.pb, ...), custom_call_target="tpu_custom_call" | custom-call | tf_op jit(solution)/shard_map/attn_own/pallas_call | solution.py:527
  93.7 3.1 %collective-permute-done.23.a1 = bf16[64,2048]{1,0:T(8,128)(2,1)S(1)} collective-permute-done((bf16[64,2048]{1,0:T(8,128)(2,1)S(1)}, bf16[64,2048]{1,0:T(8,128)(2,1)S(1)}, u32[]{:S(2)}, u32[]{:S(2)}) %collective-permute-start.23) | collective-permute-done | bytes 262176 | tf_op jit(solution)/shard_map/ppermute | solution.py:432
  96.7 1.8 dispatch.1
  98.6 61.4 %all_to_all.21.x_ref = bf16[64,16,2304]{2,1,0:T(8,128)(2,1)S(1)} all-to-all(bf16[64,16,2304]{2,1,0:T(8,128)(2,1)S(1)} %bitcast.19), channel_id=1, replica_groups=mesh['x'=4,'y'=4,'z'=4,'c'=2] {'x','y','z'}, dimensions={0} | all-to-all | bytes 9437184 | tf_op jit(solution)/shard_map/all_to_all | solution.py:555
  160.0 15.1 %ffn.1 = bf16[64,16,2304]{2,1,0:T(8,128)(2,1)S(1)} custom-call(s32[65]{0:T(128)S(1)} %get-tuple-element.29.order_ref, bf16[64,16,2304]{2,1,0:T(8,128)(2,1)S(1)} %all_to_all.21.x_ref, bf16[2048,512]{1,0:T(8,128)(2,1)S(1)} %bitcast.21, bf16[2048,512]{1,0:T(8,128)(2,1)S(1)} %bitcast.23, bf16[512,2048]{1,0:T(8,128)(2,1)S(1)} %bitcast.25, ...), custom_call_target="tpu_custom_call" | custom-call | tf_op jit(solution)/shard_map/ffn/pallas_call | solution.py:371
  175.2 63.4 %all_to_all.22 = bf16[64,16,2304]{2,1,0:T(8,128)(2,1)S(1)} all-to-all(bf16[64,16,2304]{2,1,0:T(8,128)(2,1)S(1)} %ffn.1), channel_id=1, replica_groups=mesh['x'=4,'y'=4,'z'=4,'c'=2] {'x','y','z'}, dimensions={0} | all-to-all | bytes 9437184 | tf_op jit(solution)/shard_map/all_to_all | solution.py:555
  238.6 2.9 %combine.1 = bf16[128,2048]{1,0:T(8,128)(2,1)} custom-call(bf16[1024,2304]{1,0:T(8,128)(2,1)S(1)} %bitcast.14, bf16[256,1024]{1,0:T(8,128)(2,1)S(1)} %copy-done.5, bf16[256,128]{1,0:T(8,128)(2,1)S(1)} %copy-done.7, bf16[128,2048]{1,0:T(8,128)(2,1)S(1)} %copy-done.6, s32[16]{0:T(128)S(1)} %copy-done.8), custom_call_target="tpu_custom_call" | custom-call | tf_op jit(solution)/shard_map/combine/pallas_call | solution.py:410
  (78 shorter events, 3.0 us)
Async XLA Ops:
  2.2 11.0 %collective-permute-start.2 = (bf16[64,2048]{1,0:T(8,128)(2,1)}, bf16[64,2048]{1,0:T(8,128)(2,1)S(1)}, u32[]{:S(2)}, u32[]{:S(2)}) collective-permute-start(bf16[64,2048]{1,0:T(8,128)(2,1)} %get-tuple-element.31), channel_id=1, source_target_pairs={{0,6},{2,0},{4,2},{6,4},{1,7},{3,1},{5,3},{7,5},{8,14},{10,8},{12,... | collective-permute-start | bytes 786440 | tf_op jit(solution)/shard_map/ppermute | solution.py:433
  6.2 10.6 %collective-permute-start = (bf16[64,2048]{1,0:T(8,128)(2,1)}, bf16[64,2048]{1,0:T(8,128)(2,1)S(1)}, u32[]{:S(2)}, u32[]{:S(2)}) collective-permute-start(bf16[64,2048]{1,0:T(8,128)(2,1)} %get-tuple-element.31), channel_id=1, source_target_pairs={{0,2},{2,4},{4,6},{6,0},{1,3},{3,5},{5,7},{7,1},{8,10},{10,12},{12... | collective-permute-start | bytes 786440 | tf_op jit(solution)/shard_map/ppermute | solution.py:432
  6.2 11.5 %collective-permute-start.3 = (bf16[64,2048]{1,0:T(8,128)(2,1)}, bf16[64,2048]{1,0:T(8,128)(2,1)S(1)}, u32[]{:S(2)}, u32[]{:S(2)}) collective-permute-start(bf16[64,2048]{1,0:T(8,128)(2,1)} %get-tuple-element.32), channel_id=1, source_target_pairs={{0,6},{2,0},{4,2},{6,4},{1,7},{3,1},{5,3},{7,5},{8,14},{10,8},{12,... | collective-permute-start | bytes 786440 | tf_op jit(solution)/shard_map/ppermute | solution.py:433
  9.4 11.6 %collective-permute-start.1 = (bf16[64,2048]{1,0:T(8,128)(2,1)}, bf16[64,2048]{1,0:T(8,128)(2,1)S(1)}, u32[]{:S(2)}, u32[]{:S(2)}) collective-permute-start(bf16[64,2048]{1,0:T(8,128)(2,1)} %get-tuple-element.32), channel_id=1, source_target_pairs={{0,2},{2,4},{4,6},{6,0},{1,3},{3,5},{5,7},{7,1},{8,10},{10,12},{12... | collective-permute-start | bytes 786440 | tf_op jit(solution)/shard_map/ppermute | solution.py:432
  13.2 7.8 %collective-permute-start.9 = (bf16[64,2048]{1,0:T(8,128)(2,1)S(1)}, bf16[64,2048]{1,0:T(8,128)(2,1)S(1)}, u32[]{:S(2)}, u32[]{:S(2)}) collective-permute-start(bf16[64,2048]{1,0:T(8,128)(2,1)S(1)} %collective-permute-done.2.refs_3_), channel_id=1, source_target_pairs={{0,1},{1,0},{2,3},{3,2},{4,5},{5,4},{6,7},{7,6},{8,9},{9,8},{10,11... | collective-permute-start | bytes 786440 | tf_op jit(solution)/shard_map/ppermute | solution.py:431
  16.8 4.7 %collective-permute-start.7 = (bf16[64,2048]{1,0:T(8,128)(2,1)S(1)}, bf16[64,2048]{1,0:T(8,128)(2,1)S(1)}, u32[]{:S(2)}, u32[]{:S(2)}) collective-permute-start(bf16[64,2048]{1,0:T(8,128)(2,1)S(1)} %collective-permute-done.refs_1_), channel_id=1, source_target_pairs={{0,1},{1,0},{2,3},{3,2},{4,5},{5,4},{6,7},{7,6},{8,9},{9,8},{10,11... | collective-permute-start | bytes 786440 | tf_op jit(solution)/shard_map/ppermute | solution.py:431
  16.8 10.0 %collective-permute-start.4 = (bf16[64,2048]{1,0:T(8,128)(2,1)S(1)}, bf16[64,2048]{1,0:T(8,128)(2,1)}, u32[]{:S(2)}, u32[]{:S(2)}) collective-permute-start(bf16[64,2048]{1,0:T(8,128)(2,1)S(1)} %collective-permute-done.refs_1_), channel_id=1, source_target_pairs={{0,2},{2,4},{4,6},{6,0},{1,3},{3,5},{5,7},{7,1},{8,10},{10,12},{12... | collective-permute-start | bytes 786440 | tf_op jit(solution)/shard_map/ppermute | solution.py:432
  17.7 25.0 %collective-permute-start.14 = (bf16[2048,256]{1,0:T(8,128)(2,1)}, bf16[2048,256]{1,0:T(8,128)(2,1)S(1)}, u32[]{:S(2)}, u32[]{:S(2)}) collective-permute-start(bf16[2048,256]{1,0:T(8,128)(2,1)} %refs_16_.1), channel_id=1, source_target_pairs={{0,1},{1,0},{2,3},{3,2},{4,5},{5,4},{6,7},{7,6},{8,9},{9,8},{10,11... | collective-permute-start | bytes 3145736 | tf_op jit(solution)/shard_map/ppermute | solution.py:431
  21.0 9.5 %collective-permute-start.6 = (bf16[128,2048]{1,0:T(8,128)(2,1)}, bf16[128,2048]{1,0:T(8,128)(2,1)S(1)}, u32[]{:S(2)}, u32[]{:S(2)}) collective-permute-start(bf16[128,2048]{1,0:T(8,128)(2,1)} %get-tuple-element.30.refs_0_), channel_id=1, source_target_pairs={{0,1},{1,0},{2,3},{3,2},{4,5},{5,4},{6,7},{7,6},{8,9},{9,8},{10,11... | collective-permute-start | bytes 1572872 | tf_op jit(solution)/shard_map/ppermute | solution.py:431
  21.0 5.8 %collective-permute-start.10 = (bf16[64,2048]{1,0:T(8,128)(2,1)S(1)}, bf16[64,2048]{1,0:T(8,128)(2,1)S(1)}, u32[]{:S(2)}, u32[]{:S(2)}) collective-permute-start(bf16[64,2048]{1,0:T(8,128)(2,1)S(1)} %collective-permute-done.3.refs_4_), channel_id=1, source_target_pairs={{0,1},{1,0},{2,3},{3,2},{4,5},{5,4},{6,7},{7,6},{8,9},{9,8},{10,11... | collective-permute-start | bytes 786440 | tf_op jit(solution)/shard_map/ppermute | solution.py:431
  21.5 8.4 %collective-permute-start.5 = (bf16[64,2048]{1,0:T(8,128)(2,1)S(1)}, bf16[64,2048]{1,0:T(8,128)(2,1)}, u32[]{:S(2)}, u32[]{:S(2)}) collective-permute-start(bf16[64,2048]{1,0:T(8,128)(2,1)S(1)} %collective-permute-done.3.refs_4_), channel_id=1, source_target_pairs={{0,6},{2,0},{4,2},{6,4},{1,7},{3,1},{5,3},{7,5},{8,14},{10,8},{12,... | collective-permute-start | bytes 786440 | tf_op jit(solution)/shard_map/ppermute | solution.py:433
  26.8 3.1 %collective-permute-start.8 = (bf16[64,2048]{1,0:T(8,128)(2,1)S(1)}, bf16[64,2048]{1,0:T(8,128)(2,1)S(1)}, u32[]{:S(2)}, u32[]{:S(2)}) collective-permute-start(bf16[64,2048]{1,0:T(8,128)(2,1)S(1)} %collective-permute-done.1.refs_2_), channel_id=1, source_target_pairs={{0,1},{1,0},{2,3},{3,2},{4,5},{5,4},{6,7},{7,6},{8,9},{9,8},{10,11... | collective-permute-start | bytes 786440 | tf_op jit(solution)/shard_map/ppermute | solution.py:431
  26.8 16.8 %collective-permute-start.13 = (bf16[2048,256]{1,0:T(8,128)(2,1)}, bf16[2048,256]{1,0:T(8,128)(2,1)}, u32[]{:S(2)}, u32[]{:S(2)}) collective-permute-start(bf16[2048,256]{1,0:T(8,128)(2,1)} %refs_14_.1), channel_id=1, source_target_pairs={{0,1},{1,0},{2,3},{3,2},{4,5},{5,4},{6,7},{7,6},{8,9},{9,8},{10,11... | collective-permute-start | bytes 3145736 | tf_op jit(solution)/shard_map/ppermute | solution.py:431
  29.9 27.1 %collective-permute-start.15 = (bf16[2048,256]{1,0:T(8,128)(2,1)}, bf16[2048,256]{1,0:T(8,128)(2,1)}, u32[]{:S(2)}, u32[]{:S(2)}) collective-permute-start(bf16[2048,256]{1,0:T(8,128)(2,1)} %refs_18_.1), channel_id=1, source_target_pairs={{0,1},{1,0},{2,3},{3,2},{4,5},{5,4},{6,7},{7,6},{8,9},{9,8},{10,11... | collective-permute-start | bytes 3145736 | tf_op jit(solution)/shard_map/ppermute | solution.py:431
  29.9 12.1 %collective-permute-start.11 = (bf16[64,2048]{1,0:T(8,128)(2,1)}, bf16[64,2048]{1,0:T(8,128)(2,1)}, u32[]{:S(2)}, u32[]{:S(2)}) collective-permute-start(bf16[64,2048]{1,0:T(8,128)(2,1)} %collective-permute-done.4.refs_5_), channel_id=1, source_target_pairs={{0,1},{1,0},{2,3},{3,2},{4,5},{5,4},{6,7},{7,6},{8,9},{9,8},{10,11... | collective-permute-start | bytes 786440 | tf_op jit(solution)/shard_map/ppermute | solution.py:431
  31.4 10.7 %collective-permute-start.12 = (bf16[64,2048]{1,0:T(8,128)(2,1)}, bf16[64,2048]{1,0:T(8,128)(2,1)}, u32[]{:S(2)}, u32[]{:S(2)}) collective-permute-start(bf16[64,2048]{1,0:T(8,128)(2,1)} %collective-permute-done.5.refs_6_), channel_id=1, source_target_pairs={{0,1},{1,0},{2,3},{3,2},{4,5},{5,4},{6,7},{7,6},{8,9},{9,8},{10,11... | collective-permute-start | bytes 786440 | tf_op jit(solution)/shard_map/ppermute | solution.py:431
  34.9 22.2 %all-to-all-start = ((bf16[16,64,512]{2,1,0:T(8,128)(2,1)}), bf16[16,64,512]{2,1,0:T(8,128)(2,1)S(1)}, u32[]{:S(2)}, u32[]{:S(2)}) async-start(bf16[16,64,512]{2,1,0:T(8,128)(2,1)} %bitcast.28), calls=%async_computation | async-start | bytes 2097152 | tf_op jit(solution)/shard_map/all_to_all | solution.py:464
  42.1 40.3 %collective-permute-start.18 = (bf16[2048,512]{1,0:T(8,128)(2,1)}, bf16[2048,512]{1,0:T(8,128)(2,1)}, u32[]{:S(2)}, u32[]{:S(2)}) collective-permute-start(bf16[2048,512]{1,0:T(8,128)(2,1)} %bitcast.20), channel_id=1, source_target_pairs={{0,1},{1,0},{2,3},{3,2},{4,5},{5,4},{6,7},{7,6},{8,9},{9,8},{10,11... | collective-permute-start | bytes 6291464 | tf_op jit(solution)/shard_map/ppermute | solution.py:431
  42.2 40.5 %collective-permute-start.19 = (bf16[2048,512]{1,0:T(8,128)(2,1)}, bf16[2048,512]{1,0:T(8,128)(2,1)}, u32[]{:S(2)}, u32[]{:S(2)}) collective-permute-start(bf16[2048,512]{1,0:T(8,128)(2,1)} %bitcast.22), channel_id=1, source_target_pairs={{0,1},{1,0},{2,3},{3,2},{4,5},{5,4},{6,7},{7,6},{8,9},{9,8},{10,11... | collective-permute-start | bytes 6291464 | tf_op jit(solution)/shard_map/ppermute | solution.py:431
  42.7 50.9 %collective-permute-start.20 = (bf16[512,2048]{1,0:T(8,128)(2,1)}, bf16[512,2048]{1,0:T(8,128)(2,1)}, u32[]{:S(2)}, u32[]{:S(2)}) collective-permute-start(bf16[512,2048]{1,0:T(8,128)(2,1)} %bitcast.24), channel_id=1, source_target_pairs={{0,1},{1,0},{2,3},{3,2},{4,5},{5,4},{6,7},{7,6},{8,9},{9,8},{10,11... | collective-permute-start | bytes 6291464 | tf_op jit(solution)/shard_map/ppermute | solution.py:431
  43.6 23.5 %collective-permute-start.17 = (bf16[256,2048]{1,0:T(8,128)(2,1)S(1)}, bf16[256,2048]{1,0:T(8,128)(2,1)S(1)}, u32[]{:S(2)}, u32[]{:S(2)}) collective-permute-start(bf16[256,2048]{1,0:T(8,128)(2,1)S(1)} %copy-done), channel_id=1, source_target_pairs={{0,1},{1,0},{2,3},{3,2},{4,5},{5,4},{6,7},{7,6},{8,9},{9,8},{10,11... | collective-permute-start | bytes 3145736 | tf_op jit(solution)/shard_map/ppermute | solution.py:431
  57.1 10.1 %collective-permute-start.16 = (bf16[1024,512]{1,0:T(8,128)(2,1)S(1)}, bf16[1024,512]{1,0:T(8,128)(2,1)S(1)}, u32[]{:S(2)}, u32[]{:S(2)}) collective-permute-start(bf16[1024,512]{1,0:T(8,128)(2,1)S(1)} %bitcast.15), channel_id=1, source_target_pairs={{0,1},{1,0},{2,3},{3,2},{4,5},{5,4},{6,7},{7,6},{8,9},{9,8},{10,11... | collective-permute-start | bytes 3145736 | tf_op jit(solution)/shard_map/ppermute | solution.py:431
  70.4 8.8 %collective-permute-start.21 = (bf16[64,2048]{1,0:T(8,128)(2,1)S(1)}, bf16[64,2048]{1,0:T(8,128)(2,1)S(1)}, u32[]{:S(2)}, u32[]{:S(2)}) collective-permute-start(bf16[64,2048]{1,0:T(8,128)(2,1)S(1)} %get-tuple-element.38), channel_id=1, source_target_pairs={{0,6},{2,0},{4,2},{6,4},{1,7},{3,1},{5,3},{7,5},{8,14},{10,8},{12,... | collective-permute-start | bytes 786440 | tf_op jit(solution)/shard_map/ppermute | solution.py:433
  72.4 9.9 %collective-permute-start.22 = (bf16[64,2048]{1,0:T(8,128)(2,1)S(1)}, bf16[64,2048]{1,0:T(8,128)(2,1)S(1)}, u32[]{:S(2)}, u32[]{:S(2)}) collective-permute-start(bf16[64,2048]{1,0:T(8,128)(2,1)S(1)} %get-tuple-element.40), channel_id=1, source_target_pairs={{0,2},{2,4},{4,6},{6,0},{1,3},{3,5},{5,7},{7,1},{8,10},{10,12},{12... | collective-permute-start | bytes 786440 | tf_op jit(solution)/shard_map/ppermute | solution.py:432
  79.2 14.5 %collective-permute-start.24 = (bf16[64,2048]{1,0:T(8,128)(2,1)S(1)}, bf16[64,2048]{1,0:T(8,128)(2,1)S(1)}, u32[]{:S(2)}, u32[]{:S(2)}) collective-permute-start(bf16[64,2048]{1,0:T(8,128)(2,1)S(1)} %get-tuple-element.42), channel_id=1, source_target_pairs={{0,6},{2,0},{4,2},{6,4},{1,7},{3,1},{5,3},{7,5},{8,14},{10,8},{12,... | collective-permute-start | bytes 786440 | tf_op jit(solution)/shard_map/ppermute | solution.py:433
  82.3 11.3 %collective-permute-start.25 = (bf16[64,2048]{1,0:T(8,128)(2,1)S(1)}, bf16[64,2048]{1,0:T(8,128)(2,1)S(1)}, u32[]{:S(2)}, u32[]{:S(2)}) collective-permute-start(bf16[64,2048]{1,0:T(8,128)(2,1)S(1)} %get-tuple-element.43), channel_id=1, source_target_pairs={{0,2},{2,4},{4,6},{6,0},{1,3},{3,5},{5,7},{7,1},{8,10},{10,12},{12... | collective-permute-start | bytes 786440 | tf_op jit(solution)/shard_map/ppermute | solution.py:432
  82.4 14.3 %collective-permute-start.23 = (bf16[64,2048]{1,0:T(8,128)(2,1)S(1)}, bf16[64,2048]{1,0:T(8,128)(2,1)S(1)}, u32[]{:S(2)}, u32[]{:S(2)}) collective-permute-start(bf16[64,2048]{1,0:T(8,128)(2,1)S(1)} %get-tuple-element.41), channel_id=1, source_target_pairs={{0,2},{2,4},{4,6},{6,0},{1,3},{3,5},{5,7},{7,1},{8,10},{10,12},{12... | collective-permute-start | bytes 786440 | tf_op jit(solution)/shard_map/ppermute | solution.py:432
  82.7 14.0 %collective-permute-start.26 = (bf16[64,2048]{1,0:T(8,128)(2,1)S(1)}, bf16[64,2048]{1,0:T(8,128)(2,1)S(1)}, u32[]{:S(2)}, u32[]{:S(2)}) collective-permute-start(bf16[64,2048]{1,0:T(8,128)(2,1)S(1)} %get-tuple-element.44), channel_id=1, source_target_pairs={{0,6},{2,0},{4,2},{6,4},{1,7},{3,1},{5,3},{7,5},{8,14},{10,8},{12,... | collective-permute-start | bytes 786440 | tf_op jit(solution)/shard_map/ppermute | solution.py:433
  98.5 61.5 %copy-start.1 = (bf16[1,2048,512]{2,1,0:T(8,128)(2,1)S(1)}, bf16[1,2048,512]{2,1,0:T(8,128)(2,1)}, u32[]{:S(2)}) copy-start(bf16[1,2048,512]{2,1,0:T(8,128)(2,1)} %param.29) | copy-start | bytes 6291460
  175.2 63.4 %copy-start.5 = (bf16[256,1024]{1,0:T(8,128)(2,1)S(1)}, bf16[256,1024]{1,0:T(8,128)(2,1)}, u32[]{:S(2)}) copy-start(bf16[256,1024]{1,0:T(8,128)(2,1)} %get-tuple-element.50.wm_ref) | copy-start | bytes 1572868
  175.2 63.4 %copy-start.6 = (bf16[128,2048]{1,0:T(8,128)(2,1)S(1)}, bf16[128,2048]{1,0:T(8,128)(2,1)}, u32[]{:S(2)}) copy-start(bf16[128,2048]{1,0:T(8,128)(2,1)} %get-tuple-element.52.h_ref) | copy-start | bytes 1572868
  175.2 63.4 %copy-start.7 = (bf16[256,128]{1,0:T(8,128)(2,1)S(1)}, bf16[256,128]{1,0:T(8,128)(2,1)}, u32[]{:S(2)}) copy-start(bf16[256,128]{1,0:T(8,128)(2,1)} %get-tuple-element.51.wx_ref) | copy-start | bytes 196612
  (16 other events, 260.6 us)
